TPU v7x, 128 devices: a whole 4x4x4 slice. The times are simulated.
128 devices in a mesh: grp: 4 (over y), col: 32 (over x, z, core).
Axes of the slice: x: 4, y: 4, z: 4, core: 2. Of those that a mesh axis runs over, the one named last changes fastest.
Arguments:
- blocks: bfloat16 [24576, 32, 1024], P(('grp', 'col'))
- i_index: int32 [24576], P(('grp', 'col')), may hold values from 0 to 63
- j_index: int32 [24576], P(('grp', 'col')), may hold values from 0 to 63
- k_index: int32 [24576], P(('grp', 'col')), may hold values from 0 to 15
- block_count: int32 [128], P(('grp', 'col')), may hold values from 24 to 192, as said below
- b_factor: float32 [65536, 256], P(('grp', 'col'))
- c_factor: float32 [16384, 256], P(('grp', 'col'))
Outputs:
- a_update: float32 [8192, 256], P(('grp', 'col'))
- b_update: float32 [65536, 256], P(('grp', 'col'))
Inputs may be any that keep to these rules, and one draw needn't show every extreme that they name: block_count[d] is the number of live slots of device d = 32 * (grp index) + (col index): its slots d * 192 to d * 192 + block_count[d] - 1; every other slot is ignored. Some device has exactly 192 live slots.
All inputs are finite; a program needn't handle non-finite values.
Results may differ from a plain program's by a relative error of at most 0.005.
The roundings to bfloat16 on the way count: a program that leaves them out, or rounds other values in their place, can miss the bound.
Values may be sent and summed in bfloat16 or wider, within the bound.
No kernel may reach another device: no remote copies, remote signals or barrier semaphores. Data moves between devices by JAX's collectives and lax.ppermute only.
A program may use at most 128 MiB of HBM per device.

v0:
```python
import jax
import jax.numpy as jnp
from jax import lax
from jax.experimental import pallas as pl
from jax.experimental.pallas import tpu as pltpu
from jax.sharding import Mesh
from jax.sharding import PartitionSpec as P

EDGE = 32
STEP = 16
UNROLL = 8
B_ROWS = 16 * EDGE
MODE_COST = pl.CostEstimate(flops=28_000_000_000, bytes_accessed=90_000_000, transcendentals=0)
INVERSE_COST = pl.CostEstimate(flops=16_000_000_000, bytes_accessed=50_000_000, transcendentals=0)
VMEM_BYTES = 48 << 20
ALL = ("grp", "x", "z", "core")
PLANE = ("x", "z")
F32 = jnp.float32
BF16 = jnp.bfloat16
HIGHEST = lax.Precision.HIGHEST


def invert_four(p):
    inv_det = 1.0 / (p[0][0] * p[1][1] - p[0][1] * p[0][1])
    a00, a01, a11 = p[1][1] * inv_det, -p[0][1] * inv_det, p[0][0] * inv_det
    t00 = a00 * p[0][2] + a01 * p[1][2]
    t01 = a00 * p[0][3] + a01 * p[1][3]
    t10 = a01 * p[0][2] + a11 * p[1][2]
    t11 = a01 * p[0][3] + a11 * p[1][3]
    s00 = p[2][2] - (p[0][2] * t00 + p[1][2] * t10)
    s01 = p[2][3] - (p[0][2] * t01 + p[1][2] * t11)
    s11 = p[3][3] - (p[0][3] * t01 + p[1][3] * t11)
    inv_det = 1.0 / (s00 * s11 - s01 * s01)
    z00, z01, z11 = s11 * inv_det, -s01 * inv_det, s00 * inv_det
    u00, u01 = t00 * z00 + t01 * z01, t00 * z01 + t01 * z11
    u10, u11 = t10 * z00 + t11 * z01, t10 * z01 + t11 * z11
    x00 = a00 + (u00 * t00 + u01 * t01)
    x01 = a01 + (u00 * t10 + u01 * t11)
    x11 = a11 + (u10 * t10 + u11 * t11)
    return [
        [x00, x01, -u00, -u01],
        [x01, x11, -u10, -u11],
        [-u00, -u10, z00, z01],
        [-u01, -u11, z01, z11],
    ]


def invert_block(w):
    n = w.shape[0]
    row = lax.broadcasted_iota(jnp.int32, (n, n), 0)
    col = lax.broadcasted_iota(jnp.int32, (n, n), 1)
    for k in range(0, n, 4):
        cols = [jnp.broadcast_to(w[:, k + q : k + q + 1], (n, n)) for q in range(4)]
        rows = [w[k + q : k + q + 1, :] for q in range(4)]
        pivot = [[cols[b][k + a : k + a + 1, :] for b in range(4)] for a in range(4)]
        inv = invert_four(pivot)
        lane = col[0:1, :]
        fresh = []
        for a in range(4):
            value = (inv[a][0] * rows[0] + inv[a][1] * rows[1]) + (
                inv[a][2] * rows[2] + inv[a][3] * rows[3]
            )
            for b in range(4):
                value = jnp.where(lane == k + b, inv[a][b], value)
            fresh.append(value)
        in_cols = (col >= k) & (col < k + 4)
        in_rows = (row >= k) & (row < k + 4)
        base = jnp.where(in_cols, 0.0, w)
        update = (cols[0] * fresh[0] + cols[1] * fresh[1]) + (
            cols[2] * fresh[2] + cols[3] * fresh[3]
        )
        out = base - update
        for a in range(4):
            out = jnp.where(row == k + a, fresh[a], out)
        w = out
    return w


def inverse_kernel(turn, gram, out, work):
    n = gram.shape[0]
    width = 64

    @pl.when(turn[0] == 0)
    def _():
        out[...] = jnp.zeros_like(out)

    @pl.when(turn[0] != 0)
    def _():
        row = lax.broadcasted_iota(jnp.int32, (n, n), 0)
        col = lax.broadcasted_iota(jnp.int32, (n, n), 1)
        diag = jnp.where(row == col, gram[...], 0.0)
        scale_row = lax.rsqrt(jnp.sum(diag, axis=0, keepdims=True))
        scale_col = lax.rsqrt(jnp.sum(diag, axis=1, keepdims=True))
        work[...] = gram[...] * scale_row * scale_col
        for b in range(n // width):
            span = slice(b * width, (b + 1) * width)
            block = invert_block(work[span, span])
            rows = jnp.dot(block, work[span, :], precision=HIGHEST, preferred_element_type=F32)
            parts = [jnp.zeros((width, width), F32)] * (n // width)
            parts[b] = block
            padded = jnp.concatenate(parts, axis=1)
            in_block = (col >= b * width) & (col < (b + 1) * width)
            rows = jnp.where(in_block[0:width], padded, rows)
            left = work[:, span]
            left_row = row[:, 0:width]
            left = jnp.where((left_row >= b * width) & (left_row < (b + 1) * width), 0.0, left)
            base = jnp.where(in_block, 0.0, work[...])
            work[...] = base - jnp.dot(left, rows, precision=HIGHEST, preferred_element_type=F32)
            work[span, :] = rows
        out[...] = work[...] * scale_row * scale_col


def inverse_of(turn, gram):
    n = gram.shape[0]
    return pl.pallas_call(
        inverse_kernel,
        out_shape=jax.ShapeDtypeStruct((n, n), F32),
        in_specs=[
            pl.BlockSpec(memory_space=pltpu.SMEM),
            pl.BlockSpec(memory_space=pltpu.VMEM),
        ],
        out_specs=pl.BlockSpec(memory_space=pltpu.VMEM),
        scratch_shapes=[pltpu.VMEM((n, n), F32)],
        compiler_params=pltpu.CompilerParams(vmem_limit_bytes=VMEM_BYTES),
        cost_estimate=INVERSE_COST,
        name="gram_inverse",
    )(turn, gram)


def prepare_kernel(b_factor, c_factor, own, grams):
    rank = b_factor.shape[1]
    rows = b_factor.shape[0]
    own[0:rows, :] = b_factor[...].astype(BF16)
    own[rows:, :] = c_factor[...].astype(BF16)
    for q, ref in enumerate((b_factor, c_factor)):
        grams[q * rank : (q + 1) * rank, :] = lax.dot_general(
            ref[...],
            ref[...],
            (((0,), (0,)), ((), ())),
            precision=HIGHEST,
            preferred_element_type=F32,
        )


def prepare(b_factor, c_factor):
    rank = b_factor.shape[1]
    rows = b_factor.shape[0] + c_factor.shape[0]
    return pl.pallas_call(
        prepare_kernel,
        out_shape=[
            jax.ShapeDtypeStruct((rows, rank), BF16),
            jax.ShapeDtypeStruct((2 * rank, rank), F32),
        ],
        compiler_params=pltpu.CompilerParams(vmem_limit_bytes=VMEM_BYTES),
        name="prepare",
    )(b_factor, c_factor)


def block_rows(ref, start):
    return ref[pl.ds(pl.multiple_of(start, EDGE), EDGE), :]


def mode_one_kernel(
    meta, i_idx, j_idx, k_idx, blocks, own_0, own_1, own_2, own_3, keep, send, acc, table
):
    step = pl.program_id(0)
    count, grp, core = meta[0], meta[1], meta[2]
    own = own_0.shape[0]
    c_base = B_ROWS
    half = keep.shape[0]

    @pl.when(step == 0)
    def _():
        acc[...] = jnp.zeros_like(acc)
        for q, ref in enumerate((own_0, own_1, own_2, own_3)):
            table[q * own : (q + 1) * own, :] = ref[...]

    for sub in range(STEP // UNROLL):
        base = step * STEP + sub * UNROLL

        @pl.when(base < count)
        def _():
            for u in range(UNROLL):
                s = base + u
                j, k, i = j_idx[s], k_idx[s], i_idx[s]
                b_start = ((grp - (j >> 4)) & 3) * own + (j & 15) * EDGE
                c_start = ((grp - (k >> 2)) & 3) * own + c_base + (k & 3) * EDGE
                b_rows = block_rows(table, b_start)
                c_rows = block_rows(table, c_start)
                product = (b_rows[:, None, :] * c_rows[None, :, :]).reshape(EDGE * EDGE, -1)
                result = jnp.dot(blocks[sub * UNROLL + u], product, preferred_element_type=F32)
                target = (((i >> 1) & 1) ^ core) * half + (i >> 2) * (2 * EDGE) + (i & 1) * EDGE
                target = jnp.where(s < count, target, 2 * half)
                acc[pl.ds(pl.multiple_of(target, EDGE), EDGE), :] += result

    @pl.when(step == pl.num_programs(0) - 1)
    def _():
        keep[...] = acc[0:half, :]
        send[...] = acc[half : 2 * half, :]


def mode_two_kernel(
    meta,
    i_idx,
    j_idx,
    k_idx,
    blocks,
    a_near,
    a_far,
    squares,
    own_0,
    own_1,
    own_2,
    own_3,
    keep,
    send_1,
    send_2,
    send_3,
    acc,
    turned,
    table,
    a_table,
):
    step = pl.program_id(0)
    count, grp, core = meta[0], meta[1], meta[2]
    own = own_0.shape[0]
    half = a_near.shape[0]
    part = keep.shape[0]

    @pl.when(step == 0)
    def _():
        acc[...] = jnp.zeros_like(acc)
        for q, ref in enumerate((own_0, own_1, own_2, own_3)):
            table[q * own : (q + 1) * own, :] = ref[...]
        col_norm = jnp.sqrt(squares[...] + 1e-06)
        a_table[0:half, :] = (a_near[...] / col_norm).astype(BF16)
        a_table[half : 2 * half, :] = (a_far[...] / col_norm).astype(BF16)

    lane = lax.broadcasted_iota(jnp.int32, (8, 128), 1)
    low_half = lane < 64
    even_group = (lane // 32) % 2 == 0

    def turn(block, slot):
        wide = block.astype(F32)
        for jh in range(8):
            t = [wide[il * 8 : il * 8 + 8, jh * 128 : jh * 128 + 128] for il in range(4)]
            m = [None] * 4
            for il in range(2):
                m[il] = jnp.where(low_half, t[il], pltpu.roll(t[il + 2], 64, 1))
                m[il + 2] = jnp.where(low_half, pltpu.roll(t[il], 64, 1), t[il + 2])
            for q in (0, 2):
                j = jh * 4 + q
                turned[slot, j * 8 : j * 8 + 8, :] = jnp.where(
                    even_group, m[q], pltpu.roll(m[q + 1], 32, 1)
                )
                turned[slot, j * 8 + 8 : j * 8 + 16, :] = jnp.where(
                    even_group, pltpu.roll(m[q], 96, 1), m[q + 1]
                )
        return jnp.concatenate(
            [turned[slot, pl.ds(ih, EDGE, stride=8), :].astype(BF16) for ih in range(8)], axis=1
        )

    for sub in range(STEP // UNROLL):
        base = step * STEP + sub * UNROLL

        @pl.when(base < count)
        def _():
            for u in range(UNROLL):
                s = base + u
                j, k, i = j_idx[s], k_idx[s], i_idx[s]
                a_start = (((i >> 1) & 1) ^ core) * half + (i >> 2) * (2 * EDGE) + (i & 1) * EDGE
                c_start = ((grp - (k >> 2)) & 3) * own + (k & 3) * EDGE
                a_rows = block_rows(a_table, a_start)
                c_rows = block_rows(table, c_start)
                left = turn(blocks[sub * UNROLL + u], u)
                product = jnp.concatenate(
                    [
                        a_rows[il * 8 + ih : il * 8 + ih + 1, :] * c_rows
                        for ih in range(8)
                        for il in range(4)
                    ],
                    axis=0,
                )
                result = jnp.dot(left, product, preferred_element_type=F32)
                target = (((j >> 4) - grp) & 3) * part + (j & 15) * EDGE
                target = jnp.where(s < count, target, 4 * part)
                acc[pl.ds(pl.multiple_of(target, EDGE), EDGE), :] += result

    @pl.when(step == pl.num_programs(0) - 1)
    def _():
        keep[...] = acc[0:part, :]
        for q, ref in enumerate((send_1, send_2, send_3)):
            ref[...] = acc[(q + 1) * part : (q + 2) * part, :].astype(BF16)


def slot_block(step, meta, *_):
    return (jnp.minimum(step, jnp.maximum(meta[0] - 1, 0) // STEP), 0, 0)


def whole(shape):
    return pl.BlockSpec(shape, lambda step, *_: (0, 0))


def mode_one(meta, i_index, j_index, k_index, blocks, pieces):
    rank = pieces[0].shape[1]
    half = 32 * EDGE
    return pl.pallas_call(
        mode_one_kernel,
        out_shape=[jax.ShapeDtypeStruct((half, rank), F32)] * 2,
        grid_spec=pltpu.PrefetchScalarGridSpec(
            num_scalar_prefetch=4,
            grid=(blocks.shape[0] // STEP,),
            in_specs=[pl.BlockSpec((STEP,) + blocks.shape[1:], slot_block)]
            + [whole(pieces[0].shape)] * 4,
            out_specs=[whole((half, rank))] * 2,
            scratch_shapes=[
                pltpu.VMEM((2 * half + EDGE, rank), F32),
                pltpu.VMEM((4 * pieces[0].shape[0], rank), BF16),
            ],
        ),
        compiler_params=pltpu.CompilerParams(vmem_limit_bytes=VMEM_BYTES),
        cost_estimate=MODE_COST,
        name="mode_one",
    )(meta, i_index, j_index, k_index, blocks, *pieces)


def mode_two(meta, i_index, j_index, k_index, blocks, a_near, a_far, squares, pieces):
    rank = a_near.shape[1]
    part = 16 * EDGE
    c_rows = pieces[0].shape[0] - B_ROWS
    return pl.pallas_call(
        mode_two_kernel,
        out_shape=[jax.ShapeDtypeStruct((part, rank), F32)]
        + [jax.ShapeDtypeStruct((part, rank), BF16)] * 3,
        grid_spec=pltpu.PrefetchScalarGridSpec(
            num_scalar_prefetch=4,
            grid=(blocks.shape[0] // STEP,),
            in_specs=[
                pl.BlockSpec((STEP,) + blocks.shape[1:], slot_block),
                whole(a_near.shape),
                whole(a_far.shape),
                whole(squares.shape),
            ]
            + [pl.BlockSpec((c_rows, rank), lambda step, *_: (B_ROWS // c_rows, 0))] * 4,
            out_specs=[whole((part, rank))] * 4,
            scratch_shapes=[
                pltpu.VMEM((4 * part + EDGE, rank), F32),
                pltpu.VMEM((UNROLL, 8 * EDGE, 128), F32),
                pltpu.VMEM((4 * c_rows, rank), BF16),
                pltpu.VMEM((2 * a_near.shape[0], rank), BF16),
            ],
        ),
        compiler_params=pltpu.CompilerParams(vmem_limit_bytes=VMEM_BYTES),
        cost_estimate=MODE_COST,
        name="mode_two",
    )(meta, i_index, j_index, k_index, blocks, a_near, a_far, squares, *pieces)


def to_other_core(value):
    return lax.ppermute(value, "core", [(0, 1), (1, 0)])


def along_groups(value, shift):
    size = lax.axis_size("grp")
    return lax.ppermute(value, "grp", [(p, (p + shift) % size) for p in range(size)])


def exchange(value, axes):
    return lax.all_to_all(value, axes, 0, 0)


def on_device(blocks, i_index, j_index, k_index, block_count, b_factor, c_factor):
    rank = b_factor.shape[1]
    grp, core = lax.axis_index("grp"), lax.axis_index("core")
    plane = lax.axis_size(PLANE)
    devices = lax.axis_size(ALL)
    meta = jnp.stack([block_count[0], grp, core])
    other_count = to_other_core(block_count)
    lighter = (block_count < other_count) | ((block_count == other_count) & (core == 0))
    turn = lighter.astype(jnp.int32)

    own, grams = prepare(b_factor, c_factor)
    pieces = [own] + [along_groups(own, q) for q in (1, 2, 3)]
    piece = jnp.sum(exchange(grams.reshape(devices, -1, rank), ALL), axis=0)
    piece, meta = lax.optimization_barrier((piece, meta))
    grams = exchange(jnp.broadcast_to(piece[None], (devices,) + piece.shape), ALL)

    keep, send = mode_one(meta, i_index, j_index, k_index, blocks, pieces)
    grams, keep, send = lax.optimization_barrier((grams, keep, send))
    pair_sum = (keep + to_other_core(send)).astype(BF16)
    arrived = exchange(pair_sum.reshape(plane, -1, rank), PLANE)
    sum_own = jnp.sum(arrived.astype(F32), axis=0)
    sum_near = exchange(jnp.broadcast_to(sum_own[None], (plane,) + sum_own.shape), PLANE)
    sum_near = sum_near.reshape(-1, rank)

    grams = grams.reshape(2, rank, rank)
    gram_third = grams[1]
    inverse = inverse_of(turn, grams[0] * gram_third)
    inverse = jnp.where(lighter[0], inverse, to_other_core(inverse))
    a_update = jnp.dot(sum_own, inverse, precision=HIGHEST)

    sum_far = to_other_core(sum_near)
    a_near = jnp.dot(sum_near, inverse, precision=HIGHEST)
    squares = jnp.sum(a_near * a_near, axis=0, keepdims=True)
    squares = squares + along_groups(squares, 1) + along_groups(squares, 2) + along_groups(squares, 3)
    squares = squares + to_other_core(squares)
    a_far = jnp.dot(sum_far, inverse, precision=HIGHEST)
    gram_near = jnp.dot(a_near.T, a_near, precision=HIGHEST)
    gram_plane = gram_near + to_other_core(gram_near)
    gram_parts = [gram_plane] + [along_groups(gram_plane, q) for q in (1, 2, 3)]

    keep, *sends = mode_two(
        meta, i_index, j_index, k_index, blocks, a_near, a_far, squares, pieces
    )
    gram_parts, keep = lax.optimization_barrier((gram_parts, keep))
    gram_first = gram_parts[0] + gram_parts[1] + gram_parts[2] + gram_parts[3]
    col_norm = jnp.sqrt(squares + 1e-06)
    gram_two = gram_first / (col_norm.reshape(rank, 1) * col_norm) * gram_third
    inverse = inverse_of(turn, gram_two)
    inverse, sends = lax.optimization_barrier((inverse, sends))
    inverse = jnp.where(lighter[0], inverse, to_other_core(inverse))
    arrived = [along_groups(value, q + 1).astype(F32) for q, value in enumerate(sends)]
    own_two = keep + arrived[0] + arrived[1] + arrived[2]
    b_update = jnp.dot(own_two, inverse, precision=HIGHEST)
    return a_update, b_update


def solution(mesh):
    groups, columns = mesh.shape["grp"], mesh.shape["col"]
    side = round((columns // 2) ** 0.5)
    fine = Mesh(mesh.devices.reshape(groups, side, side, 2), ALL)
    row, flat = P(ALL, None), P(ALL)
    return jax.shard_map(
        on_device,
        mesh=fine,
        in_specs=(P(ALL, None, None), flat, flat, flat, flat, row, row),
        out_specs=(row, row),
        check_vma=False,
    )
```

profile of v0, /device:TPU:1, one launch (start us, length us, event | category | flops | bytes accessed | tf_op | source)
XLA Modules:
  0.0 154.8 jit_solution(9767464379881882963)
XLA Ops:
  4.4 11.5 %all-to-all-start = ((f32[128,4,256]{2,1,0:T(4,128)}), f32[128,4,256]{2,1,0:T(4,128)S(1)}, u32[]{:S(2)}, u32[]{:S(2)}) async-start(f32[128,4,256]{2,1,0:T(4,128)} %reshape.22), calls=%async_computation | async-start | bytes 1048576 | tf_op jit(solution)/shard_map/all_to_all | solution.py:369
  17.3 2.4 %collective-permute-start.1 = (bf16[640,256]{1,0:T(8,128)(2,1)S(1)}, bf16[640,256]{1,0:T(8,128)(2,1)S(1)}, u32[]{:S(2)}, u32[]{:S(2)}) collective-permute-start(bf16[640,256]{1,0:T(8,128)(2,1)S(1)} %get-tuple-element.27.own_0), channel_id=1, source_target_pairs={{0,64},{32,96},{64,0},{96,32},{1,65},{33,97},{65,1},{97,33},{2,66}... | collective-permute-start | bytes 983048 | tf_op jit(solution)/shard_map/ppermute | solution.py:365
  21.6 7.8 %all-to-all-done = f32[128,4,256]{2,1,0:T(4,128)S(1)} async-done(((f32[128,4,256]{2,1,0:T(4,128)}), f32[128,4,256]{2,1,0:T(4,128)S(1)}, u32[]{:S(2)}, u32[]{:S(2)}) %all-to-all-start) | async-done | bytes 524320 | tf_op jit(solution)/shard_map/all_to_all | solution.py:369
  30.5 5.7 %all-to-all-start.1 = ((f32[128,4,256]{2,1,0:T(4,128)}), f32[128,4,256]{2,1,0:T(4,128)}, u32[]{:S(2)}, u32[]{:S(2)}) async-start(f32[128,4,256]{2,1,0:T(4,128)} %broadcast_in_dim.6), calls=%async_computation.1 | async-start | bytes 1048576 | tf_op jit(solution)/shard_map/all_to_all | solution.py:369
  36.1 2.5 %collective-permute-done.1.own_2 = bf16[640,256]{1,0:T(8,128)(2,1)S(1)} collective-permute-done((bf16[640,256]{1,0:T(8,128)(2,1)S(1)}, bf16[640,256]{1,0:T(8,128)(2,1)S(1)}, u32[]{:S(2)}, u32[]{:S(2)}) %collective-permute-start.1) | collective-permute-done | bytes 327712 | tf_op jit(solution)/shard_map/ppermute | solution.py:365
  40.7 6.5 %mode_one.1 = (f32[1024,256]{1,0:T(8,128)S(1)}, f32[1024,256]{1,0:T(8,128)S(1)}) custom-call(s32[3]{0:T(128)S(1)} %pad_add_fusion.meta, s32[192]{0:T(256)S(1)} %copy-done.2, s32[192]{0:T(256)S(1)} %copy-done.4, s32[192]{0:T(256)S(1)} %copy-done.6, bf16[192,32,1024]{2,1,0:T(8,128)(2,1)} %blocks.3, bf16[640,256]{1,0:T(8,128)(2,1)S(1)} %get-tuple-element.27.own_0, ...), custom_call_target="tpu_custom_call" | custom-call | flops 28000000000 | bytes 90000000 | tf_op jit(solution)/shard_map/mode_one/pallas_call | solution.py:307
  47.3 2.2 %all-to-all-done.1 = f32[128,4,256]{2,1,0:T(4,128)} async-done(((f32[128,4,256]{2,1,0:T(4,128)}), f32[128,4,256]{2,1,0:T(4,128)}, u32[]{:S(2)}, u32[]{:S(2)}) %all-to-all-start.1) | async-done | bytes 524320 | tf_op jit(solution)/shard_map/all_to_all | solution.py:369
  49.5 2.5 %collective-permute-start.3 = (f32[1024,256]{1,0:T(8,128)S(1)}, f32[1024,256]{1,0:T(8,128)S(1)}, u32[]{:S(2)}, u32[]{:S(2)}) collective-permute-start(f32[1024,256]{1,0:T(8,128)S(1)} %get-tuple-element.31), channel_id=1, source_target_pairs={{0,1},{1,0},{2,3},{3,2},{4,5},{5,4},{6,7},{7,6},{8,9},{9,8},{10,11... | collective-permute-start | bytes 3145736 | tf_op jit(solution)/shard_map/ppermute | solution.py:360
  52.0 2.3 %collective-permute-done.3 = f32[1024,256]{1,0:T(8,128)S(1)} collective-permute-done((f32[1024,256]{1,0:T(8,128)S(1)}, f32[1024,256]{1,0:T(8,128)S(1)}, u32[]{:S(2)}, u32[]{:S(2)}) %collective-permute-start.3) | collective-permute-done | bytes 1048608 | tf_op jit(solution)/shard_map/ppermute | solution.py:360
  55.2 12.8 %all-to-all-start.2 = ((bf16[16,64,256]{2,1,0:T(8,128)(2,1)}), bf16[16,64,256]{2,1,0:T(8,128)(2,1)S(1)}, u32[]{:S(2)}, u32[]{:S(2)}) async-start(bf16[16,64,256]{2,1,0:T(8,128)(2,1)} %bitcast.2), calls=%async_computation.2 | async-start | bytes 1048576 | tf_op jit(solution)/shard_map/all_to_all | solution.py:369
  72.1 6.1 %all-to-all-done.2 = bf16[16,64,256]{2,1,0:T(8,128)(2,1)S(1)} async-done(((bf16[16,64,256]{2,1,0:T(8,128)(2,1)}), bf16[16,64,256]{2,1,0:T(8,128)(2,1)S(1)}, u32[]{:S(2)}, u32[]{:S(2)}) %all-to-all-start.2) | async-done | bytes 524320 | tf_op jit(solution)/shard_map/all_to_all | solution.py:369
  79.4 4.2 %all-to-all-start.3 = ((f32[16,64,256]{2,1,0:T(8,128)}), f32[16,64,256]{2,1,0:T(8,128)S(1)}, u32[]{:S(2)}, u32[]{:S(2)}) async-start(f32[16,64,256]{2,1,0:T(8,128)} %broadcast_in_dim.7), calls=%async_computation.3 | async-start | bytes 2097152 | tf_op jit(solution)/shard_map/all_to_all | solution.py:369
  83.6 13.7 %gram_inverse.2 = f32[256,256]{1,0:T(8,128)S(1)} custom-call(s32[1]{0:T(128)S(6)} %convert_element_type.20.turn, f32[256,256]{1,0:T(8,128)S(1)} %mul.24.gram), custom_call_target="tpu_custom_call" | custom-call | flops 16000000000 | bytes 50000000 | tf_op jit(solution)/shard_map/gram_inverse/pallas_call | solution.py:115
  98.7 3.1 %collective-permute-start.10 = (f32[1024,256]{1,0:T(8,128)S(1)}, f32[1024,256]{1,0:T(8,128)S(1)}, u32[]{:S(2)}, u32[]{:S(2)}) collective-permute-start(f32[1024,256]{1,0:T(8,128)S(1)} %bitcast.16), channel_id=1, source_target_pairs={{0,1},{1,0},{2,3},{3,2},{4,5},{5,4},{6,7},{7,6},{8,9},{9,8},{10,11... | collective-permute-start | bytes 3145736 | tf_op jit(solution)/shard_map/ppermute | solution.py:360
  103.0 2.6 %collective-permute-start.13 = (f32[1,256]{1,0:T(1,128)S(1)}, f32[1,256]{1,0:T(1,128)S(1)}, u32[]{:S(2)}, u32[]{:S(2)}) collective-permute-start(f32[1,256]{1,0:T(1,128)S(1)} %bitcast.21), channel_id=1, source_target_pairs={{0,96},{32,0},{64,32},{96,64},{1,97},{33,1},{65,33},{97,65},{2,98}... | collective-permute-start | bytes 3080 | tf_op jit(solution)/shard_map/ppermute | solution.py:365
  105.6 1.8 %fusion.11 = f32[256,256]{1,0:T(8,128)S(1)} fusion(f32[1024,256]{1,0:T(8,128)S(1)} %get-tuple-element.51.a_near), kind=kOutput, calls=%fused_computation.19 | convolution fusion | flops 805306368 | bytes 1310720 | tf_op jit(solution)/shard_map/dot_general | solution.py:408
  111.3 2.1 %collective-permute-start.8 = (f32[256,256]{1,0:T(8,128)S(1)}, f32[256,256]{1,0:T(8,128)S(1)}, u32[]{:S(2)}, u32[]{:S(2)}) collective-permute-start(f32[256,256]{1,0:T(8,128)S(1)} %add.43), channel_id=1, source_target_pairs={{0,64},{32,96},{64,0},{96,32},{1,65},{33,97},{65,1},{97,33},{2,66}... | collective-permute-start | bytes 786440 | tf_op jit(solution)/shard_map/ppermute | solution.py:365
  115.5 7.4 %mode_two.1 = (f32[512,256]{1,0:T(8,128)S(1)}, bf16[512,256]{1,0:T(8,128)(2,1)S(1)}, bf16[512,256]{1,0:T(8,128)(2,1)S(1)}, bf16[512,256]{1,0:T(8,128)(2,1)S(1)}) custom-call(s32[3]{0:T(128)S(1)} %pad_add_fusion.meta, s32[192]{0:T(256)S(1)} %copy-done.3, s32[192]{0:T(256)S(1)} %copy-done.5, s32[192]{0:T(256)S(1)} %copy-done.7, bf16[192,32,1024]{2,1,0:T(8,128)(2,1)} %blocks.3, ...), custom_call_target="tpu_custom_call" | custom-call | flops 28000000000 | bytes 90000000 | tf_op jit(solution)/shard_map/mode_two/pallas_call | solution.py:331
  122.9 2.3 %collective-permute-done.8 = f32[256,256]{1,0:T(8,128)S(1)} collective-permute-done((f32[256,256]{1,0:T(8,128)S(1)}, f32[256,256]{1,0:T(8,128)S(1)}, u32[]{:S(2)}, u32[]{:S(2)}) %collective-permute-start.8) | collective-permute-done | bytes 262176 | tf_op jit(solution)/shard_map/ppermute | solution.py:365
  125.3 13.5 %gram_inverse.3 = f32[256,256]{1,0:T(8,128)S(1)} custom-call(s32[1]{0:T(128)S(6)} %convert_element_type.20.turn, f32[256,256]{1,0:T(8,128)S(1)} %divide_multiply_fusion.gram), custom_call_target="tpu_custom_call" | custom-call | flops 16000000000 | bytes 50000000 | tf_op jit(solution)/shard_map/gram_inverse/pallas_call | solution.py:115
  139.9 2.5 %collective-permute-start.17 = (bf16[512,256]{1,0:T(8,128)(2,1)S(1)}, bf16[512,256]{1,0:T(8,128)(2,1)S(1)}, u32[]{:S(2)}, u32[]{:S(2)}) collective-permute-start(bf16[512,256]{1,0:T(8,128)(2,1)S(1)} %get-tuple-element.44), channel_id=1, source_target_pairs={{0,96},{32,0},{64,32},{96,64},{1,97},{33,1},{65,33},{97,65},{2,98}... | collective-permute-start | bytes 786440 | tf_op jit(solution)/shard_map/ppermute | solution.py:365
  142.4 2.8 %collective-permute-start.18 = (f32[256,256]{1,0:T(8,128)S(1)}, f32[256,256]{1,0:T(8,128)S(1)}, u32[]{:S(2)}, u32[]{:S(2)}) collective-permute-start(f32[256,256]{1,0:T(8,128)S(1)} %gram_inverse.3), channel_id=1, source_target_pairs={{0,1},{1,0},{2,3},{3,2},{4,5},{5,4},{6,7},{7,6},{8,9},{9,8},{10,11... | collective-permute-start | bytes 786440 | tf_op jit(solution)/shard_map/ppermute | solution.py:360
  146.1 3.6 %collective-permute-done.15 = bf16[512,256]{1,0:T(8,128)(2,1)S(1)} collective-permute-done((bf16[512,256]{1,0:T(8,128)(2,1)S(1)}, bf16[512,256]{1,0:T(8,128)(2,1)S(1)}, u32[]{:S(2)}, u32[]{:S(2)}) %collective-permute-start.15) | collective-permute-done | bytes 262176 | tf_op jit(solution)/shard_map/ppermute | solution.py:365
  149.7 3.7 %collective-permute-done.17 = bf16[512,256]{1,0:T(8,128)(2,1)S(1)} collective-permute-done((bf16[512,256]{1,0:T(8,128)(2,1)S(1)}, bf16[512,256]{1,0:T(8,128)(2,1)S(1)}, u32[]{:S(2)}, u32[]{:S(2)}) %collective-permute-start.17) | collective-permute-done | bytes 262176 | tf_op jit(solution)/shard_map/ppermute | solution.py:365
  (64 shorter events, 26.4 us)
Async XLA Ops:
  4.4 25.1 %all-to-all-start = ((f32[128,4,256]{2,1,0:T(4,128)}), f32[128,4,256]{2,1,0:T(4,128)S(1)}, u32[]{:S(2)}, u32[]{:S(2)}) async-start(f32[128,4,256]{2,1,0:T(4,128)} %reshape.22), calls=%async_computation | async-start | bytes 1048576 | tf_op jit(solution)/shard_map/all_to_all | solution.py:369
  15.9 20.3 %collective-permute-start = (bf16[640,256]{1,0:T(8,128)(2,1)S(1)}, bf16[640,256]{1,0:T(8,128)(2,1)S(1)}, u32[]{:S(2)}, u32[]{:S(2)}) collective-permute-start(bf16[640,256]{1,0:T(8,128)(2,1)S(1)} %get-tuple-element.27.own_0), channel_id=1, source_target_pairs={{0,32},{32,64},{64,96},{96,0},{1,33},{33,65},{65,97},{97,1},{2,34}... | collective-permute-start | bytes 983048 | tf_op jit(solution)/shard_map/ppermute | solution.py:365
  17.3 21.3 %collective-permute-start.1 = (bf16[640,256]{1,0:T(8,128)(2,1)S(1)}, bf16[640,256]{1,0:T(8,128)(2,1)S(1)}, u32[]{:S(2)}, u32[]{:S(2)}) collective-permute-start(bf16[640,256]{1,0:T(8,128)(2,1)S(1)} %get-tuple-element.27.own_0), channel_id=1, source_target_pairs={{0,64},{32,96},{64,0},{96,32},{1,65},{33,97},{65,1},{97,33},{2,66}... | collective-permute-start | bytes 983048 | tf_op jit(solution)/shard_map/ppermute | solution.py:365
  19.8 18.9 %collective-permute-start.2 = (bf16[640,256]{1,0:T(8,128)(2,1)S(1)}, bf16[640,256]{1,0:T(8,128)(2,1)S(1)}, u32[]{:S(2)}, u32[]{:S(2)}) collective-permute-start(bf16[640,256]{1,0:T(8,128)(2,1)S(1)} %get-tuple-element.27.own_0), channel_id=1, source_target_pairs={{0,96},{32,0},{64,32},{96,64},{1,97},{33,1},{65,33},{97,65},{2,98}... | collective-permute-start | bytes 983048 | tf_op jit(solution)/shard_map/ppermute | solution.py:365
  30.5 19.0 %all-to-all-start.1 = ((f32[128,4,256]{2,1,0:T(4,128)}), f32[128,4,256]{2,1,0:T(4,128)}, u32[]{:S(2)}, u32[]{:S(2)}) async-start(f32[128,4,256]{2,1,0:T(4,128)} %broadcast_in_dim.6), calls=%async_computation.1 | async-start | bytes 1048576 | tf_op jit(solution)/shard_map/all_to_all | solution.py:369
  49.5 4.8 %collective-permute-start.3 = (f32[1024,256]{1,0:T(8,128)S(1)}, f32[1024,256]{1,0:T(8,128)S(1)}, u32[]{:S(2)}, u32[]{:S(2)}) collective-permute-start(f32[1024,256]{1,0:T(8,128)S(1)} %get-tuple-element.31), channel_id=1, source_target_pairs={{0,1},{1,0},{2,3},{3,2},{4,5},{5,4},{6,7},{7,6},{8,9},{9,8},{10,11... | collective-permute-start | bytes 3145736 | tf_op jit(solution)/shard_map/ppermute | solution.py:360
  55.2 23.0 %all-to-all-start.2 = ((bf16[16,64,256]{2,1,0:T(8,128)(2,1)}), bf16[16,64,256]{2,1,0:T(8,128)(2,1)S(1)}, u32[]{:S(2)}, u32[]{:S(2)}) async-start(bf16[16,64,256]{2,1,0:T(8,128)(2,1)} %bitcast.2), calls=%async_computation.2 | async-start | bytes 1048576 | tf_op jit(solution)/shard_map/all_to_all | solution.py:369
  68.1 1.6 %collective-permute-start.4 = (s32[1]{0:T(128)}, s32[1]{0:T(128)}, u32[]{:S(2)}, u32[]{:S(2)}) collective-permute-start(s32[1]{0:T(128)} %param.11), channel_id=1, source_target_pairs={{0,1},{1,0},{2,3},{3,2},{4,5},{5,4},{6,7},{7,6},{8,9},{9,8},{10,11... | collective-permute-start | bytes 20 | tf_op jit(solution)/shard_map/ppermute | solution.py:360
  79.4 19.3 %all-to-all-start.3 = ((f32[16,64,256]{2,1,0:T(8,128)}), f32[16,64,256]{2,1,0:T(8,128)S(1)}, u32[]{:S(2)}, u32[]{:S(2)}) async-start(f32[16,64,256]{2,1,0:T(8,128)} %broadcast_in_dim.7), calls=%async_computation.3 | async-start | bytes 2097152 | tf_op jit(solution)/shard_map/all_to_all | solution.py:369
  83.6 31.9 %copy-start.3 = (s32[192]{0:T(256)S(1)}, s32[192]{0:T(256)}, u32[]{:S(2)}) copy-start(s32[192]{0:T(256)} %i_idx.3) | copy-start | bytes 2308
  97.3 4.5 %collective-permute-start.5 = (f32[256,256]{1,0:T(8,128)S(1)}, f32[256,256]{1,0:T(8,128)S(1)}, u32[]{:S(2)}, u32[]{:S(2)}) collective-permute-start(f32[256,256]{1,0:T(8,128)S(1)} %gram_inverse.2), channel_id=1, source_target_pairs={{0,1},{1,0},{2,3},{3,2},{4,5},{5,4},{6,7},{7,6},{8,9},{9,8},{10,11... | collective-permute-start | bytes 786440 | tf_op jit(solution)/shard_map/ppermute | solution.py:360
  98.7 15.7 %collective-permute-start.10 = (f32[1024,256]{1,0:T(8,128)S(1)}, f32[1024,256]{1,0:T(8,128)S(1)}, u32[]{:S(2)}, u32[]{:S(2)}) collective-permute-start(f32[1024,256]{1,0:T(8,128)S(1)} %bitcast.16), channel_id=1, source_target_pairs={{0,1},{1,0},{2,3},{3,2},{4,5},{5,4},{6,7},{7,6},{8,9},{9,8},{10,11... | collective-permute-start | bytes 3145736 | tf_op jit(solution)/shard_map/ppermute | solution.py:360
  102.9 5.2 %collective-permute-start.11 = (f32[1,256]{1,0:T(1,128)S(1)}, f32[1,256]{1,0:T(1,128)S(1)}, u32[]{:S(2)}, u32[]{:S(2)}) collective-permute-start(f32[1,256]{1,0:T(1,128)S(1)} %bitcast.19), channel_id=1, source_target_pairs={{0,32},{32,64},{64,96},{96,0},{1,33},{33,65},{65,97},{97,1},{2,34}... | collective-permute-start | bytes 3080 | tf_op jit(solution)/shard_map/ppermute | solution.py:365
  103.0 5.2 %collective-permute-start.12 = (f32[1,256]{1,0:T(1,128)S(1)}, f32[1,256]{1,0:T(1,128)S(1)}, u32[]{:S(2)}, u32[]{:S(2)}) collective-permute-start(f32[1,256]{1,0:T(1,128)S(1)} %bitcast.20), channel_id=1, source_target_pairs={{0,64},{32,96},{64,0},{96,32},{1,65},{33,97},{65,1},{97,33},{2,66}... | collective-permute-start | bytes 3080 | tf_op jit(solution)/shard_map/ppermute | solution.py:365
  103.0 5.1 %collective-permute-start.13 = (f32[1,256]{1,0:T(1,128)S(1)}, f32[1,256]{1,0:T(1,128)S(1)}, u32[]{:S(2)}, u32[]{:S(2)}) collective-permute-start(f32[1,256]{1,0:T(1,128)S(1)} %bitcast.21), channel_id=1, source_target_pairs={{0,96},{32,0},{64,32},{96,64},{1,97},{33,1},{65,33},{97,65},{2,98}... | collective-permute-start | bytes 3080 | tf_op jit(solution)/shard_map/ppermute | solution.py:365
  107.5 2.1 %collective-permute-start.6 = (f32[256,256]{1,0:T(8,128)S(1)}, f32[256,256]{1,0:T(8,128)S(1)}, u32[]{:S(2)}, u32[]{:S(2)}) collective-permute-start(f32[256,256]{1,0:T(8,128)S(1)} %fusion.11), channel_id=1, source_target_pairs={{0,1},{1,0},{2,3},{3,2},{4,5},{5,4},{6,7},{7,6},{8,9},{9,8},{10,11... | collective-permute-start | bytes 786440 | tf_op jit(solution)/shard_map/ppermute | solution.py:360
  108.1 1.4 collective-permute-start.14
  109.6 13.2 %collective-permute-start.7 = (f32[256,256]{1,0:T(8,128)S(1)}, f32[256,256]{1,0:T(8,128)S(1)}, u32[]{:S(2)}, u32[]{:S(2)}) collective-permute-start(f32[256,256]{1,0:T(8,128)S(1)} %add.43), channel_id=1, source_target_pairs={{0,32},{32,64},{64,96},{96,0},{1,33},{33,65},{65,97},{97,1},{2,34}... | collective-permute-start | bytes 786440 | tf_op jit(solution)/shard_map/ppermute | solution.py:365
  111.3 13.9 %collective-permute-start.8 = (f32[256,256]{1,0:T(8,128)S(1)}, f32[256,256]{1,0:T(8,128)S(1)}, u32[]{:S(2)}, u32[]{:S(2)}) collective-permute-start(f32[256,256]{1,0:T(8,128)S(1)} %add.43), channel_id=1, source_target_pairs={{0,64},{32,96},{64,0},{96,32},{1,65},{33,97},{65,1},{97,33},{2,66}... | collective-permute-start | bytes 786440 | tf_op jit(solution)/shard_map/ppermute | solution.py:365
  113.4 11.7 %collective-permute-start.9 = (f32[256,256]{1,0:T(8,128)S(1)}, f32[256,256]{1,0:T(8,128)S(1)}, u32[]{:S(2)}, u32[]{:S(2)}) collective-permute-start(f32[256,256]{1,0:T(8,128)S(1)} %add.43), channel_id=1, source_target_pairs={{0,96},{32,0},{64,32},{96,64},{1,97},{33,1},{65,33},{97,65},{2,98}... | collective-permute-start | bytes 786440 | tf_op jit(solution)/shard_map/ppermute | solution.py:365
  138.8 10.9 %collective-permute-start.15 = (bf16[512,256]{1,0:T(8,128)(2,1)S(1)}, bf16[512,256]{1,0:T(8,128)(2,1)S(1)}, u32[]{:S(2)}, u32[]{:S(2)}) collective-permute-start(bf16[512,256]{1,0:T(8,128)(2,1)S(1)} %get-tuple-element.42), channel_id=1, source_target_pairs={{0,32},{32,64},{64,96},{96,0},{1,33},{33,65},{65,97},{97,1},{2,34}... | collective-permute-start | bytes 786440 | tf_op jit(solution)/shard_map/ppermute | solution.py:365
  139.9 9.8 %collective-permute-start.16 = (bf16[512,256]{1,0:T(8,128)(2,1)S(1)}, bf16[512,256]{1,0:T(8,128)(2,1)S(1)}, u32[]{:S(2)}, u32[]{:S(2)}) collective-permute-start(bf16[512,256]{1,0:T(8,128)(2,1)S(1)} %get-tuple-element.43), channel_id=1, source_target_pairs={{0,64},{32,96},{64,0},{96,32},{1,65},{33,97},{65,1},{97,33},{2,66}... | collective-permute-start | bytes 786440 | tf_op jit(solution)/shard_map/ppermute | solution.py:365
  139.9 13.4 %collective-permute-start.17 = (bf16[512,256]{1,0:T(8,128)(2,1)S(1)}, bf16[512,256]{1,0:T(8,128)(2,1)S(1)}, u32[]{:S(2)}, u32[]{:S(2)}) collective-permute-start(bf16[512,256]{1,0:T(8,128)(2,1)S(1)} %get-tuple-element.44), channel_id=1, source_target_pairs={{0,96},{32,0},{64,32},{96,64},{1,97},{33,1},{65,33},{97,65},{2,98}... | collective-permute-start | bytes 786440 | tf_op jit(solution)/shard_map/ppermute | solution.py:365
  142.4 11.0 %collective-permute-start.18 = (f32[256,256]{1,0:T(8,128)S(1)}, f32[256,256]{1,0:T(8,128)S(1)}, u32[]{:S(2)}, u32[]{:S(2)}) collective-permute-start(f32[256,256]{1,0:T(8,128)S(1)} %gram_inverse.3), channel_id=1, source_target_pairs={{0,1},{1,0},{2,3},{3,2},{4,5},{5,4},{6,7},{7,6},{8,9},{9,8},{10,11... | collective-permute-start | bytes 786440 | tf_op jit(solution)/shard_map/ppermute | solution.py:360
  (7 other events, 67.7 us)
where the time goes:
time: 157 us; the launch traced here: 155 us
  starting transfers between devices  60.4 us (38%)
  Pallas kernels  42 us (27%)
  waiting for transfers between devices  34 us (22%)
  local copies, waits for them, and re-layouts  8.13 us (5%)
  matrix products  6.16 us (4%)
  between operations  2.69 us (2%)
    all_to_all x4, starting transfers between devices, exchange(): return lax.all_to_all(value, axes, 0, 0)  34.2 us
    pallas_call x2, Pallas kernels, inverse_of(): pl.pallas_call(inverse_kernel, out_shape=jax.ShapeDtypeStruct((n, n), F32...  27.2 us
    all_to_all x4, waiting for transfers between devices, exchange(): return lax.all_to_all(value, axes, 0, 0)  17.5 us
    ppermute x12, starting transfers between devices, along_groups(): lax.ppermute(value, 'grp', [(p, (p + shift) % size) for p in range(size)])  16.2 us
    ppermute x12, waiting for transfers between devices, along_groups(): lax.ppermute(value, 'grp', [(p, (p + shift) % size) for p in range(size)])  12.1 us
    ppermute x7, starting transfers between devices, to_other_core(): return lax.ppermute(value, 'core', [(0, 1), (1, 0)])  10.1 us
    pallas_call x1, Pallas kernels, mode_two(): pl.pallas_call(mode_two_kernel, out_shape=[jax.ShapeDtypeStruct((part, ra...  7.38 us
    pallas_call x1, Pallas kernels, mode_one(): pl.pallas_call(mode_one_kernel, out_shape=[jax.ShapeDtypeStruct((half, ra...  6.55 us
  transfers between devices with their start and end apart: 23, of which 11 were waited for; matrix products, arithmetic and copies ran while one was open for 5% of the time, Pallas kernels for 18%

commit v1 on v0

v1 whole, which is shorter than its diff:
```python
import jax
import jax.numpy as jnp
from jax import lax
from jax.experimental import pallas as pl
from jax.experimental.pallas import tpu as pltpu
from jax.sharding import Mesh
from jax.sharding import PartitionSpec as P

EDGE = 32
GROUP = 8
B_ROWS = 16 * EDGE
MODE_COST = pl.CostEstimate(flops=15_000_000_000, bytes_accessed=48_000_000, transcendentals=0)
INVERSE_COST = pl.CostEstimate(flops=16_000_000_000, bytes_accessed=50_000_000, transcendentals=0)
VMEM_BYTES = 48 << 20
ALL = ("grp", "x", "z", "core")
PLANE = ("x", "z")
CHIPS = ("grp", "x", "z")
F32 = jnp.float32
BF16 = jnp.bfloat16
HIGHEST = lax.Precision.HIGHEST


def invert_four(p):
    inv_det = 1.0 / (p[0][0] * p[1][1] - p[0][1] * p[0][1])
    a00, a01, a11 = p[1][1] * inv_det, -p[0][1] * inv_det, p[0][0] * inv_det
    t00 = a00 * p[0][2] + a01 * p[1][2]
    t01 = a00 * p[0][3] + a01 * p[1][3]
    t10 = a01 * p[0][2] + a11 * p[1][2]
    t11 = a01 * p[0][3] + a11 * p[1][3]
    s00 = p[2][2] - (p[0][2] * t00 + p[1][2] * t10)
    s01 = p[2][3] - (p[0][2] * t01 + p[1][2] * t11)
    s11 = p[3][3] - (p[0][3] * t01 + p[1][3] * t11)
    inv_det = 1.0 / (s00 * s11 - s01 * s01)
    z00, z01, z11 = s11 * inv_det, -s01 * inv_det, s00 * inv_det
    u00, u01 = t00 * z00 + t01 * z01, t00 * z01 + t01 * z11
    u10, u11 = t10 * z00 + t11 * z01, t10 * z01 + t11 * z11
    x00 = a00 + (u00 * t00 + u01 * t01)
    x01 = a01 + (u00 * t10 + u01 * t11)
    x11 = a11 + (u10 * t10 + u11 * t11)
    return [
        [x00, x01, -u00, -u01],
        [x01, x11, -u10, -u11],
        [-u00, -u10, z00, z01],
        [-u01, -u11, z01, z11],
    ]


def invert_block(w):
    n = w.shape[0]
    row = lax.broadcasted_iota(jnp.int32, (n, n), 0)
    col = lax.broadcasted_iota(jnp.int32, (n, n), 1)
    for k in range(0, n, 4):
        cols = [jnp.broadcast_to(w[:, k + q : k + q + 1], (n, n)) for q in range(4)]
        rows = [w[k + q : k + q + 1, :] for q in range(4)]
        pivot = [[cols[b][k + a : k + a + 1, :] for b in range(4)] for a in range(4)]
        inv = invert_four(pivot)
        lane = col[0:1, :]
        fresh = []
        for a in range(4):
            value = (inv[a][0] * rows[0] + inv[a][1] * rows[1]) + (
                inv[a][2] * rows[2] + inv[a][3] * rows[3]
            )
            for b in range(4):
                value = jnp.where(lane == k + b, inv[a][b], value)
            fresh.append(value)
        in_cols = (col >= k) & (col < k + 4)
        in_rows = (row >= k) & (row < k + 4)
        base = jnp.where(in_cols, 0.0, w)
        update = (cols[0] * fresh[0] + cols[1] * fresh[1]) + (
            cols[2] * fresh[2] + cols[3] * fresh[3]
        )
        out = base - update
        for a in range(4):
            out = jnp.where(row == k + a, fresh[a], out)
        w = out
    return w


def tiles_of(matrix):
    across = matrix.shape[1] // 128
    return [
        (r * across + c, slice(r * 8, r * 8 + 8), slice(c * 128, c * 128 + 128))
        for r in range(matrix.shape[0] // 8)
        for c in range(across)
    ]


def invert(out, work):
    n = work.shape[0]
    width = 64
    row = lax.broadcasted_iota(jnp.int32, (n, n), 0)
    col = lax.broadcasted_iota(jnp.int32, (n, n), 1)
    diag = jnp.where(row == col, work[...], 0.0)
    scale_row = lax.rsqrt(jnp.sum(diag, axis=0, keepdims=True))
    scale_col = lax.rsqrt(jnp.sum(diag, axis=1, keepdims=True))
    work[...] = work[...] * scale_row * scale_col
    for b in range(n // width):
        span = slice(b * width, (b + 1) * width)
        block = invert_block(work[span, span])
        rows = jnp.dot(block, work[span, :], precision=HIGHEST, preferred_element_type=F32)
        parts = [jnp.zeros((width, width), F32)] * (n // width)
        parts[b] = block
        padded = jnp.concatenate(parts, axis=1)
        in_block = (col >= b * width) & (col < (b + 1) * width)
        rows = jnp.where(in_block[0:width], padded, rows)
        left = work[:, span]
        left_row = row[:, 0:width]
        left = jnp.where((left_row >= b * width) & (left_row < (b + 1) * width), 0.0, left)
        base = jnp.where(in_block, 0.0, work[...])
        work[...] = base - jnp.dot(left, rows, precision=HIGHEST, preferred_element_type=F32)
        work[span, :] = rows
    out[...] = work[...] * scale_row * scale_col


def first_inverse_kernel(meta, turn, near, far, out, work):
    @pl.when(turn[0] == 0)
    def _():
        out[...] = jnp.zeros_like(out)

    @pl.when(turn[0] != 0)
    def _():
        for t, rows, cols in tiles_of(work):
            work[rows, cols] = near[t] * far[t]
        invert(out, work)


def second_inverse_kernel(meta, turn, part_0, part_1, part_2, part_3, near, far, out, work):
    n = work.shape[0]

    @pl.when(turn[0] == 0)
    def _():
        out[...] = jnp.zeros_like(out)

    @pl.when(turn[0] != 0)
    def _():
        gram = (part_0[...] + part_1[...]) + (part_2[...] + part_3[...])
        row = lax.broadcasted_iota(jnp.int32, (n, n), 0)
        col = lax.broadcasted_iota(jnp.int32, (n, n), 1)
        diag = jnp.where(row == col, gram, 0.0)
        norm_row = jnp.sqrt(jnp.sum(diag, axis=0, keepdims=True) + 1e-06)
        norm_col = jnp.sqrt(jnp.sum(diag, axis=1, keepdims=True) + 1e-06)
        work[...] = gram / (norm_col * norm_row)
        third_is_near = meta[2] == 1
        for t, rows, cols in tiles_of(work):
            work[rows, cols] = work[rows, cols] * jnp.where(third_is_near, near[t], far[t])
        invert(out, work)


def inverse_of(kernel, name, meta, turn, *arrays):
    n = 256
    return pl.pallas_call(
        kernel,
        out_shape=jax.ShapeDtypeStruct((n, n), F32),
        in_specs=[pl.BlockSpec(memory_space=pltpu.SMEM)] * 2
        + [pl.BlockSpec(memory_space=pltpu.VMEM)] * len(arrays),
        out_specs=pl.BlockSpec(memory_space=pltpu.VMEM),
        scratch_shapes=[pltpu.VMEM((n, n), F32)],
        compiler_params=pltpu.CompilerParams(vmem_limit_bytes=VMEM_BYTES),
        cost_estimate=INVERSE_COST,
        name=name,
    )(meta, turn, *arrays)


def prepare_kernel(meta, b_factor, c_factor, own, gram_keep, gram_send):
    rows = b_factor.shape[0]
    core = meta[2]
    own[0:rows, :] = b_factor[...].astype(BF16)
    own[rows:, :] = c_factor[...].astype(BF16)
    for q, ref in enumerate((b_factor, c_factor)):
        gram = lax.dot_general(
            ref[...],
            ref[...],
            (((0,), (0,)), ((), ())),
            precision=HIGHEST,
            preferred_element_type=F32,
        )

        @pl.when(core == q)
        def _():
            for t, r, c in tiles_of(gram):
                gram_keep[t] = gram[r, c]

        @pl.when(core != q)
        def _():
            for t, r, c in tiles_of(gram):
                gram_send[t] = gram[r, c]


def prepare(meta, b_factor, c_factor):
    rank = b_factor.shape[1]
    rows = b_factor.shape[0] + c_factor.shape[0]
    tiles = jax.ShapeDtypeStruct((rank * rank // 1024, 8, 128), F32)
    return pl.pallas_call(
        prepare_kernel,
        out_shape=[jax.ShapeDtypeStruct((rows, rank), BF16), tiles, tiles],
        in_specs=[pl.BlockSpec(memory_space=pltpu.SMEM)]
        + [pl.BlockSpec(memory_space=pltpu.VMEM)] * 2,
        compiler_params=pltpu.CompilerParams(vmem_limit_bytes=VMEM_BYTES),
        name="prepare",
    )(meta, b_factor, c_factor)


def order_kernel(meta, i_idx, j_idx, order_one, order_two, ends):
    slots = i_idx.shape[0]
    grp, core = meta[1], meta[2]

    def clear(s, carry):
        order_one[s] = 0
        order_two[s] = 0
        return carry

    lax.fori_loop(0, slots, clear, 0, unroll=8)

    def place(s, carry):
        front_one, front_two = carry
        one = ((i_idx[s] >> 1) & 1) ^ core
        two = jnp.where((j_idx[s] >> 4) == grp, 0, 1)
        order_one[jnp.where(one == 1, front_one, slots - 1 - (s - front_one))] = s
        order_two[jnp.where(two == 1, front_two, slots - 1 - (s - front_two))] = s
        return front_one + one, front_two + two

    ends[0], ends[1] = lax.fori_loop(0, meta[0], place, (jnp.int32(0), jnp.int32(0)))


def order_slots(meta, i_index, j_index):
    table = jax.ShapeDtypeStruct(i_index.shape, jnp.int32)
    smem = pl.BlockSpec(memory_space=pltpu.SMEM)
    return pl.pallas_call(
        order_kernel,
        out_shape=[table, table, jax.ShapeDtypeStruct((2,), jnp.int32)],
        in_specs=[smem] * 3,
        out_specs=[smem] * 3,
        name="order_slots",
    )(meta, i_index, j_index)


def block_rows(ref, start):
    return ref[pl.ds(pl.multiple_of(start, EDGE), EDGE), :]


def copy_all(copies):
    for copy in copies:
        copy.start()
    return copies


def wait_all(copies):
    for copy in copies:
        copy.wait()


def for_each_group(first, count, order, blocks, buffer, sems, one_slot):
    slots = order.shape[0]
    groups = (count + GROUP - 1) // GROUP

    def slot_at(place):
        place = jnp.minimum(place, slots - 1)
        return order[place if first else slots - 1 - place]

    def copies(group):
        side = group & 1
        return [
            pltpu.make_async_copy(
                blocks.at[slot_at(group * GROUP + u)], buffer.at[side, u], sems.at[side, u]
            )
            for u in range(GROUP)
        ]

    @pl.when(groups > 0)
    def _():
        copy_all(copies(0))

    def one_group(group, carry):
        @pl.when(group + 1 < groups)
        def _():
            copy_all(copies(group + 1))

        wait_all(copies(group))
        for u in range(GROUP):
            place = group * GROUP + u
            one_slot(buffer[group & 1, u], u, slot_at(place), place < count)
        return carry

    lax.fori_loop(0, groups, one_group, 0)


def mode_one_kernel(
    first,
    meta,
    ends,
    order,
    i_idx,
    j_idx,
    k_idx,
    blocks,
    own_0,
    own_1,
    own_2,
    own_3,
    out,
    buffer,
    table,
    acc,
    sems,
    table_sems,
):
    grp = meta[1]
    own = own_0.shape[0]
    half = out.shape[0]
    count = ends[0] if first else meta[0] - ends[0]
    pieces = copy_all(
        [
            pltpu.make_async_copy(ref, table.at[pl.ds(q * own, own)], table_sems.at[q])
            for q, ref in enumerate((own_0, own_1, own_2, own_3))
        ]
    )
    acc[...] = jnp.zeros_like(acc)
    wait_all(pieces)

    def one_slot(block, u, s, live):
        j, k, i = j_idx[s], k_idx[s], i_idx[s]
        b_rows = block_rows(table, ((grp - (j >> 4)) & 3) * own + (j & 15) * EDGE)
        c_rows = block_rows(table, ((grp - (k >> 2)) & 3) * own + B_ROWS + (k & 3) * EDGE)
        product = (b_rows[:, None, :] * c_rows[None, :, :]).reshape(EDGE * EDGE, -1)
        result = jnp.dot(block, product, preferred_element_type=F32)
        target = jnp.where(live, (i >> 2) * (2 * EDGE) + (i & 1) * EDGE, half)
        acc[pl.ds(pl.multiple_of(target, EDGE), EDGE), :] += result

    for_each_group(first, count, order, blocks, buffer, sems, one_slot)
    out[...] = acc[0:half, :]


def turn_block(block, turned, u):
    lane = lax.broadcasted_iota(jnp.int32, (8, 128), 1)
    low_half = lane < 64
    even_group = (lane // 32) % 2 == 0
    wide = block.astype(F32)
    for jh in range(8):
        t = [wide[il * 8 : il * 8 + 8, jh * 128 : jh * 128 + 128] for il in range(4)]
        m = [None] * 4
        for il in range(2):
            m[il] = jnp.where(low_half, t[il], pltpu.roll(t[il + 2], 64, 1))
            m[il + 2] = jnp.where(low_half, pltpu.roll(t[il], 64, 1), t[il + 2])
        for q in (0, 2):
            j = jh * 4 + q
            turned[u, j * 8 : j * 8 + 8, :] = jnp.where(
                even_group, m[q], pltpu.roll(m[q + 1], 32, 1)
            )
            turned[u, j * 8 + 8 : j * 8 + 16, :] = jnp.where(
                even_group, pltpu.roll(m[q], 96, 1), m[q + 1]
            )
    return jnp.concatenate(
        [turned[u, pl.ds(ih, EDGE, stride=8), :].astype(BF16) for ih in range(8)], axis=1
    )


def mode_two_slots(
    first, meta, ends, order, i_idx, j_idx, k_idx, blocks, owns, a_table, scratch, part
):
    buffer, turned, table, acc, sems, table_sems = scratch
    grp, core = meta[1], meta[2]
    c_rows = table.shape[0] // 4
    half = a_table.shape[0] // 2
    count = ends[1] if first else meta[0] - ends[1]
    pieces = copy_all(
        [
            pltpu.make_async_copy(
                ref.at[pl.ds(B_ROWS, c_rows)],
                table.at[pl.ds(q * c_rows, c_rows)],
                table_sems.at[q],
            )
            for q, ref in enumerate(owns)
        ]
    )
    acc[...] = jnp.zeros_like(acc)
    wait_all(pieces)

    def one_slot(block, u, s, live):
        j, k, i = j_idx[s], k_idx[s], i_idx[s]
        a_rows = block_rows(
            a_table,
            (((i >> 1) & 1) ^ core) * half + (i >> 2) * (2 * EDGE) + (i & 1) * EDGE,
        )
        c_block = block_rows(table, ((grp - (k >> 2)) & 3) * c_rows + (k & 3) * EDGE)
        left = turn_block(block, turned, u)
        product = jnp.concatenate(
            [
                a_rows[il * 8 + ih : il * 8 + ih + 1, :] * c_block
                for ih in range(8)
                for il in range(4)
            ],
            axis=0,
        )
        result = jnp.dot(left, product, preferred_element_type=F32)
        target = (j & 15) * EDGE
        if first:
            target += (((j >> 4) - grp - 1) & 3) * part
        target = jnp.where(live, target, acc.shape[0] - EDGE)
        acc[pl.ds(pl.multiple_of(target, EDGE), EDGE), :] += result

    for_each_group(first, count, order, blocks, buffer, sems, one_slot)


def mode_two_others_kernel(
    meta,
    ends,
    order,
    i_idx,
    j_idx,
    k_idx,
    blocks,
    own_0,
    own_1,
    own_2,
    own_3,
    a_near,
    a_far,
    squares,
    send_1,
    send_2,
    send_3,
    a_table,
    *scratch,
):
    half = a_near.shape[0]
    part = send_1.shape[0]
    col_norm = jnp.sqrt(squares[...] + 1e-06)
    a_table[0:half, :] = (a_near[...] / col_norm).astype(BF16)
    a_table[half : 2 * half, :] = (a_far[...] / col_norm).astype(BF16)
    owns = (own_0, own_1, own_2, own_3)
    mode_two_slots(
        True, meta, ends, order, i_idx, j_idx, k_idx, blocks, owns, a_table, scratch, part
    )
    acc = scratch[3]
    for q, ref in enumerate((send_1, send_2, send_3)):
        ref[...] = acc[q * part : (q + 1) * part, :].astype(BF16)


def mode_two_own_kernel(
    meta,
    ends,
    order,
    i_idx,
    j_idx,
    k_idx,
    blocks,
    own_0,
    own_1,
    own_2,
    own_3,
    a_table,
    keep,
    *scratch,
):
    part = keep.shape[0]
    owns = (own_0, own_1, own_2, own_3)
    mode_two_slots(
        False, meta, ends, order, i_idx, j_idx, k_idx, blocks, owns, a_table, scratch, part
    )
    keep[...] = scratch[3][0:part, :]


def mode_call(kernel, name, scalars, in_place, resident, out_shape, scratch):
    smem, anywhere, vmem = (
        pl.BlockSpec(memory_space=pltpu.SMEM),
        pl.BlockSpec(memory_space=pl.ANY),
        pl.BlockSpec(memory_space=pltpu.VMEM),
    )
    blocks = in_place[0]
    buffer = pltpu.VMEM((2, GROUP) + blocks.shape[1:], blocks.dtype)
    return pl.pallas_call(
        kernel,
        out_shape=out_shape,
        in_specs=[smem] * len(scalars) + [anywhere] * len(in_place) + [vmem] * len(resident),
        out_specs=[vmem] * len(out_shape),
        scratch_shapes=[buffer]
        + scratch
        + [pltpu.SemaphoreType.DMA((2, GROUP)), pltpu.SemaphoreType.DMA((4,))],
        compiler_params=pltpu.CompilerParams(vmem_limit_bytes=VMEM_BYTES),
        cost_estimate=MODE_COST,
        name=name,
    )(*scalars, *in_place, *resident)


def mode_one(first, meta, ends, order, indices, blocks, pieces):
    own, rank = pieces[0].shape
    half = 32 * EDGE

    def kernel(*refs):
        mode_one_kernel(first, *refs)

    [out] = mode_call(
        kernel,
        "mode_one_other_core" if first else "mode_one_own_core",
        (meta, ends, order) + indices,
        [blocks] + pieces,
        [],
        [jax.ShapeDtypeStruct((half, rank), F32)],
        [pltpu.VMEM((4 * own, rank), BF16), pltpu.VMEM((half + EDGE, rank), F32)],
    )
    return out


def mode_two(first, meta, ends, order, indices, blocks, pieces, resident):
    rank = pieces[0].shape[1]
    part = 16 * EDGE
    c_rows = pieces[0].shape[0] - B_ROWS
    sent = jax.ShapeDtypeStruct((part, rank), BF16)
    if first:
        out_shape = [sent] * 3 + [jax.ShapeDtypeStruct((64 * EDGE, rank), BF16)]
    else:
        out_shape = [jax.ShapeDtypeStruct((part, rank), F32)]
    return mode_call(
        mode_two_others_kernel if first else mode_two_own_kernel,
        "mode_two_other_groups" if first else "mode_two_own_group",
        (meta, ends, order) + indices,
        [blocks] + pieces,
        resident,
        out_shape,
        [
            pltpu.VMEM((GROUP, 8 * EDGE, 128), F32),
            pltpu.VMEM((4 * c_rows, rank), BF16),
            pltpu.VMEM(((3 if first else 1) * part + EDGE, rank), F32),
        ],
    )


def to_other_core(value):
    return lax.ppermute(value, "core", [(0, 1), (1, 0)])


def along_groups(value, shift):
    size = lax.axis_size("grp")
    return lax.ppermute(value, "grp", [(p, (p + shift) % size) for p in range(size)])


def exchange(value, axes):
    return lax.all_to_all(value, axes, 0, 0)


def on_device(blocks, i_index, j_index, k_index, block_count, b_factor, c_factor):
    rank = b_factor.shape[1]
    grp, core = lax.axis_index("grp"), lax.axis_index("core")
    plane = lax.axis_size(PLANE)
    chips = lax.axis_size(CHIPS)
    indices = (i_index, j_index, k_index)
    meta = jnp.stack([block_count[0], grp, core])

    own, gram_keep, gram_send = prepare(meta, b_factor, c_factor)
    order_one, order_two, ends = order_slots(meta, i_index, j_index)
    gram_pair = gram_keep + to_other_core(gram_send)
    pieces = [own] + [along_groups(own, q) for q in (1, 2, 3)]
    gram_parts = exchange(gram_pair.reshape(chips, -1, 8, 128), CHIPS)
    send = mode_one(True, meta, ends, order_one, indices, blocks, pieces)
    piece = jnp.sum(gram_parts, axis=0)
    piece, send = lax.optimization_barrier((piece, send))
    spread = jnp.broadcast_to(piece[None], (chips,) + piece.shape)
    spread, order_one = lax.optimization_barrier((spread, order_one))
    gram_near = exchange(spread, CHIPS)
    keep = mode_one(False, meta, ends, order_one, indices, blocks, pieces)
    gram_near, keep = lax.optimization_barrier((gram_near, keep))
    gram_near = gram_near.reshape(-1, 8, 128)
    gram_far = to_other_core(gram_near)

    pair_sum = (keep + to_other_core(send)).astype(BF16)
    arrived = exchange(pair_sum.reshape(plane, -1, rank), PLANE)
    sum_own = jnp.sum(arrived.astype(F32), axis=0)
    sum_near = exchange(jnp.broadcast_to(sum_own[None], (plane,) + sum_own.shape), PLANE)
    sum_near = sum_near.reshape(-1, rank)

    other_count = to_other_core(block_count)
    lighter = (block_count < other_count) | ((block_count == other_count) & (core == 0))
    turn = lighter.astype(jnp.int32)
    inverse = inverse_of(first_inverse_kernel, "first_inverse", meta, turn, gram_near, gram_far)
    inverse = jnp.where(lighter[0], inverse, to_other_core(inverse))
    a_update = jnp.dot(sum_own, inverse, precision=HIGHEST)

    sum_far = to_other_core(sum_near)
    a_near = jnp.dot(sum_near, inverse, precision=HIGHEST)
    squares = jnp.sum(a_near * a_near, axis=0, keepdims=True)
    squares = squares + along_groups(squares, 1) + along_groups(squares, 2) + along_groups(squares, 3)
    squares = squares + to_other_core(squares)
    a_far = jnp.dot(sum_far, inverse, precision=HIGHEST)
    gram_core = jnp.dot(a_near.T, a_near, precision=HIGHEST)
    gram_plane = gram_core + to_other_core(gram_core)
    gram_parts = [gram_plane] + [along_groups(gram_plane, q) for q in (1, 2, 3)]

    *sends, a_table = mode_two(
        True, meta, ends, order_two, indices, blocks, pieces, [a_near, a_far, squares]
    )
    gram_parts, sends = lax.optimization_barrier((gram_parts, sends))
    inverse = inverse_of(
        second_inverse_kernel, "second_inverse", meta, turn, *gram_parts, gram_near, gram_far
    )
    inverse, sends, a_table = lax.optimization_barrier((inverse, sends, a_table))
    [keep] = mode_two(False, meta, ends, order_two, indices, blocks, pieces, [a_table])
    inverse = jnp.where(lighter[0], inverse, to_other_core(inverse))
    arrived = [along_groups(value, q + 1) for q, value in enumerate(sends)]
    arrived, keep = lax.optimization_barrier((arrived, keep))
    arrived = [value.astype(F32) for value in arrived]
    own_two = keep + arrived[0] + arrived[1] + arrived[2]
    b_update = jnp.dot(own_two, inverse, precision=HIGHEST)
    return a_update, b_update


def solution(mesh):
    groups, columns = mesh.shape["grp"], mesh.shape["col"]
    side = round((columns // 2) ** 0.5)
    fine = Mesh(mesh.devices.reshape(groups, side, side, 2), ALL)
    row, flat = P(ALL, None), P(ALL)
    return jax.shard_map(
        on_device,
        mesh=fine,
        in_specs=(P(ALL, None, None), flat, flat, flat, flat, row, row),
        out_specs=(row, row),
        check_vma=False,
    )
```

time: 157 us -> 163 us (1.038)
  starting transfers between devices: 60.4 us -> 86.6 us
  waiting for transfers between devices: 34 us -> 18.2 us
  Pallas kernels: 42 us -> 34.4 us
  other arithmetic: 1.47 us -> 3.18 us
    ppermute x12, starting transfers between devices: 16.2 us -> 29.3 us  [along_groups(): lax.ppermute(value, 'grp', [(p, (p + shift) % size) for p in range(size)])]
    pallas_call x4 -> x7, Pallas kernels: 41.2 us -> 32.4 us  [the longest x4 28.4 us: mode_call(): pl.pallas_call(kernel, out_shape=out_shape, in_specs=[smem] * len(scalars...]
    all_to_all x4, starting transfers between devices: 34.2 us -> 41 us  [exchange(): return lax.all_to_all(value, axes, 0, 0)]
    all_to_all x4, waiting for transfers between devices: 17.5 us -> 10.8 us  [exchange(): return lax.all_to_all(value, axes, 0, 0)]
    ppermute x7 -> x9, starting transfers between devices: 10.1 us -> 16.3 us  [to_other_core(): return lax.ppermute(value, 'core', [(0, 1), (1, 0)])]
    ppermute x12, waiting for transfers between devices: 12.1 us -> 6.29 us  [along_groups(): lax.ppermute(value, 'grp', [(p, (p + shift) % size) for p in range(size)])]
    ppermute x7 -> x9, waiting for transfers between devices: 4.36 us -> 1.12 us  [to_other_core(): return lax.ppermute(value, 'core', [(0, 1), (1, 0)])]
    unnamed x16 -> x38, local copies, waits for them, and re-layouts: 3.99 us -> 6.84 us
  transfers between devices with their start and end apart: 23 -> 25, of which waited for: 11 -> 9; matrix products, arithmetic and copies ran while one was open for 5% -> 4% of each run, Pallas kernels for 18% -> 20%
where the time goes in v1:
time: 163 us; the launch traced here: 160 us
  starting transfers between devices  86.6 us (53%)
  Pallas kernels  34.4 us (21%)
  waiting for transfers between devices  18.2 us (11%)
  local copies, waits for them, and re-layouts  8.66 us (5%)
  matrix products  6.17 us (4%)
  other arithmetic  3.18 us (2%)
  between operations  2.9 us (2%)
    all_to_all x4, starting transfers between devices, exchange(): return lax.all_to_all(value, axes, 0, 0)  41 us
    ppermute x12, starting transfers between devices, along_groups(): lax.ppermute(value, 'grp', [(p, (p + shift) % size) for p in range(size)])  29.3 us
    pallas_call x4, Pallas kernels, mode_call(): pl.pallas_call(kernel, out_shape=out_shape, in_specs=[smem] * len(scalars...  28.4 us
    ppermute x9, starting transfers between devices, to_other_core(): return lax.ppermute(value, 'core', [(0, 1), (1, 0)])  16.3 us
    all_to_all x4, waiting for transfers between devices, exchange(): return lax.all_to_all(value, axes, 0, 0)  10.8 us
    unnamed x38, local copies, waits for them, and re-layouts  6.84 us
    ppermute x12, waiting for transfers between devices, along_groups(): lax.ppermute(value, 'grp', [(p, (p + shift) % size) for p in range(size)])  6.29 us
  transfers between devices with their start and end apart: 25, of which 9 were waited for; matrix products, arithmetic and copies ran while one was open for 4% of the time, Pallas kernels for 20%

profile of v1, /device:TPU:1, one launch (start us, length us, event | category | flops | bytes accessed | tf_op | source)
XLA Modules:
  0.0 160.1 jit_solution(16643016141304667601)
XLA Ops:
  3.3 2.0 %prepare.1 = (bf16[640,256]{1,0:T(8,128)(2,1)S(1)}, f32[64,8,128]{2,1,0:T(8,128)S(1)}, f32[64,8,128]{2,1,0:T(8,128)S(1)}) custom-call(s32[3]{0:T(128)S(1)} %pad_add_fusion.meta.refs_0_, f32[512,256]{1,0:T(8,128)S(1)} %copy-done, f32[128,256]{1,0:T(8,128)S(1)} %copy-done.1), custom_call_target="tpu_custom_call" | custom-call | tf_op jit(solution)/shard_map/prepare/pallas_call | solution.py:193
  5.3 1.5 collective-permute-start
  8.2 2.6 %collective-permute-start.2 = (bf16[640,256]{1,0:T(8,128)(2,1)S(1)}, bf16[640,256]{1,0:T(8,128)(2,1)S(1)}, u32[]{:S(2)}, u32[]{:S(2)}) collective-permute-start(bf16[640,256]{1,0:T(8,128)(2,1)S(1)} %get-tuple-element.38.refs_7_.own_0), channel_id=1, source_target_pairs={{0,64},{32,96},{64,0},{96,32},{1,65},{33,97},{65,1},{97,33},{2,66}... | collective-permute-start | bytes 983048 | tf_op jit(solution)/shard_map/ppermute | solution.py:534
  11.9 2.6 %order_slots.1 = (s32[192]{0:T(256)}, s32[192]{0:T(256)}, s32[2]{0:T(128)}) custom-call(s32[3]{0:T(128)} %copy-done.2, s32[192]{0:T(256)} %i_idx.5, s32[192]{0:T(256)} %j_idx.5), custom_call_target="tpu_custom_call" | custom-call | tf_op jit(solution)/shard_map/order_slots/pallas_call | solution.py:228
  15.3 10.1 %all-to-all-start = ((f32[64,1,8,128]{3,2,1,0:T(8,128)}), f32[64,1,8,128]{3,2,1,0:T(8,128)S(1)}, u32[]{:S(2)}, u32[]{:S(2)}) async-start(f32[64,1,8,128]{3,2,1,0:T(8,128)} %add_bitcast_fusion), calls=%async_computation | async-start | bytes 524288 | tf_op jit(solution)/shard_map/all_to_all | solution.py:538
  29.6 5.9 %mode_one_other_core.1 = f32[1024,256]{1,0:T(8,128)S(1)} custom-call(s32[3]{0:T(128)S(1)} %copy-done.3, s32[2]{0:T(128)S(1)} %copy-done.17, s32[192]{0:T(256)S(1)} %copy-done.15, s32[192]{0:T(256)S(1)} %copy-done.5, s32[192]{0:T(256)S(1)} %copy-done.7, s32[192]{0:T(256)S(1)} %copy-done.12, bf16[192,32,1024]{2,1,0:T(8,128)(2,1)} %blocks.3, ...), custom_call_target="tpu_custom_call" | custom-call | flops 15000000512 | bytes 48000000 | tf_op jit(solution)/shard_map/mode_one_other_core/pallas_call | solution.py:471
  36.8 15.3 %all-to-all-start.1 = ((f32[64,1,8,128]{3,2,1,0:T(8,128)}), f32[64,1,8,128]{3,2,1,0:T(8,128)S(1)}, u32[]{:S(2)}, u32[]{:S(2)}) async-start(f32[64,1,8,128]{3,2,1,0:T(8,128)} %broadcast_in_dim.18), calls=%async_computation.1 | async-start | bytes 524288 | tf_op jit(solution)/shard_map/all_to_all | solution.py:538
  53.2 7.8 %mode_one_own_core.1 = f32[1024,256]{1,0:T(8,128)S(1)} custom-call(s32[3]{0:T(128)S(1)} %copy-done.4, s32[2]{0:T(128)S(1)} %copy-done.18, s32[192]{0:T(256)S(1)} %copy-done.16, s32[192]{0:T(256)S(1)} %copy-done.6, s32[192]{0:T(256)S(1)} %copy-done.8, s32[192]{0:T(256)S(1)} %copy-done.13, bf16[192,32,1024]{2,1,0:T(8,128)(2,1)} %blocks.3, ...), custom_call_target="tpu_custom_call" | custom-call | flops 15000000512 | bytes 48000000 | tf_op jit(solution)/shard_map/mode_one_own_core/pallas_call | solution.py:471
  61.5 2.1 %add_convert_fusion = bf16[1024,256]{1,0:T(8,128)(2,1)} fusion(f32[1024,256]{1,0:T(8,128)S(1)} %mode_one_own_core.1, f32[1024,256]{1,0:T(8,128)} %collective-permute-done.4), kind=kLoop, calls=%fused_computation.2 | loop fusion | flops 524288 | bytes 2621440 | tf_op jit(solution)/shard_map/convert_element_type | solution.py:565
  63.7 12.0 %all-to-all-start.2 = ((bf16[16,64,256]{2,1,0:T(8,128)(2,1)}), bf16[16,64,256]{2,1,0:T(8,128)(2,1)S(1)}, u32[]{:S(2)}, u32[]{:S(2)}) async-start(bf16[16,64,256]{2,1,0:T(8,128)(2,1)} %bitcast.6), calls=%async_computation.2 | async-start | bytes 1048576 | tf_op jit(solution)/shard_map/all_to_all | solution.py:538
  78.6 6.0 %all-to-all-done.2 = bf16[16,64,256]{2,1,0:T(8,128)(2,1)S(1)} async-done(((bf16[16,64,256]{2,1,0:T(8,128)(2,1)}), bf16[16,64,256]{2,1,0:T(8,128)(2,1)S(1)}, u32[]{:S(2)}, u32[]{:S(2)}) %all-to-all-start.2) | async-done | bytes 524320 | tf_op jit(solution)/shard_map/all_to_all | solution.py:538
  85.8 3.7 %all-to-all-start.3 = ((f32[16,64,256]{2,1,0:T(8,128)}), f32[16,64,256]{2,1,0:T(8,128)S(1)}, u32[]{:S(2)}, u32[]{:S(2)}) async-start(f32[16,64,256]{2,1,0:T(8,128)} %broadcast_in_dim.19), calls=%async_computation.3 | async-start | bytes 2097152 | tf_op jit(solution)/shard_map/all_to_all | solution.py:538
  90.2 11.0 %collective-permute-start.7 = (f32[256,256]{1,0:T(8,128)S(1)}, f32[256,256]{1,0:T(8,128)S(1)}, u32[]{:S(2)}, u32[]{:S(2)}) collective-permute-start(f32[256,256]{1,0:T(8,128)S(1)} %first_inverse.1), channel_id=1, source_target_pairs={{0,1},{1,0},{2,3},{3,2},{4,5},{5,4},{6,7},{7,6},{8,9},{9,8},{10,11... | collective-permute-start | bytes 786440 | tf_op jit(solution)/shard_map/ppermute | solution.py:529
  101.2 3.7 %all-to-all-done.3 = f32[16,64,256]{2,1,0:T(8,128)S(1)} async-done(((f32[16,64,256]{2,1,0:T(8,128)}), f32[16,64,256]{2,1,0:T(8,128)S(1)}, u32[]{:S(2)}, u32[]{:S(2)}) %all-to-all-start.3) | async-done | bytes 1048608 | tf_op jit(solution)/shard_map/all_to_all | solution.py:538
  106.0 1.9 %collective-permute-start.13 = (f32[1,256]{1,0:T(1,128)S(1)}, f32[1,256]{1,0:T(1,128)S(1)}, u32[]{:S(2)}, u32[]{:S(2)}) collective-permute-start(f32[1,256]{1,0:T(1,128)S(1)} %bitcast.27), channel_id=1, source_target_pairs={{0,32},{32,64},{64,96},{96,0},{1,33},{33,65},{65,97},{97,1},{2,34}... | collective-permute-start | bytes 3080 | tf_op jit(solution)/shard_map/ppermute | solution.py:534
  107.9 2.5 %collective-permute-start.15 = (f32[1,256]{1,0:T(1,128)S(1)}, f32[1,256]{1,0:T(1,128)S(1)}, u32[]{:S(2)}, u32[]{:S(2)}) collective-permute-start(f32[1,256]{1,0:T(1,128)S(1)} %bitcast.29), channel_id=1, source_target_pairs={{0,96},{32,0},{64,32},{96,64},{1,97},{33,1},{65,33},{97,65},{2,98}... | collective-permute-start | bytes 3080 | tf_op jit(solution)/shard_map/ppermute | solution.py:534
  110.4 1.8 %fusion.10 = f32[256,256]{1,0:T(8,128)S(1)} fusion(f32[1024,256]{1,0:T(8,128)S(1)} %get-tuple-element.67.a_near), kind=kOutput, calls=%fused_computation.17 | convolution fusion | flops 805306368 | bytes 1310720 | tf_op jit(solution)/shard_map/dot_general | solution.py:584
  114.6 1.5 collective-permute-start.10
  118.6 9.4 %mode_two_other_groups.1 = (bf16[512,256]{1,0:T(8,128)(2,1)S(1)}, bf16[512,256]{1,0:T(8,128)(2,1)S(1)}, bf16[512,256]{1,0:T(8,128)(2,1)S(1)}, bf16[2048,256]{1,0:T(8,128)(2,1)S(1)}) custom-call(s32[3]{0:T(128)S(1)} %copy-done.4, s32[2]{0:T(128)S(1)} %copy-done.18, s32[192]{0:T(256)S(1)} %copy-done.14, s32[192]{0:T(256)S(1)} %copy-done.6, s32[192]{0:T(256)S(1)} %copy-done.8, ...), custom_call_target="tpu_custom_call" | custom-call | flops 15000000512 | bytes 48000000 | tf_op jit(solution)/shard_map/mode_two_other_groups/pallas_call | solution.py:471
  131.8 15.7 %collective-permute-start.18 = (bf16[512,256]{1,0:T(8,128)(2,1)S(1)}, bf16[512,256]{1,0:T(8,128)(2,1)S(1)}, u32[]{:S(2)}, u32[]{:S(2)}) collective-permute-start(bf16[512,256]{1,0:T(8,128)(2,1)S(1)} %get-tuple-element.58), channel_id=1, source_target_pairs={{0,64},{32,96},{64,0},{96,32},{1,65},{33,97},{65,1},{97,33},{2,66}... | collective-permute-start | bytes 786440 | tf_op jit(solution)/shard_map/ppermute | solution.py:534
  147.5 1.8 %collective-permute-start.20 = (f32[256,256]{1,0:T(8,128)S(1)}, f32[256,256]{1,0:T(8,128)S(1)}, u32[]{:S(2)}, u32[]{:S(2)}) collective-permute-start(f32[256,256]{1,0:T(8,128)S(1)} %second_inverse.1), channel_id=1, source_target_pairs={{0,1},{1,0},{2,3},{3,2},{4,5},{5,4},{6,7},{7,6},{8,9},{9,8},{10,11... | collective-permute-start | bytes 786440 | tf_op jit(solution)/shard_map/ppermute | solution.py:529
  149.2 5.3 %mode_two_own_group.1 = f32[512,256]{1,0:T(8,128)S(1)} custom-call(s32[3]{0:T(128)S(1)} %copy-done.4, s32[2]{0:T(128)S(1)} %copy-done.18, s32[192]{0:T(256)S(1)} %copy-done.14, s32[192]{0:T(256)S(1)} %copy-done.6, s32[192]{0:T(256)S(1)} %copy-done.8, s32[192]{0:T(256)S(1)} %copy-done.13, bf16[192,32,1024]{2,1,0:T(8,128)(2,1)} %blocks.3, ...), custom_call_target="tpu_custom_call" | custom-call | flops 15000000512 | bytes 48000000 | tf_op jit(solution)/shard_map/mode_two_own_group/pallas_call | solution.py:471
  154.6 4.1 %collective-permute-done.18 = bf16[512,256]{1,0:T(8,128)(2,1)S(1)} collective-permute-done((bf16[512,256]{1,0:T(8,128)(2,1)S(1)}, bf16[512,256]{1,0:T(8,128)(2,1)S(1)}, u32[]{:S(2)}, u32[]{:S(2)}) %collective-permute-start.18) | collective-permute-done | bytes 262176 | tf_op jit(solution)/shard_map/ppermute | solution.py:534
  158.7 1.5 fusion
  (88 shorter events, 25.5 us)
Async XLA Ops:
  5.3 9.2 %collective-permute-start = (f32[64,8,128]{2,1,0:T(8,128)S(1)}, f32[64,8,128]{2,1,0:T(8,128)S(1)}, u32[]{:S(2)}, u32[]{:S(2)}) collective-permute-start(f32[64,8,128]{2,1,0:T(8,128)S(1)} %get-tuple-element.35), channel_id=1, source_target_pairs={{0,1},{1,0},{2,3},{3,2},{4,5},{5,4},{6,7},{7,6},{8,9},{9,8},{10,11... | collective-permute-start | bytes 786440 | tf_op jit(solution)/shard_map/ppermute | solution.py:529
  6.8 18.6 %collective-permute-start.1 = (bf16[640,256]{1,0:T(8,128)(2,1)S(1)}, bf16[640,256]{1,0:T(8,128)(2,1)S(1)}, u32[]{:S(2)}, u32[]{:S(2)}) collective-permute-start(bf16[640,256]{1,0:T(8,128)(2,1)S(1)} %get-tuple-element.38.refs_7_.own_0), channel_id=1, source_target_pairs={{0,32},{32,64},{64,96},{96,0},{1,33},{33,65},{65,97},{97,1},{2,34}... | collective-permute-start | bytes 983048 | tf_op jit(solution)/shard_map/ppermute | solution.py:534
  8.2 17.4 %collective-permute-start.2 = (bf16[640,256]{1,0:T(8,128)(2,1)S(1)}, bf16[640,256]{1,0:T(8,128)(2,1)S(1)}, u32[]{:S(2)}, u32[]{:S(2)}) collective-permute-start(bf16[640,256]{1,0:T(8,128)(2,1)S(1)} %get-tuple-element.38.refs_7_.own_0), channel_id=1, source_target_pairs={{0,64},{32,96},{64,0},{96,32},{1,65},{33,97},{65,1},{97,33},{2,66}... | collective-permute-start | bytes 983048 | tf_op jit(solution)/shard_map/ppermute | solution.py:534
  10.8 14.8 %collective-permute-start.3 = (bf16[640,256]{1,0:T(8,128)(2,1)S(1)}, bf16[640,256]{1,0:T(8,128)(2,1)S(1)}, u32[]{:S(2)}, u32[]{:S(2)}) collective-permute-start(bf16[640,256]{1,0:T(8,128)(2,1)S(1)} %get-tuple-element.38.refs_7_.own_0), channel_id=1, source_target_pairs={{0,96},{32,0},{64,32},{96,64},{1,97},{33,1},{65,33},{97,65},{2,98}... | collective-permute-start | bytes 983048 | tf_op jit(solution)/shard_map/ppermute | solution.py:534
  15.3 20.8 %all-to-all-start = ((f32[64,1,8,128]{3,2,1,0:T(8,128)}), f32[64,1,8,128]{3,2,1,0:T(8,128)S(1)}, u32[]{:S(2)}, u32[]{:S(2)}) async-start(f32[64,1,8,128]{3,2,1,0:T(8,128)} %add_bitcast_fusion), calls=%async_computation | async-start | bytes 524288 | tf_op jit(solution)/shard_map/all_to_all | solution.py:538
  36.8 24.7 %all-to-all-start.1 = ((f32[64,1,8,128]{3,2,1,0:T(8,128)}), f32[64,1,8,128]{3,2,1,0:T(8,128)S(1)}, u32[]{:S(2)}, u32[]{:S(2)}) async-start(f32[64,1,8,128]{3,2,1,0:T(8,128)} %broadcast_in_dim.18), calls=%async_computation.1 | async-start | bytes 524288 | tf_op jit(solution)/shard_map/all_to_all | solution.py:538
  52.1 9.4 %collective-permute-start.4 = (f32[1024,256]{1,0:T(8,128)S(1)}, f32[1024,256]{1,0:T(8,128)}, u32[]{:S(2)}, u32[]{:S(2)}) collective-permute-start(f32[1024,256]{1,0:T(8,128)S(1)} %mode_one_other_core.1), channel_id=1, source_target_pairs={{0,1},{1,0},{2,3},{3,2},{4,5},{5,4},{6,7},{7,6},{8,9},{9,8},{10,11... | collective-permute-start | bytes 3145736 | tf_op jit(solution)/shard_map/ppermute | solution.py:529
  63.7 20.9 %all-to-all-start.2 = ((bf16[16,64,256]{2,1,0:T(8,128)(2,1)}), bf16[16,64,256]{2,1,0:T(8,128)(2,1)S(1)}, u32[]{:S(2)}, u32[]{:S(2)}) async-start(bf16[16,64,256]{2,1,0:T(8,128)(2,1)} %bitcast.6), calls=%async_computation.2 | async-start | bytes 1048576 | tf_op jit(solution)/shard_map/all_to_all | solution.py:538
  75.6 13.8 %collective-permute-start.6 = (f32[64,8,128]{2,1,0:T(8,128)S(1)}, f32[64,8,128]{2,1,0:T(8,128)S(1)}, u32[]{:S(2)}, u32[]{:S(2)}) collective-permute-start(f32[64,8,128]{2,1,0:T(8,128)S(1)} %bitcast.22), channel_id=1, source_target_pairs={{0,1},{1,0},{2,3},{3,2},{4,5},{5,4},{6,7},{7,6},{8,9},{9,8},{10,11... | collective-permute-start | bytes 786440 | tf_op jit(solution)/shard_map/ppermute | solution.py:529
  75.7 1.6 collective-permute-start.5
  85.8 19.2 %all-to-all-start.3 = ((f32[16,64,256]{2,1,0:T(8,128)}), f32[16,64,256]{2,1,0:T(8,128)S(1)}, u32[]{:S(2)}, u32[]{:S(2)}) async-start(f32[16,64,256]{2,1,0:T(8,128)} %broadcast_in_dim.19), calls=%async_computation.3 | async-start | bytes 2097152 | tf_op jit(solution)/shard_map/all_to_all | solution.py:538
  90.2 14.8 %collective-permute-start.7 = (f32[256,256]{1,0:T(8,128)S(1)}, f32[256,256]{1,0:T(8,128)S(1)}, u32[]{:S(2)}, u32[]{:S(2)}) collective-permute-start(f32[256,256]{1,0:T(8,128)S(1)} %first_inverse.1), channel_id=1, source_target_pairs={{0,1},{1,0},{2,3},{3,2},{4,5},{5,4},{6,7},{7,6},{8,9},{9,8},{10,11... | collective-permute-start | bytes 786440 | tf_op jit(solution)/shard_map/ppermute | solution.py:529
  105.0 12.6 %collective-permute-start.12 = (f32[1024,256]{1,0:T(8,128)S(1)}, f32[1024,256]{1,0:T(8,128)S(1)}, u32[]{:S(2)}, u32[]{:S(2)}) collective-permute-start(f32[1024,256]{1,0:T(8,128)S(1)} %bitcast.25), channel_id=1, source_target_pairs={{0,1},{1,0},{2,3},{3,2},{4,5},{5,4},{6,7},{7,6},{8,9},{9,8},{10,11... | collective-permute-start | bytes 3145736 | tf_op jit(solution)/shard_map/ppermute | solution.py:529
  106.0 7.0 %collective-permute-start.13 = (f32[1,256]{1,0:T(1,128)S(1)}, f32[1,256]{1,0:T(1,128)S(1)}, u32[]{:S(2)}, u32[]{:S(2)}) collective-permute-start(f32[1,256]{1,0:T(1,128)S(1)} %bitcast.27), channel_id=1, source_target_pairs={{0,32},{32,64},{64,96},{96,0},{1,33},{33,65},{65,97},{97,1},{2,34}... | collective-permute-start | bytes 3080 | tf_op jit(solution)/shard_map/ppermute | solution.py:534
  107.9 5.0 %collective-permute-start.14 = (f32[1,256]{1,0:T(1,128)S(1)}, f32[1,256]{1,0:T(1,128)S(1)}, u32[]{:S(2)}, u32[]{:S(2)}) collective-permute-start(f32[1,256]{1,0:T(1,128)S(1)} %bitcast.28), channel_id=1, source_target_pairs={{0,64},{32,96},{64,0},{96,32},{1,65},{33,97},{65,1},{97,33},{2,66}... | collective-permute-start | bytes 3080 | tf_op jit(solution)/shard_map/ppermute | solution.py:534
  107.9 5.0 %collective-permute-start.15 = (f32[1,256]{1,0:T(1,128)S(1)}, f32[1,256]{1,0:T(1,128)S(1)}, u32[]{:S(2)}, u32[]{:S(2)}) collective-permute-start(f32[1,256]{1,0:T(1,128)S(1)} %bitcast.29), channel_id=1, source_target_pairs={{0,96},{32,0},{64,32},{96,64},{1,97},{33,1},{65,33},{97,65},{2,98}... | collective-permute-start | bytes 3080 | tf_op jit(solution)/shard_map/ppermute | solution.py:534
  112.3 2.3 %collective-permute-start.8 = (f32[256,256]{1,0:T(8,128)S(1)}, f32[256,256]{1,0:T(8,128)S(1)}, u32[]{:S(2)}, u32[]{:S(2)}) collective-permute-start(f32[256,256]{1,0:T(8,128)S(1)} %fusion.10), channel_id=1, source_target_pairs={{0,1},{1,0},{2,3},{3,2},{4,5},{5,4},{6,7},{7,6},{8,9},{9,8},{10,11... | collective-permute-start | bytes 786440 | tf_op jit(solution)/shard_map/ppermute | solution.py:529
  114.6 13.5 %collective-permute-start.10 = (f32[256,256]{1,0:T(8,128)S(1)}, f32[256,256]{1,0:T(8,128)S(1)}, u32[]{:S(2)}, u32[]{:S(2)}) collective-permute-start(f32[256,256]{1,0:T(8,128)S(1)} %add.32.part_0), channel_id=1, source_target_pairs={{0,64},{32,96},{64,0},{96,32},{1,65},{33,97},{65,1},{97,33},{2,66}... | collective-permute-start | bytes 786440 | tf_op jit(solution)/shard_map/ppermute | solution.py:534
  116.1 12.9 %collective-permute-start.11 = (f32[256,256]{1,0:T(8,128)S(1)}, f32[256,256]{1,0:T(8,128)S(1)}, u32[]{:S(2)}, u32[]{:S(2)}) collective-permute-start(f32[256,256]{1,0:T(8,128)S(1)} %add.32.part_0), channel_id=1, source_target_pairs={{0,96},{32,0},{64,32},{96,64},{1,97},{33,1},{65,33},{97,65},{2,98}... | collective-permute-start | bytes 786440 | tf_op jit(solution)/shard_map/ppermute | solution.py:534
  117.4 12.6 %collective-permute-start.9 = (f32[256,256]{1,0:T(8,128)S(1)}, f32[256,256]{1,0:T(8,128)S(1)}, u32[]{:S(2)}, u32[]{:S(2)}) collective-permute-start(f32[256,256]{1,0:T(8,128)S(1)} %add.32.part_0), channel_id=1, source_target_pairs={{0,32},{32,64},{64,96},{96,0},{1,33},{33,65},{65,97},{97,1},{2,34}... | collective-permute-start | bytes 786440 | tf_op jit(solution)/shard_map/ppermute | solution.py:534
  130.6 23.9 %collective-permute-start.17 = (bf16[512,256]{1,0:T(8,128)(2,1)S(1)}, bf16[512,256]{1,0:T(8,128)(2,1)S(1)}, u32[]{:S(2)}, u32[]{:S(2)}) collective-permute-start(bf16[512,256]{1,0:T(8,128)(2,1)S(1)} %get-tuple-element.57), channel_id=1, source_target_pairs={{0,32},{32,64},{64,96},{96,0},{1,33},{33,65},{65,97},{97,1},{2,34}... | collective-permute-start | bytes 786440 | tf_op jit(solution)/shard_map/ppermute | solution.py:534
  131.8 26.9 %collective-permute-start.18 = (bf16[512,256]{1,0:T(8,128)(2,1)S(1)}, bf16[512,256]{1,0:T(8,128)(2,1)S(1)}, u32[]{:S(2)}, u32[]{:S(2)}) collective-permute-start(bf16[512,256]{1,0:T(8,128)(2,1)S(1)} %get-tuple-element.58), channel_id=1, source_target_pairs={{0,64},{32,96},{64,0},{96,32},{1,65},{33,97},{65,1},{97,33},{2,66}... | collective-permute-start | bytes 786440 | tf_op jit(solution)/shard_map/ppermute | solution.py:534
  147.5 11.2 %collective-permute-start.19 = (bf16[512,256]{1,0:T(8,128)(2,1)S(1)}, bf16[512,256]{1,0:T(8,128)(2,1)S(1)}, u32[]{:S(2)}, u32[]{:S(2)}) collective-permute-start(bf16[512,256]{1,0:T(8,128)(2,1)S(1)} %get-tuple-element.59), channel_id=1, source_target_pairs={{0,96},{32,0},{64,32},{96,64},{1,97},{33,1},{65,33},{97,65},{2,98}... | collective-permute-start | bytes 786440 | tf_op jit(solution)/shard_map/ppermute | solution.py:534
  147.5 11.2 %collective-permute-start.20 = (f32[256,256]{1,0:T(8,128)S(1)}, f32[256,256]{1,0:T(8,128)S(1)}, u32[]{:S(2)}, u32[]{:S(2)}) collective-permute-start(f32[256,256]{1,0:T(8,128)S(1)} %second_inverse.1), channel_id=1, source_target_pairs={{0,1},{1,0},{2,3},{3,2},{4,5},{5,4},{6,7},{7,6},{8,9},{9,8},{10,11... | collective-permute-start | bytes 786440 | tf_op jit(solution)/shard_map/ppermute | solution.py:529
  (20 other events, 221.2 us)

commit v2 on v1

--- a/solution.py
+++ b/solution.py
@@ -8,13 +8,18 @@
 
 EDGE = 32
 GROUP = 8
+DEPTH = 4
 B_ROWS = 16 * EDGE
+C_ROWS = 4 * EDGE
+COUNT_ROWS = 16
 MODE_COST = pl.CostEstimate(flops=15_000_000_000, bytes_accessed=48_000_000, transcendentals=0)
+LAST_PASS_COST = pl.CostEstimate(flops=2_000_000_000, bytes_accessed=6_000_000, transcendentals=0)
 INVERSE_COST = pl.CostEstimate(flops=16_000_000_000, bytes_accessed=50_000_000, transcendentals=0)
 VMEM_BYTES = 48 << 20
 ALL = ("grp", "x", "z", "core")
 PLANE = ("x", "z")
 CHIPS = ("grp", "x", "z")
+RING = ("grp", "core")
 F32 = jnp.float32
 BF16 = jnp.bfloat16
 HIGHEST = lax.Precision.HIGHEST
@@ -112,26 +117,36 @@
     out[...] = work[...] * scale_row * scale_col
 
 
-def first_inverse_kernel(meta, turn, near, far, out, work):
-    @pl.when(turn[0] == 0)
+def takes_turn(meta, ring, other_ring):
+    mine, other = jnp.max(ring[...]), jnp.max(other_ring[...])
+    return (mine < other) | ((mine == other) & (meta[2] == 0))
+
+
+def first_inverse_kernel(meta, ring, other_ring, near, far, out, work):
+    mine = takes_turn(meta, ring, other_ring)
+
+    @pl.when(jnp.logical_not(mine))
     def _():
         out[...] = jnp.zeros_like(out)
 
-    @pl.when(turn[0] != 0)
+    @pl.when(mine)
     def _():
         for t, rows, cols in tiles_of(work):
             work[rows, cols] = near[t] * far[t]
         invert(out, work)
 
 
-def second_inverse_kernel(meta, turn, part_0, part_1, part_2, part_3, near, far, out, work):
+def second_inverse_kernel(
+    meta, ring, other_ring, part_0, part_1, part_2, part_3, near, far, out, work
+):
     n = work.shape[0]
-
-    @pl.when(turn[0] == 0)
+    mine = takes_turn(meta, ring, other_ring)
+
+    @pl.when(jnp.logical_not(mine))
     def _():
         out[...] = jnp.zeros_like(out)
 
-    @pl.when(turn[0] != 0)
+    @pl.when(mine)
     def _():
         gram = (part_0[...] + part_1[...]) + (part_2[...] + part_3[...])
         row = lax.broadcasted_iota(jnp.int32, (n, n), 0)
@@ -146,26 +161,28 @@
         invert(out, work)
 
 
-def inverse_of(kernel, name, meta, turn, *arrays):
+def inverse_of(kernel, name, meta, *arrays):
     n = 256
     return pl.pallas_call(
         kernel,
         out_shape=jax.ShapeDtypeStruct((n, n), F32),
-        in_specs=[pl.BlockSpec(memory_space=pltpu.SMEM)] * 2
+        in_specs=[pl.BlockSpec(memory_space=pltpu.SMEM)]
         + [pl.BlockSpec(memory_space=pltpu.VMEM)] * len(arrays),
         out_specs=pl.BlockSpec(memory_space=pltpu.VMEM),
         scratch_shapes=[pltpu.VMEM((n, n), F32)],
         compiler_params=pltpu.CompilerParams(vmem_limit_bytes=VMEM_BYTES),
         cost_estimate=INVERSE_COST,
         name=name,
-    )(meta, turn, *arrays)
+    )(meta, *arrays)
 
 
 def prepare_kernel(meta, b_factor, c_factor, own, gram_keep, gram_send):
     rows = b_factor.shape[0]
     core = meta[2]
     own[0:rows, :] = b_factor[...].astype(BF16)
-    own[rows:, :] = c_factor[...].astype(BF16)
+    own[rows : rows + C_ROWS, :] = c_factor[...].astype(BF16)
+    count = meta[0].astype(F32)
+    own[rows + C_ROWS :, :] = jnp.full((COUNT_ROWS, own.shape[1]), count, F32).astype(BF16)
     for q, ref in enumerate((b_factor, c_factor)):
         gram = lax.dot_general(
             ref[...],
@@ -188,7 +205,7 @@
 
 def prepare(meta, b_factor, c_factor):
     rank = b_factor.shape[1]
-    rows = b_factor.shape[0] + c_factor.shape[0]
+    rows = b_factor.shape[0] + c_factor.shape[0] + COUNT_ROWS
     tiles = jax.ShapeDtypeStruct((rank * rank // 1024, 8, 128), F32)
     return pl.pallas_call(
         prepare_kernel,
@@ -200,38 +217,47 @@
     )(meta, b_factor, c_factor)
 
 
-def order_kernel(meta, i_idx, j_idx, order_one, order_two, ends):
+def order_kernel(meta, i_idx, j_idx, k_idx, order_one, order_two):
     slots = i_idx.shape[0]
-    grp, core = meta[1], meta[2]
-
-    def clear(s, carry):
-        order_one[s] = 0
-        order_two[s] = 0
+    count, grp, core = meta[0], meta[1], meta[2]
+
+    def place(s, front_one, front_two, i, j, k):
+        entry = s + 256 * (i + 64 * (j + 64 * k))
+        one = ((i >> 1) & 1) ^ core
+        two = jnp.where((j >> 4) == grp, 0, 1)
+        order_one[jnp.where(one == 1, front_one, slots - 1 - (s - front_one))] = entry
+        order_two[jnp.where(two == 1, front_two, slots - 1 - (s - front_two))] = entry
+        return front_one + one, front_two + two
+
+    def place_four(q, carry):
+        found = [(i_idx[4 * q + u], j_idx[4 * q + u], k_idx[4 * q + u]) for u in range(4)]
+        for u in range(4):
+            carry = place(4 * q + u, *carry, *found[u])
         return carry
 
-    lax.fori_loop(0, slots, clear, 0, unroll=8)
-
-    def place(s, carry):
-        front_one, front_two = carry
-        one = ((i_idx[s] >> 1) & 1) ^ core
-        two = jnp.where((j_idx[s] >> 4) == grp, 0, 1)
-        order_one[jnp.where(one == 1, front_one, slots - 1 - (s - front_one))] = s
-        order_two[jnp.where(two == 1, front_two, slots - 1 - (s - front_two))] = s
-        return front_one + one, front_two + two
-
-    ends[0], ends[1] = lax.fori_loop(0, meta[0], place, (jnp.int32(0), jnp.int32(0)))
-
-
-def order_slots(meta, i_index, j_index):
-    table = jax.ShapeDtypeStruct(i_index.shape, jnp.int32)
+    def place_one(s, carry):
+        return place(s, *carry, i_idx[s], j_idx[s], k_idx[s])
+
+    zero = (jnp.int32(0), jnp.int32(0))
+    fours = count // 4
+    ends = lax.fori_loop(4 * fours, count, place_one, lax.fori_loop(0, fours, place_four, zero))
+    for order, front in zip((order_one, order_two), ends):
+        order[slots] = front
+        order[slots + 1] = count - front
+        order[slots + 2] = grp
+        order[slots + 3] = core
+
+
+def order_slots(meta, i_index, j_index, k_index):
+    table = jax.ShapeDtypeStruct((i_index.shape[0] + 64,), jnp.int32)
     smem = pl.BlockSpec(memory_space=pltpu.SMEM)
     return pl.pallas_call(
         order_kernel,
-        out_shape=[table, table, jax.ShapeDtypeStruct((2,), jnp.int32)],
-        in_specs=[smem] * 3,
-        out_specs=[smem] * 3,
+        out_shape=[table] * 2,
+        in_specs=[smem] * 4,
+        out_specs=[smem] * 2,
         name="order_slots",
-    )(meta, i_index, j_index)
+    )(meta, i_index, j_index, k_index)
 
 
 def block_rows(ref, start):
@@ -249,76 +275,68 @@
         copy.wait()
 
 
-def for_each_group(first, count, order, blocks, buffer, sems, one_slot):
-    slots = order.shape[0]
+def for_each_group(first, order, blocks, buffer, sems, prepare_tables, one_slot):
+    slots = blocks.shape[0]
+    count = order[slots if first else slots + 1]
     groups = (count + GROUP - 1) // GROUP
 
-    def slot_at(place):
-        place = jnp.minimum(place, slots - 1)
+    def entry_at(place):
+        place = jnp.minimum(place, count - 1)
         return order[place if first else slots - 1 - place]
 
     def copies(group):
-        side = group & 1
+        side = group & (DEPTH - 1)
         return [
             pltpu.make_async_copy(
-                blocks.at[slot_at(group * GROUP + u)], buffer.at[side, u], sems.at[side, u]
+                blocks.at[entry_at(group * GROUP + u) & 255], buffer.at[side, u], sems.at[side, u]
             )
             for u in range(GROUP)
         ]
 
-    @pl.when(groups > 0)
-    def _():
-        copy_all(copies(0))
+    for ahead in range(DEPTH - 1):
+
+        @pl.when(ahead < groups)
+        def _():
+            copy_all(copies(ahead))
+
+    prepare_tables()
 
     def one_group(group, carry):
-        @pl.when(group + 1 < groups)
+        @pl.when(group + DEPTH - 1 < groups)
         def _():
-            copy_all(copies(group + 1))
+            copy_all(copies(group + DEPTH - 1))
 
         wait_all(copies(group))
         for u in range(GROUP):
             place = group * GROUP + u
-            one_slot(buffer[group & 1, u], u, slot_at(place), place < count)
+            entry = entry_at(place)
+            i, j, k = (entry >> 8) & 63, (entry >> 14) & 63, (entry >> 20) & 15
+            one_slot(buffer[group & (DEPTH - 1), u], u, i, j, k, place < count)
         return carry
 
     lax.fori_loop(0, groups, one_group, 0)
 
 
 def mode_one_kernel(
-    first,
-    meta,
-    ends,
-    order,
-    i_idx,
-    j_idx,
-    k_idx,
-    blocks,
-    own_0,
-    own_1,
-    own_2,
-    own_3,
-    out,
-    buffer,
-    table,
-    acc,
-    sems,
-    table_sems,
+    first, order, blocks, own_0, own_1, own_2, own_3, out, *rest
 ):
-    grp = meta[1]
+    ring = rest[0] if first else None
+    buffer, table, acc, sems, table_sems = rest[-5:]
+    grp = order[blocks.shape[0] + 2]
     own = own_0.shape[0]
     half = out.shape[0]
-    count = ends[0] if first else meta[0] - ends[0]
-    pieces = copy_all(
-        [
-            pltpu.make_async_copy(ref, table.at[pl.ds(q * own, own)], table_sems.at[q])
-            for q, ref in enumerate((own_0, own_1, own_2, own_3))
-        ]
-    )
-    acc[...] = jnp.zeros_like(acc)
-    wait_all(pieces)
-
-    def one_slot(block, u, s, live):
-        j, k, i = j_idx[s], k_idx[s], i_idx[s]
+
+    def prepare_tables():
+        pieces = copy_all(
+            [
+                pltpu.make_async_copy(ref, table.at[pl.ds(q * own, own)], table_sems.at[q])
+                for q, ref in enumerate((own_0, own_1, own_2, own_3))
+            ]
+        )
+        acc[...] = jnp.zeros_like(acc)
+        wait_all(pieces)
+
+    def one_slot(block, u, i, j, k, live):
         b_rows = block_rows(table, ((grp - (j >> 4)) & 3) * own + (j & 15) * EDGE)
         c_rows = block_rows(table, ((grp - (k >> 2)) & 3) * own + B_ROWS + (k & 3) * EDGE)
         product = (b_rows[:, None, :] * c_rows[None, :, :]).reshape(EDGE * EDGE, -1)
@@ -326,8 +344,14 @@
         target = jnp.where(live, (i >> 2) * (2 * EDGE) + (i & 1) * EDGE, half)
         acc[pl.ds(pl.multiple_of(target, EDGE), EDGE), :] += result
 
-    for_each_group(first, count, order, blocks, buffer, sems, one_slot)
+    for_each_group(first, order, blocks, buffer, sems, prepare_tables, one_slot)
     out[...] = acc[0:half, :]
+    if first:
+        counts = [
+            table[(q + 1) * own - COUNT_ROWS : (q + 1) * own, 0:128].astype(F32) for q in range(4)
+        ]
+        most = jnp.maximum(jnp.maximum(counts[0], counts[1]), jnp.maximum(counts[2], counts[3]))
+        ring[...] = most[0:8, :]
 
 
 def turn_block(block, turned, u):
@@ -354,38 +378,35 @@
     )
 
 
-def mode_two_slots(
-    first, meta, ends, order, i_idx, j_idx, k_idx, blocks, owns, a_table, scratch, part
-):
+def mode_two_slots(first, order, blocks, owns, a_table, scratch, part):
     buffer, turned, table, acc, sems, table_sems = scratch
-    grp, core = meta[1], meta[2]
-    c_rows = table.shape[0] // 4
+    grp, core = order[blocks.shape[0] + 2], order[blocks.shape[0] + 3]
     half = a_table.shape[0] // 2
-    count = ends[1] if first else meta[0] - ends[1]
-    pieces = copy_all(
-        [
-            pltpu.make_async_copy(
-                ref.at[pl.ds(B_ROWS, c_rows)],
-                table.at[pl.ds(q * c_rows, c_rows)],
-                table_sems.at[q],
-            )
-            for q, ref in enumerate(owns)
-        ]
-    )
-    acc[...] = jnp.zeros_like(acc)
-    wait_all(pieces)
-
-    def one_slot(block, u, s, live):
-        j, k, i = j_idx[s], k_idx[s], i_idx[s]
+
+    def prepare_tables():
+        pieces = copy_all(
+            [
+                pltpu.make_async_copy(
+                    ref.at[pl.ds(B_ROWS, C_ROWS)],
+                    table.at[pl.ds(q * C_ROWS, C_ROWS)],
+                    table_sems.at[q],
+                )
+                for q, ref in enumerate(owns)
+            ]
+        )
+        acc[...] = jnp.zeros_like(acc)
+        wait_all(pieces)
+
+    def one_slot(block, u, i, j, k, live):
         a_rows = block_rows(
             a_table,
             (((i >> 1) & 1) ^ core) * half + (i >> 2) * (2 * EDGE) + (i & 1) * EDGE,
         )
-        c_block = block_rows(table, ((grp - (k >> 2)) & 3) * c_rows + (k & 3) * EDGE)
+        c_rows = block_rows(table, ((grp - (k >> 2)) & 3) * C_ROWS + (k & 3) * EDGE)
         left = turn_block(block, turned, u)
         product = jnp.concatenate(
             [
-                a_rows[il * 8 + ih : il * 8 + ih + 1, :] * c_block
+                a_rows[il * 8 + ih : il * 8 + ih + 1, :] * c_rows
                 for ih in range(8)
                 for il in range(4)
             ],
@@ -398,16 +419,11 @@
         target = jnp.where(live, target, acc.shape[0] - EDGE)
         acc[pl.ds(pl.multiple_of(target, EDGE), EDGE), :] += result
 
-    for_each_group(first, count, order, blocks, buffer, sems, one_slot)
+    for_each_group(first, order, blocks, buffer, sems, prepare_tables, one_slot)
 
 
 def mode_two_others_kernel(
-    meta,
-    ends,
     order,
-    i_idx,
-    j_idx,
-    k_idx,
     blocks,
     own_0,
     own_1,
@@ -427,84 +443,62 @@
     col_norm = jnp.sqrt(squares[...] + 1e-06)
     a_table[0:half, :] = (a_near[...] / col_norm).astype(BF16)
     a_table[half : 2 * half, :] = (a_far[...] / col_norm).astype(BF16)
-    owns = (own_0, own_1, own_2, own_3)
-    mode_two_slots(
-        True, meta, ends, order, i_idx, j_idx, k_idx, blocks, owns, a_table, scratch, part
-    )
+    mode_two_slots(True, order, blocks, (own_0, own_1, own_2, own_3), a_table, scratch, part)
     acc = scratch[3]
     for q, ref in enumerate((send_1, send_2, send_3)):
         ref[...] = acc[q * part : (q + 1) * part, :].astype(BF16)
 
 
-def mode_two_own_kernel(
-    meta,
-    ends,
-    order,
-    i_idx,
-    j_idx,
-    k_idx,
-    blocks,
-    own_0,
-    own_1,
-    own_2,
-    own_3,
-    a_table,
-    keep,
-    *scratch,
-):
+def mode_two_own_kernel(order, blocks, own_0, own_1, own_2, own_3, a_table, keep, *scratch):
     part = keep.shape[0]
-    owns = (own_0, own_1, own_2, own_3)
-    mode_two_slots(
-        False, meta, ends, order, i_idx, j_idx, k_idx, blocks, owns, a_table, scratch, part
-    )
+    mode_two_slots(False, order, blocks, (own_0, own_1, own_2, own_3), a_table, scratch, part)
     keep[...] = scratch[3][0:part, :]
 
 
-def mode_call(kernel, name, scalars, in_place, resident, out_shape, scratch):
+def mode_call(kernel, name, order, in_place, resident, out_shape, scratch):
     smem, anywhere, vmem = (
         pl.BlockSpec(memory_space=pltpu.SMEM),
         pl.BlockSpec(memory_space=pl.ANY),
         pl.BlockSpec(memory_space=pltpu.VMEM),
     )
     blocks = in_place[0]
-    buffer = pltpu.VMEM((2, GROUP) + blocks.shape[1:], blocks.dtype)
+    buffer = pltpu.VMEM((DEPTH, GROUP) + blocks.shape[1:], blocks.dtype)
     return pl.pallas_call(
         kernel,
         out_shape=out_shape,
-        in_specs=[smem] * len(scalars) + [anywhere] * len(in_place) + [vmem] * len(resident),
+        in_specs=[smem] + [anywhere] * len(in_place) + [vmem] * len(resident),
         out_specs=[vmem] * len(out_shape),
         scratch_shapes=[buffer]
         + scratch
-        + [pltpu.SemaphoreType.DMA((2, GROUP)), pltpu.SemaphoreType.DMA((4,))],
+        + [pltpu.SemaphoreType.DMA((DEPTH, GROUP)), pltpu.SemaphoreType.DMA((4,))],
         compiler_params=pltpu.CompilerParams(vmem_limit_bytes=VMEM_BYTES),
-        cost_estimate=MODE_COST,
+        cost_estimate=LAST_PASS_COST if name == "mode_two_own_group" else MODE_COST,
         name=name,
-    )(*scalars, *in_place, *resident)
-
-
-def mode_one(first, meta, ends, order, indices, blocks, pieces):
+    )(order, *in_place, *resident)
+
+
+def mode_one(first, order, blocks, pieces):
     own, rank = pieces[0].shape
     half = 32 * EDGE
 
     def kernel(*refs):
         mode_one_kernel(first, *refs)
 
-    [out] = mode_call(
+    return mode_call(
         kernel,
         "mode_one_other_core" if first else "mode_one_own_core",
-        (meta, ends, order) + indices,
+        order,
         [blocks] + pieces,
         [],
-        [jax.ShapeDtypeStruct((half, rank), F32)],
+        [jax.ShapeDtypeStruct((half, rank), F32)]
+        + ([jax.ShapeDtypeStruct((8, 128), F32)] if first else []),
         [pltpu.VMEM((4 * own, rank), BF16), pltpu.VMEM((half + EDGE, rank), F32)],
     )
-    return out
-
-
-def mode_two(first, meta, ends, order, indices, blocks, pieces, resident):
+
+
+def mode_two(first, order, blocks, pieces, resident):
     rank = pieces[0].shape[1]
     part = 16 * EDGE
-    c_rows = pieces[0].shape[0] - B_ROWS
     sent = jax.ShapeDtypeStruct((part, rank), BF16)
     if first:
         out_shape = [sent] * 3 + [jax.ShapeDtypeStruct((64 * EDGE, rank), BF16)]
@@ -513,13 +507,13 @@
     return mode_call(
         mode_two_others_kernel if first else mode_two_own_kernel,
         "mode_two_other_groups" if first else "mode_two_own_group",
-        (meta, ends, order) + indices,
+        order,
         [blocks] + pieces,
         resident,
         out_shape,
         [
             pltpu.VMEM((GROUP, 8 * EDGE, 128), F32),
-            pltpu.VMEM((4 * c_rows, rank), BF16),
+            pltpu.VMEM((4 * C_ROWS, rank), BF16),
             pltpu.VMEM(((3 if first else 1) * part + EDGE, rank), F32),
         ],
     )
@@ -543,24 +537,25 @@
     grp, core = lax.axis_index("grp"), lax.axis_index("core")
     plane = lax.axis_size(PLANE)
     chips = lax.axis_size(CHIPS)
-    indices = (i_index, j_index, k_index)
+    ring_size = lax.axis_size(RING)
     meta = jnp.stack([block_count[0], grp, core])
 
     own, gram_keep, gram_send = prepare(meta, b_factor, c_factor)
-    order_one, order_two, ends = order_slots(meta, i_index, j_index)
+    order_one, order_two = order_slots(meta, i_index, j_index, k_index)
     gram_pair = gram_keep + to_other_core(gram_send)
     pieces = [own] + [along_groups(own, q) for q in (1, 2, 3)]
     gram_parts = exchange(gram_pair.reshape(chips, -1, 8, 128), CHIPS)
-    send = mode_one(True, meta, ends, order_one, indices, blocks, pieces)
+    send, ring = mode_one(True, order_one, blocks, pieces)
     piece = jnp.sum(gram_parts, axis=0)
     piece, send = lax.optimization_barrier((piece, send))
     spread = jnp.broadcast_to(piece[None], (chips,) + piece.shape)
-    spread, order_one = lax.optimization_barrier((spread, order_one))
+    spread, pieces = lax.optimization_barrier((spread, pieces))
     gram_near = exchange(spread, CHIPS)
-    keep = mode_one(False, meta, ends, order_one, indices, blocks, pieces)
+    [keep] = mode_one(False, order_one, blocks, pieces)
     gram_near, keep = lax.optimization_barrier((gram_near, keep))
     gram_near = gram_near.reshape(-1, 8, 128)
     gram_far = to_other_core(gram_near)
+    rings = (ring, to_other_core(ring))
 
     pair_sum = (keep + to_other_core(send)).astype(BF16)
     arrived = exchange(pair_sum.reshape(plane, -1, rank), PLANE)
@@ -568,38 +563,35 @@
     sum_near = exchange(jnp.broadcast_to(sum_own[None], (plane,) + sum_own.shape), PLANE)
     sum_near = sum_near.reshape(-1, rank)
 
-    other_count = to_other_core(block_count)
-    lighter = (block_count < other_count) | ((block_count == other_count) & (core == 0))
-    turn = lighter.astype(jnp.int32)
-    inverse = inverse_of(first_inverse_kernel, "first_inverse", meta, turn, gram_near, gram_far)
-    inverse = jnp.where(lighter[0], inverse, to_other_core(inverse))
-    a_update = jnp.dot(sum_own, inverse, precision=HIGHEST)
+    inverse = inverse_of(first_inverse_kernel, "first_inverse", meta, *rings, gram_near, gram_far)
+    mine, other = rings[0][0, 0], rings[1][0, 0]
+    lighter = (mine < other) | ((mine == other) & (core == 0))
+    inverse = jnp.where(lighter, inverse, to_other_core(inverse))
 
     sum_far = to_other_core(sum_near)
     a_near = jnp.dot(sum_near, inverse, precision=HIGHEST)
     squares = jnp.sum(a_near * a_near, axis=0, keepdims=True)
-    squares = squares + along_groups(squares, 1) + along_groups(squares, 2) + along_groups(squares, 3)
-    squares = squares + to_other_core(squares)
+    squares = exchange(jnp.broadcast_to(squares[None], (ring_size,) + squares.shape), RING)
+    squares = jnp.sum(squares, axis=0)
     a_far = jnp.dot(sum_far, inverse, precision=HIGHEST)
     gram_core = jnp.dot(a_near.T, a_near, precision=HIGHEST)
     gram_plane = gram_core + to_other_core(gram_core)
     gram_parts = [gram_plane] + [along_groups(gram_plane, q) for q in (1, 2, 3)]
 
-    *sends, a_table = mode_two(
-        True, meta, ends, order_two, indices, blocks, pieces, [a_near, a_far, squares]
+    *sends, a_table = mode_two(True, order_two, blocks, pieces, [a_near, a_far, squares])
+    gram_parts, sends = lax.optimization_barrier((gram_parts, sends))
+    second = inverse_of(
+        second_inverse_kernel, "second_inverse", meta, *rings, *gram_parts, gram_near, gram_far
     )
-    gram_parts, sends = lax.optimization_barrier((gram_parts, sends))
-    inverse = inverse_of(
-        second_inverse_kernel, "second_inverse", meta, turn, *gram_parts, gram_near, gram_far
-    )
-    inverse, sends, a_table = lax.optimization_barrier((inverse, sends, a_table))
-    [keep] = mode_two(False, meta, ends, order_two, indices, blocks, pieces, [a_table])
-    inverse = jnp.where(lighter[0], inverse, to_other_core(inverse))
+    second, a_table = lax.optimization_barrier((second, a_table))
+    [keep] = mode_two(False, order_two, blocks, pieces, [a_table])
+    a_update = jnp.dot(sum_own, inverse, precision=HIGHEST)
     arrived = [along_groups(value, q + 1) for q, value in enumerate(sends)]
-    arrived, keep = lax.optimization_barrier((arrived, keep))
+    arrived, keep, second = lax.optimization_barrier((arrived, keep, second))
+    second = jnp.where(lighter, second, to_other_core(second))
     arrived = [value.astype(F32) for value in arrived]
     own_two = keep + arrived[0] + arrived[1] + arrived[2]
-    b_update = jnp.dot(own_two, inverse, precision=HIGHEST)
+    b_update = jnp.dot(own_two, second, precision=HIGHEST)
     return a_update, b_update
 
 

time: 163 us -> 160 us (0.982)
  starting transfers between devices: 86.6 us -> 47.5 us
  Pallas kernels: 34.4 us -> 57.7 us
  blocking collectives: 0 us -> 11.5 us
  local copies, waits for them, and re-layouts: 8.66 us -> 5.46 us
  matrix products: 6.17 us -> 8.61 us
    pallas_call x2, Pallas kernels: 1.32 us -> 28.7 us  [inverse_of(): pl.pallas_call(kernel, out_shape=jax.ShapeDtypeStruct((n, n), F32), in_sp...]
    ppermute x12 -> x9, starting transfers between devices: 29.3 us -> 11 us  [along_groups(): lax.ppermute(value, 'grp', [(p, (p + shift) % size) for p in range(size)])]
    ppermute x9 -> x8, starting transfers between devices: 16.3 us -> 3.02 us  [to_other_core(): return lax.ppermute(value, 'core', [(0, 1), (1, 0)])]
    all_to_all x0 -> x1, blocking collectives: none -> 11.5 us  [exchange(): return lax.all_to_all(value, axes, 0, 0)]
    all_to_all x4, starting transfers between devices: 41 us -> 33.4 us  [exchange(): return lax.all_to_all(value, axes, 0, 0)]
    unnamed x38 -> x14, local copies, waits for them, and re-layouts: 6.84 us -> 2.64 us
    pallas_call x5, Pallas kernels: 31.1 us -> 27 us  [the longest x4 24.9 us: mode_call(): pl.pallas_call(kernel, out_shape=out_shape, in_specs=[smem] + [anywhere]...]
    all_to_all x4, waiting for transfers between devices: 10.8 us -> 13.7 us  [exchange(): return lax.all_to_all(value, axes, 0, 0)]
  transfers between devices with their start and end apart: 25 -> 21, of which waited for: 9 -> 5; matrix products, arithmetic and copies ran while one was open for 4% -> 7% of each run, Pallas kernels for 20% -> 35%
where the time goes in v2:
time: 160 us; the launch traced here: 158 us
  Pallas kernels  57.7 us (36%)
  starting transfers between devices  47.5 us (30%)
  waiting for transfers between devices  18.6 us (12%)
  blocking collectives  11.5 us (7%)
  matrix products  8.61 us (5%)
  local copies, waits for them, and re-layouts  5.46 us (3%)
  between operations  4.18 us (3%)
  other arithmetic  4.13 us (3%)
    all_to_all x4, starting transfers between devices, exchange(): return lax.all_to_all(value, axes, 0, 0)  33.4 us
    pallas_call x2, Pallas kernels, inverse_of(): pl.pallas_call(kernel, out_shape=jax.ShapeDtypeStruct((n, n), F32), in_sp...  28.7 us
    pallas_call x4, Pallas kernels, mode_call(): pl.pallas_call(kernel, out_shape=out_shape, in_specs=[smem] + [anywhere]...  24.9 us
    all_to_all x4, waiting for transfers between devices, exchange(): return lax.all_to_all(value, axes, 0, 0)  13.7 us
    all_to_all x1, blocking collectives, exchange(): return lax.all_to_all(value, axes, 0, 0)  11.5 us
    ppermute x9, starting transfers between devices, along_groups(): lax.ppermute(value, 'grp', [(p, (p + shift) % size) for p in range(size)])  11 us
    ppermute x9, waiting for transfers between devices, along_groups(): lax.ppermute(value, 'grp', [(p, (p + shift) % size) for p in range(size)])  4.26 us
  transfers between devices with their start and end apart: 21, of which 5 were waited for; matrix products, arithmetic and copies ran while one was open for 7% of the time, Pallas kernels for 35%

profile of v2, /device:TPU:1, one launch (start us, length us, event | category | flops | bytes accessed | tf_op | source)
XLA Modules:
  0.0 157.7 jit_solution(15165427458666036547)
XLA Ops:
  3.3 2.0 %prepare.1 = (bf16[656,256]{1,0:T(8,128)(2,1)S(1)}, f32[64,8,128]{2,1,0:T(8,128)S(1)}, f32[64,8,128]{2,1,0:T(8,128)S(1)}) custom-call(s32[3]{0:T(128)S(1)} %pad_add_fusion.meta, f32[512,256]{1,0:T(8,128)S(1)} %copy-done, f32[128,256]{1,0:T(8,128)S(1)} %copy-done.1), custom_call_target="tpu_custom_call" | custom-call | tf_op jit(solution)/shard_map/prepare/pallas_call | solution.py:210
  8.2 2.6 %collective-permute-start.2 = (bf16[656,256]{1,0:T(8,128)(2,1)S(1)}, bf16[656,256]{1,0:T(8,128)(2,1)S(1)}, u32[]{:S(2)}, u32[]{:S(2)}) collective-permute-start(bf16[656,256]{1,0:T(8,128)(2,1)S(1)} %get-tuple-element.43.refs_2_.own_0), channel_id=1, source_target_pairs={{0,64},{32,96},{64,0},{96,32},{1,65},{33,97},{65,1},{97,33},{2,66}... | collective-permute-start | bytes 1007624 | tf_op jit(solution)/shard_map/ppermute | solution.py:528
  11.9 2.1 %order_slots.1 = (s32[256]{0:T(256)}, s32[256]{0:T(256)}) custom-call(s32[3]{0:T(128)} %copy-done.2, s32[192]{0:T(256)} %i_idx.1, s32[192]{0:T(256)} %j_idx.1, s32[192]{0:T(256)} %k_idx.1), custom_call_target="tpu_custom_call" | custom-call | tf_op jit(solution)/shard_map/order_slots/pallas_call | solution.py:254
  14.7 8.7 %all-to-all-start = ((f32[64,1,8,128]{3,2,1,0:T(8,128)}), f32[64,1,8,128]{3,2,1,0:T(8,128)S(1)}, u32[]{:S(2)}, u32[]{:S(2)}) async-start(f32[64,1,8,128]{3,2,1,0:T(8,128)} %add_bitcast_fusion), calls=%async_computation | async-start | bytes 524288 | tf_op jit(solution)/shard_map/all_to_all | solution.py:532
  23.4 2.6 %collective-permute-done.2.refs_4_.own_2 = bf16[656,256]{1,0:T(8,128)(2,1)S(1)} collective-permute-done((bf16[656,256]{1,0:T(8,128)(2,1)S(1)}, bf16[656,256]{1,0:T(8,128)(2,1)S(1)}, u32[]{:S(2)}, u32[]{:S(2)}) %collective-permute-start.2) | collective-permute-done | bytes 335904 | tf_op jit(solution)/shard_map/ppermute | solution.py:528
  26.7 6.2 %mode_one_other_core.1 = (f32[1024,256]{1,0:T(8,128)}, f32[8,128]{1,0:T(8,128)S(1)}) custom-call(s32[256]{0:T(256)S(1)} %copy-done.5, bf16[192,32,1024]{2,1,0:T(8,128)(2,1)} %blocks.3, bf16[656,256]{1,0:T(8,128)(2,1)S(1)} %get-tuple-element.43.refs_2_.own_0, bf16[656,256]{1,0:T(8,128)(2,1)S(1)} %collective-permute-done.1.refs_3_.own_1, ...), custom_call_target="tpu_custom_call" | custom-call | flops 15000000512 | bytes 48000000 | tf_op jit(solution)/shard_map/mode_one_other_core/pallas_call | solution.py:466
  33.7 16.8 %all-to-all-start.1 = ((f32[64,1,8,128]{3,2,1,0:T(8,128)}), f32[64,1,8,128]{3,2,1,0:T(8,128)S(1)}, u32[]{:S(2)}, u32[]{:S(2)}) async-start(f32[64,1,8,128]{3,2,1,0:T(8,128)} %broadcast_in_dim.9), calls=%async_computation.1 | async-start | bytes 524288 | tf_op jit(solution)/shard_map/all_to_all | solution.py:532
  50.7 6.0 %mode_one_own_core.1 = f32[1024,256]{1,0:T(8,128)S(1)} custom-call(s32[256]{0:T(256)S(1)} %copy-done.6, bf16[192,32,1024]{2,1,0:T(8,128)(2,1)} %blocks.3, bf16[656,256]{1,0:T(8,128)(2,1)S(1)} %get-tuple-element.43.refs_2_.own_0, bf16[656,256]{1,0:T(8,128)(2,1)S(1)} %collective-permute-done.1.refs_3_.own_1, ...), custom_call_target="tpu_custom_call" | custom-call | flops 15000000512 | bytes 48000000 | tf_op jit(solution)/shard_map/mode_one_own_core/pallas_call | solution.py:466
  56.7 4.0 %all-to-all-done.1 = f32[64,1,8,128]{3,2,1,0:T(8,128)S(1)} async-done(((f32[64,1,8,128]{3,2,1,0:T(8,128)}), f32[64,1,8,128]{3,2,1,0:T(8,128)S(1)}, u32[]{:S(2)}, u32[]{:S(2)}) %all-to-all-start.1) | async-done | bytes 262176 | tf_op jit(solution)/shard_map/all_to_all | solution.py:532
  60.7 2.1 %add_convert_fusion = bf16[1024,256]{1,0:T(8,128)(2,1)} fusion(f32[1024,256]{1,0:T(8,128)S(1)} %mode_one_own_core.1, f32[1024,256]{1,0:T(8,128)} %collective-permute-done.4), kind=kLoop, calls=%fused_computation.2 | loop fusion | flops 524288 | bytes 2621440 | tf_op jit(solution)/shard_map/convert_element_type | solution.py:560
  62.9 3.6 %all-to-all-start.2 = ((bf16[16,64,256]{2,1,0:T(8,128)(2,1)}), bf16[16,64,256]{2,1,0:T(8,128)(2,1)S(1)}, u32[]{:S(2)}, u32[]{:S(2)}) async-start(bf16[16,64,256]{2,1,0:T(8,128)(2,1)} %bitcast.6), calls=%async_computation.2 | async-start | bytes 1048576 | tf_op jit(solution)/shard_map/all_to_all | solution.py:532
  67.0 9.7 %all-to-all-done.2 = bf16[16,64,256]{2,1,0:T(8,128)(2,1)S(1)} async-done(((bf16[16,64,256]{2,1,0:T(8,128)(2,1)}), bf16[16,64,256]{2,1,0:T(8,128)(2,1)S(1)}, u32[]{:S(2)}, u32[]{:S(2)}) %all-to-all-start.2) | async-done | bytes 524320 | tf_op jit(solution)/shard_map/all_to_all | solution.py:532
  77.9 4.3 %all-to-all-start.3 = ((f32[16,64,256]{2,1,0:T(8,128)}), f32[16,64,256]{2,1,0:T(8,128)}, u32[]{:S(2)}, u32[]{:S(2)}) async-start(f32[16,64,256]{2,1,0:T(8,128)} %broadcast_in_dim.10), calls=%async_computation.3 | async-start | bytes 2097152 | tf_op jit(solution)/shard_map/all_to_all | solution.py:532
  82.2 14.4 %first_inverse.1 = f32[256,256]{1,0:T(8,128)S(1)} custom-call(s32[3]{0:T(128)S(1)} %copy-done.3, f32[8,128]{1,0:T(8,128)S(1)} %get-tuple-element.49.ring, f32[8,128]{1,0:T(8,128)S(1)} %collective-permute-done.5.other_ring, f32[64,8,128]{2,1,0:T(8,128)S(1)} %bitcast.23, f32[64,8,128]{2,1,0:T(8,128)S(1)} %collective-permute-done.6.far), custom_call_target="tpu_custom_call" | custom-call | flops 16000000000 | bytes 50000000 | tf_op jit(solution)/shard_map/first_inverse/pallas_call | solution.py:166
  100.9 2.2 %multiply_reduce_fusion = (f32[256]{0:T(256)S(1)}, f32[1024,256]{1,0:T(8,128)S(1)}) fusion(f32[1024,256]{1,0:T(8,128)} %bitcast.10, f32[256,256]{1,0:T(8,128)S(1)} %broadcast_select_fusion), kind=kOutput, calls=%fused_computation | convolution fusion | flops 805830400 | bytes 2360320 | tf_op jit(solution)/shard_map/dot_general | solution.py:572
  103.2 1.8 %fusion.10 = f32[256,256]{1,0:T(8,128)S(1)} fusion(f32[1024,256]{1,0:T(8,128)S(1)} %get-tuple-element.71.a_near), kind=kOutput, calls=%fused_computation.16 | convolution fusion | flops 805306368 | bytes 1310720 | tf_op jit(solution)/shard_map/dot_general | solution.py:577
  105.1 11.5 %all_to_all.25 = f32[8,1,256]{2,1,0:T(1,128)S(1)} all-to-all(f32[8,1,256]{2,1,0:T(1,128)S(1)} %broadcast_in_dim.22), channel_id=1, replica_groups=mesh['grp'=4,'x'=4,'z'=4,'core'=2] {'grp','core'}, dimensions={0} | all-to-all | bytes 16384 | tf_op jit(solution)/shard_map/all_to_all | solution.py:532
  118.6 1.8 %collective-permute-start.11 = (f32[256,256]{1,0:T(8,128)S(1)}, f32[256,256]{1,0:T(8,128)S(1)}, u32[]{:S(2)}, u32[]{:S(2)}) collective-permute-start(f32[256,256]{1,0:T(8,128)S(1)} %add.20.part_0), channel_id=1, source_target_pairs={{0,96},{32,0},{64,32},{96,64},{1,97},{33,1},{65,33},{97,65},{2,98}... | collective-permute-start | bytes 786440 | tf_op jit(solution)/shard_map/ppermute | solution.py:528
  120.5 2.2 %fusion.11.a_far = f32[1024,256]{1,0:T(8,128)S(1)} fusion(f32[1024,256]{1,0:T(8,128)} %collective-permute-done.12, f32[256,256]{1,0:T(8,128)S(1)} %broadcast_select_fusion), kind=kOutput, calls=%fused_computation.17 | convolution fusion | flops 805306368 | bytes 2359296 | tf_op jit(solution)/shard_map/dot_general | solution.py:576
  122.7 8.7 %mode_two_other_groups.1 = (bf16[512,256]{1,0:T(8,128)(2,1)S(1)}, bf16[512,256]{1,0:T(8,128)(2,1)S(1)}, bf16[512,256]{1,0:T(8,128)(2,1)S(1)}, bf16[2048,256]{1,0:T(8,128)(2,1)S(1)}) custom-call(s32[256]{0:T(256)S(1)} %copy-done.4, bf16[192,32,1024]{2,1,0:T(8,128)(2,1)} %blocks.3, bf16[656,256]{1,0:T(8,128)(2,1)S(1)} %get-tuple-element.43.refs_2_.own_0, ...), custom_call_target="tpu_custom_call" | custom-call | flops 15000000512 | bytes 48000000 | tf_op jit(solution)/shard_map/mode_two_other_groups/pallas_call | solution.py:466
  131.5 1.7 %collective-permute-done.9.part_1 = f32[256,256]{1,0:T(8,128)S(1)} collective-permute-done((f32[256,256]{1,0:T(8,128)S(1)}, f32[256,256]{1,0:T(8,128)S(1)}, u32[]{:S(2)}, u32[]{:S(2)}) %collective-permute-start.9) | collective-permute-done | bytes 262176 | tf_op jit(solution)/shard_map/ppermute | solution.py:528
  133.1 2.1 %collective-permute-start.14 = (bf16[512,256]{1,0:T(8,128)(2,1)S(1)}, bf16[512,256]{1,0:T(8,128)(2,1)S(1)}, u32[]{:S(2)}, u32[]{:S(2)}) collective-permute-start(bf16[512,256]{1,0:T(8,128)(2,1)S(1)} %get-tuple-element.56), channel_id=1, source_target_pairs={{0,64},{32,96},{64,0},{96,32},{1,65},{33,97},{65,1},{97,33},{2,66}... | collective-permute-start | bytes 786440 | tf_op jit(solution)/shard_map/ppermute | solution.py:528
  136.3 14.4 %second_inverse.1 = f32[256,256]{1,0:T(8,128)S(1)} custom-call(s32[3]{0:T(128)S(1)} %copy-done.3, f32[8,128]{1,0:T(8,128)S(1)} %get-tuple-element.49.ring, f32[8,128]{1,0:T(8,128)S(1)} %collective-permute-done.5.other_ring, f32[256,256]{1,0:T(8,128)S(1)} %add.20.part_0, f32[256,256]{1,0:T(8,128)S(1)} %collective-permute-done.9.part_1, ...), custom_call_target="tpu_custom_call" | custom-call | flops 16000000000 | bytes 50000000 | tf_op jit(solution)/shard_map/second_inverse/pallas_call | solution.py:166
  150.7 3.9 %mode_two_own_group.1 = f32[512,256]{1,0:T(8,128)S(1)} custom-call(s32[256]{0:T(256)S(1)} %copy-done.4, bf16[192,32,1024]{2,1,0:T(8,128)(2,1)} %blocks.3, bf16[656,256]{1,0:T(8,128)(2,1)S(1)} %get-tuple-element.43.refs_2_.own_0, bf16[656,256]{1,0:T(8,128)(2,1)S(1)} %collective-permute-done.1.refs_3_.own_1, ...), custom_call_target="tpu_custom_call" | custom-call | flops 2000000000 | bytes 6000000 | tf_op jit(solution)/shard_map/mode_two_own_group/pallas_call | solution.py:466
  (59 shorter events, 18.0 us)
Async XLA Ops:
  5.3 8.7 %collective-permute-start = (f32[64,8,128]{2,1,0:T(8,128)S(1)}, f32[64,8,128]{2,1,0:T(8,128)S(1)}, u32[]{:S(2)}, u32[]{:S(2)}) collective-permute-start(f32[64,8,128]{2,1,0:T(8,128)S(1)} %get-tuple-element.37), channel_id=1, source_target_pairs={{0,1},{1,0},{2,3},{3,2},{4,5},{5,4},{6,7},{7,6},{8,9},{9,8},{10,11... | collective-permute-start | bytes 786440 | tf_op jit(solution)/shard_map/ppermute | solution.py:523
  6.8 16.6 %collective-permute-start.1 = (bf16[656,256]{1,0:T(8,128)(2,1)S(1)}, bf16[656,256]{1,0:T(8,128)(2,1)S(1)}, u32[]{:S(2)}, u32[]{:S(2)}) collective-permute-start(bf16[656,256]{1,0:T(8,128)(2,1)S(1)} %get-tuple-element.43.refs_2_.own_0), channel_id=1, source_target_pairs={{0,32},{32,64},{64,96},{96,0},{1,33},{33,65},{65,97},{97,1},{2,34}... | collective-permute-start | bytes 1007624 | tf_op jit(solution)/shard_map/ppermute | solution.py:528
  8.2 17.8 %collective-permute-start.2 = (bf16[656,256]{1,0:T(8,128)(2,1)S(1)}, bf16[656,256]{1,0:T(8,128)(2,1)S(1)}, u32[]{:S(2)}, u32[]{:S(2)}) collective-permute-start(bf16[656,256]{1,0:T(8,128)(2,1)S(1)} %get-tuple-element.43.refs_2_.own_0), channel_id=1, source_target_pairs={{0,64},{32,96},{64,0},{96,32},{1,65},{33,97},{65,1},{97,33},{2,66}... | collective-permute-start | bytes 1007624 | tf_op jit(solution)/shard_map/ppermute | solution.py:528
  10.8 15.2 %collective-permute-start.3 = (bf16[656,256]{1,0:T(8,128)(2,1)S(1)}, bf16[656,256]{1,0:T(8,128)(2,1)S(1)}, u32[]{:S(2)}, u32[]{:S(2)}) collective-permute-start(bf16[656,256]{1,0:T(8,128)(2,1)S(1)} %get-tuple-element.43.refs_2_.own_0), channel_id=1, source_target_pairs={{0,96},{32,0},{64,32},{96,64},{1,97},{33,1},{65,33},{97,65},{2,98}... | collective-permute-start | bytes 1007624 | tf_op jit(solution)/shard_map/ppermute | solution.py:528
  14.7 18.2 %all-to-all-start = ((f32[64,1,8,128]{3,2,1,0:T(8,128)}), f32[64,1,8,128]{3,2,1,0:T(8,128)S(1)}, u32[]{:S(2)}, u32[]{:S(2)}) async-start(f32[64,1,8,128]{3,2,1,0:T(8,128)} %add_bitcast_fusion), calls=%async_computation | async-start | bytes 524288 | tf_op jit(solution)/shard_map/all_to_all | solution.py:532
  26.7 24.0 %copy-start.6 = (s32[256]{0:T(256)S(1)}, s32[256]{0:T(256)}, u32[]{:S(2)}) copy-start(s32[256]{0:T(256)} %get-tuple-element.38.refs_0_) | copy-start | bytes 3076
  33.7 27.0 %all-to-all-start.1 = ((f32[64,1,8,128]{3,2,1,0:T(8,128)}), f32[64,1,8,128]{3,2,1,0:T(8,128)S(1)}, u32[]{:S(2)}, u32[]{:S(2)}) async-start(f32[64,1,8,128]{3,2,1,0:T(8,128)} %broadcast_in_dim.9), calls=%async_computation.1 | async-start | bytes 524288 | tf_op jit(solution)/shard_map/all_to_all | solution.py:532
  50.6 31.7 %copy-start.3 = (s32[3]{0:T(128)S(1)}, s32[3]{0:T(128)}, u32[]{:S(2)}) copy-start(s32[3]{0:T(128)} %copy-done.2) | copy-start | bytes 40
  50.6 10.2 %collective-permute-start.4 = (f32[1024,256]{1,0:T(8,128)}, f32[1024,256]{1,0:T(8,128)}, u32[]{:S(2)}, u32[]{:S(2)}) collective-permute-start(f32[1024,256]{1,0:T(8,128)} %get-tuple-element.48), channel_id=1, source_target_pairs={{0,1},{1,0},{2,3},{3,2},{4,5},{5,4},{6,7},{7,6},{8,9},{9,8},{10,11... | collective-permute-start | bytes 3145736 | tf_op jit(solution)/shard_map/ppermute | solution.py:523
  62.9 13.9 %all-to-all-start.2 = ((bf16[16,64,256]{2,1,0:T(8,128)(2,1)}), bf16[16,64,256]{2,1,0:T(8,128)(2,1)S(1)}, u32[]{:S(2)}, u32[]{:S(2)}) async-start(bf16[16,64,256]{2,1,0:T(8,128)(2,1)} %bitcast.6), calls=%async_computation.2 | async-start | bytes 1048576 | tf_op jit(solution)/shard_map/all_to_all | solution.py:532
  66.4 15.8 %collective-permute-start.6 = (f32[64,8,128]{2,1,0:T(8,128)S(1)}, f32[64,8,128]{2,1,0:T(8,128)S(1)}, u32[]{:S(2)}, u32[]{:S(2)}) collective-permute-start(f32[64,8,128]{2,1,0:T(8,128)S(1)} %bitcast.22), channel_id=1, source_target_pairs={{0,1},{1,0},{2,3},{3,2},{4,5},{5,4},{6,7},{7,6},{8,9},{9,8},{10,11... | collective-permute-start | bytes 786440 | tf_op jit(solution)/shard_map/ppermute | solution.py:523
  66.8 15.4 %collective-permute-start.5 = (f32[8,128]{1,0:T(8,128)S(1)}, f32[8,128]{1,0:T(8,128)S(1)}, u32[]{:S(2)}, u32[]{:S(2)}) collective-permute-start(f32[8,128]{1,0:T(8,128)S(1)} %get-tuple-element.49.ring), channel_id=1, source_target_pairs={{0,1},{1,0},{2,3},{3,2},{4,5},{5,4},{6,7},{7,6},{8,9},{9,8},{10,11... | collective-permute-start | bytes 12296 | tf_op jit(solution)/shard_map/ppermute | solution.py:523
  77.9 22.5 %all-to-all-start.3 = ((f32[16,64,256]{2,1,0:T(8,128)}), f32[16,64,256]{2,1,0:T(8,128)}, u32[]{:S(2)}, u32[]{:S(2)}) async-start(f32[16,64,256]{2,1,0:T(8,128)} %broadcast_in_dim.10), calls=%async_computation.3 | async-start | bytes 2097152 | tf_op jit(solution)/shard_map/all_to_all | solution.py:532
  82.2 40.5 %copy-start.4 = (s32[256]{0:T(256)S(1)}, s32[256]{0:T(256)}, u32[]{:S(2)}) copy-start(s32[256]{0:T(256)} %get-tuple-element.51.order) | copy-start | bytes 3076
  96.6 4.3 %collective-permute-start.7 = (f32[256,256]{1,0:T(8,128)S(1)}, f32[256,256]{1,0:T(8,128)S(1)}, u32[]{:S(2)}, u32[]{:S(2)}) collective-permute-start(f32[256,256]{1,0:T(8,128)S(1)} %first_inverse.1), channel_id=1, source_target_pairs={{0,1},{1,0},{2,3},{3,2},{4,5},{5,4},{6,7},{7,6},{8,9},{9,8},{10,11... | collective-permute-start | bytes 786440 | tf_op jit(solution)/shard_map/ppermute | solution.py:523
  100.3 20.1 %collective-permute-start.12 = (f32[1024,256]{1,0:T(8,128)}, f32[1024,256]{1,0:T(8,128)}, u32[]{:S(2)}, u32[]{:S(2)}) collective-permute-start(f32[1024,256]{1,0:T(8,128)} %bitcast.10), channel_id=1, source_target_pairs={{0,1},{1,0},{2,3},{3,2},{4,5},{5,4},{6,7},{7,6},{8,9},{9,8},{10,11... | collective-permute-start | bytes 3145736 | tf_op jit(solution)/shard_map/ppermute | solution.py:523
  105.0 11.7 %collective-permute-start.8 = (f32[256,256]{1,0:T(8,128)S(1)}, f32[256,256]{1,0:T(8,128)}, u32[]{:S(2)}, u32[]{:S(2)}) collective-permute-start(f32[256,256]{1,0:T(8,128)S(1)} %fusion.10), channel_id=1, source_target_pairs={{0,1},{1,0},{2,3},{3,2},{4,5},{5,4},{6,7},{7,6},{8,9},{9,8},{10,11... | collective-permute-start | bytes 786440 | tf_op jit(solution)/shard_map/ppermute | solution.py:523
  117.7 13.7 %collective-permute-start.10 = (f32[256,256]{1,0:T(8,128)S(1)}, f32[256,256]{1,0:T(8,128)S(1)}, u32[]{:S(2)}, u32[]{:S(2)}) collective-permute-start(f32[256,256]{1,0:T(8,128)S(1)} %add.20.part_0), channel_id=1, source_target_pairs={{0,64},{32,96},{64,0},{96,32},{1,65},{33,97},{65,1},{97,33},{2,66}... | collective-permute-start | bytes 786440 | tf_op jit(solution)/shard_map/ppermute | solution.py:528
  118.6 12.8 %collective-permute-start.11 = (f32[256,256]{1,0:T(8,128)S(1)}, f32[256,256]{1,0:T(8,128)S(1)}, u32[]{:S(2)}, u32[]{:S(2)}) collective-permute-start(f32[256,256]{1,0:T(8,128)S(1)} %add.20.part_0), channel_id=1, source_target_pairs={{0,96},{32,0},{64,32},{96,64},{1,97},{33,1},{65,33},{97,65},{2,98}... | collective-permute-start | bytes 786440 | tf_op jit(solution)/shard_map/ppermute | solution.py:528
  120.5 12.7 %collective-permute-start.9 = (f32[256,256]{1,0:T(8,128)S(1)}, f32[256,256]{1,0:T(8,128)S(1)}, u32[]{:S(2)}, u32[]{:S(2)}) collective-permute-start(f32[256,256]{1,0:T(8,128)S(1)} %add.20.part_0), channel_id=1, source_target_pairs={{0,32},{32,64},{64,96},{96,0},{1,33},{33,65},{65,97},{97,1},{2,34}... | collective-permute-start | bytes 786440 | tf_op jit(solution)/shard_map/ppermute | solution.py:528
  133.1 21.5 %collective-permute-start.13 = (bf16[512,256]{1,0:T(8,128)(2,1)S(1)}, bf16[512,256]{1,0:T(8,128)(2,1)S(1)}, u32[]{:S(2)}, u32[]{:S(2)}) collective-permute-start(bf16[512,256]{1,0:T(8,128)(2,1)S(1)} %get-tuple-element.55), channel_id=1, source_target_pairs={{0,32},{32,64},{64,96},{96,0},{1,33},{33,65},{65,97},{97,1},{2,34}... | collective-permute-start | bytes 786440 | tf_op jit(solution)/shard_map/ppermute | solution.py:528
  133.1 21.5 %collective-permute-start.14 = (bf16[512,256]{1,0:T(8,128)(2,1)S(1)}, bf16[512,256]{1,0:T(8,128)(2,1)S(1)}, u32[]{:S(2)}, u32[]{:S(2)}) collective-permute-start(bf16[512,256]{1,0:T(8,128)(2,1)S(1)} %get-tuple-element.56), channel_id=1, source_target_pairs={{0,64},{32,96},{64,0},{96,32},{1,65},{33,97},{65,1},{97,33},{2,66}... | collective-permute-start | bytes 786440 | tf_op jit(solution)/shard_map/ppermute | solution.py:528
  135.2 19.4 %collective-permute-start.15 = (bf16[512,256]{1,0:T(8,128)(2,1)S(1)}, bf16[512,256]{1,0:T(8,128)(2,1)S(1)}, u32[]{:S(2)}, u32[]{:S(2)}) collective-permute-start(bf16[512,256]{1,0:T(8,128)(2,1)S(1)} %get-tuple-element.57), channel_id=1, source_target_pairs={{0,96},{32,0},{64,32},{96,64},{1,97},{33,1},{65,33},{97,65},{2,98}... | collective-permute-start | bytes 786440 | tf_op jit(solution)/shard_map/ppermute | solution.py:528
  154.6 1.6 %collective-permute-start.16 = (f32[256,256]{1,0:T(8,128)S(1)}, f32[256,256]{1,0:T(8,128)S(1)}, u32[]{:S(2)}, u32[]{:S(2)}) collective-permute-start(f32[256,256]{1,0:T(8,128)S(1)} %second_inverse.1), channel_id=1, source_target_pairs={{0,1},{1,0},{2,3},{3,2},{4,5},{5,4},{6,7},{7,6},{8,9},{9,8},{10,11... | collective-permute-start | bytes 786440 | tf_op jit(solution)/shard_map/ppermute | solution.py:523
  (4 other events, 11.2 us)

commit v3 on v2

--- a/solution.py
+++ b/solution.py
@@ -15,11 +15,11 @@
 MODE_COST = pl.CostEstimate(flops=15_000_000_000, bytes_accessed=48_000_000, transcendentals=0)
 LAST_PASS_COST = pl.CostEstimate(flops=2_000_000_000, bytes_accessed=6_000_000, transcendentals=0)
 INVERSE_COST = pl.CostEstimate(flops=16_000_000_000, bytes_accessed=50_000_000, transcendentals=0)
-VMEM_BYTES = 48 << 20
+VMEM_BYTES = 8 << 20
+MODE_VMEM_BYTES = 48 << 20
 ALL = ("grp", "x", "z", "core")
 PLANE = ("x", "z")
 CHIPS = ("grp", "x", "z")
-RING = ("grp", "core")
 F32 = jnp.float32
 BF16 = jnp.bfloat16
 HIGHEST = lax.Precision.HIGHEST
@@ -176,9 +176,17 @@
     )(meta, *arrays)
 
 
-def prepare_kernel(meta, b_factor, c_factor, own, gram_keep, gram_send):
+def prepare_kernel(meta, b_hbm, c_hbm, own, gram_keep, gram_send, b_factor, c_factor, sems):
     rows = b_factor.shape[0]
     core = meta[2]
+    wait_all(
+        copy_all(
+            [
+                pltpu.make_async_copy(b_hbm, b_factor, sems.at[0]),
+                pltpu.make_async_copy(c_hbm, c_factor, sems.at[1]),
+            ]
+        )
+    )
     own[0:rows, :] = b_factor[...].astype(BF16)
     own[rows : rows + C_ROWS, :] = c_factor[...].astype(BF16)
     count = meta[0].astype(F32)
@@ -211,7 +219,12 @@
         prepare_kernel,
         out_shape=[jax.ShapeDtypeStruct((rows, rank), BF16), tiles, tiles],
         in_specs=[pl.BlockSpec(memory_space=pltpu.SMEM)]
-        + [pl.BlockSpec(memory_space=pltpu.VMEM)] * 2,
+        + [pl.BlockSpec(memory_space=pl.ANY)] * 2,
+        scratch_shapes=[
+            pltpu.VMEM(b_factor.shape, F32),
+            pltpu.VMEM(c_factor.shape, F32),
+            pltpu.SemaphoreType.DMA((2,)),
+        ],
         compiler_params=pltpu.CompilerParams(vmem_limit_bytes=VMEM_BYTES),
         name="prepare",
     )(meta, b_factor, c_factor)
@@ -440,9 +453,9 @@
 ):
     half = a_near.shape[0]
     part = send_1.shape[0]
-    col_norm = jnp.sqrt(squares[...] + 1e-06)
-    a_table[0:half, :] = (a_near[...] / col_norm).astype(BF16)
-    a_table[half : 2 * half, :] = (a_far[...] / col_norm).astype(BF16)
+    inv_norm = 1.0 / jnp.sqrt(squares[...] + 1e-06)
+    a_table[0:half, :] = (a_near[...] * inv_norm).astype(BF16)
+    a_table[half : 2 * half, :] = (a_far[...] * inv_norm).astype(BF16)
     mode_two_slots(True, order, blocks, (own_0, own_1, own_2, own_3), a_table, scratch, part)
     acc = scratch[3]
     for q, ref in enumerate((send_1, send_2, send_3)):
@@ -471,7 +484,7 @@
         scratch_shapes=[buffer]
         + scratch
         + [pltpu.SemaphoreType.DMA((DEPTH, GROUP)), pltpu.SemaphoreType.DMA((4,))],
-        compiler_params=pltpu.CompilerParams(vmem_limit_bytes=VMEM_BYTES),
+        compiler_params=pltpu.CompilerParams(vmem_limit_bytes=MODE_VMEM_BYTES),
         cost_estimate=LAST_PASS_COST if name == "mode_two_own_group" else MODE_COST,
         name=name,
     )(order, *in_place, *resident)
@@ -537,12 +550,12 @@
     grp, core = lax.axis_index("grp"), lax.axis_index("core")
     plane = lax.axis_size(PLANE)
     chips = lax.axis_size(CHIPS)
-    ring_size = lax.axis_size(RING)
     meta = jnp.stack([block_count[0], grp, core])
 
     own, gram_keep, gram_send = prepare(meta, b_factor, c_factor)
-    order_one, order_two = order_slots(meta, i_index, j_index, k_index)
     gram_pair = gram_keep + to_other_core(gram_send)
+    gram_pair, late_meta = lax.optimization_barrier((gram_pair, meta))
+    order_one, order_two = order_slots(late_meta, i_index, j_index, k_index)
     pieces = [own] + [along_groups(own, q) for q in (1, 2, 3)]
     gram_parts = exchange(gram_pair.reshape(chips, -1, 8, 128), CHIPS)
     send, ring = mode_one(True, order_one, blocks, pieces)
@@ -564,15 +577,13 @@
     sum_near = sum_near.reshape(-1, rank)
 
     inverse = inverse_of(first_inverse_kernel, "first_inverse", meta, *rings, gram_near, gram_far)
-    mine, other = rings[0][0, 0], rings[1][0, 0]
-    lighter = (mine < other) | ((mine == other) & (core == 0))
-    inverse = jnp.where(lighter, inverse, to_other_core(inverse))
+    inverse = lax.optimization_barrier(inverse + to_other_core(inverse))
 
     sum_far = to_other_core(sum_near)
     a_near = jnp.dot(sum_near, inverse, precision=HIGHEST)
     squares = jnp.sum(a_near * a_near, axis=0, keepdims=True)
-    squares = exchange(jnp.broadcast_to(squares[None], (ring_size,) + squares.shape), RING)
-    squares = jnp.sum(squares, axis=0)
+    squares = squares + along_groups(squares, 1) + along_groups(squares, 2) + along_groups(squares, 3)
+    squares = squares + to_other_core(squares)
     a_far = jnp.dot(sum_far, inverse, precision=HIGHEST)
     gram_core = jnp.dot(a_near.T, a_near, precision=HIGHEST)
     gram_plane = gram_core + to_other_core(gram_core)
@@ -588,7 +599,7 @@
     a_update = jnp.dot(sum_own, inverse, precision=HIGHEST)
     arrived = [along_groups(value, q + 1) for q, value in enumerate(sends)]
     arrived, keep, second = lax.optimization_barrier((arrived, keep, second))
-    second = jnp.where(lighter, second, to_other_core(second))
+    second = lax.optimization_barrier(second + to_other_core(second))
     arrived = [value.astype(F32) for value in arrived]
     own_two = keep + arrived[0] + arrived[1] + arrived[2]
     b_update = jnp.dot(own_two, second, precision=HIGHEST)

time: 160 us -> 157 us (0.981); the launches traced: 158 us -> 157 us
  starting transfers between devices: 47.5 us -> 84.4 us
  Pallas kernels: 57.7 us -> 36.7 us
  blocking collectives: 11.5 us -> 0 us
  between operations: 4.18 us -> 1.57 us
    ppermute x8 -> x9, starting transfers between devices: 3.02 us -> 36.2 us  [to_other_core(): return lax.ppermute(value, 'core', [(0, 1), (1, 0)])]
    pallas_call x2, Pallas kernels: 28.7 us -> 1.8 us  [inverse_of(): pl.pallas_call(kernel, out_shape=jax.ShapeDtypeStruct((n, n), F32), in_sp...]
    all_to_all x1 -> x0, blocking collectives: 11.5 us -> none  [exchange(): return lax.all_to_all(value, axes, 0, 0)]
    ppermute x9 -> x12, starting transfers between devices: 11 us -> 18.4 us  [along_groups(): lax.ppermute(value, 'grp', [(p, (p + shift) % size) for p in range(size)])]
    all_to_all x4, waiting for transfers between devices: 13.7 us -> 7.12 us  [exchange(): return lax.all_to_all(value, axes, 0, 0)]
    pallas_call x4, Pallas kernels: 24.9 us -> 30.4 us  [mode_call(): pl.pallas_call(kernel, out_shape=out_shape, in_specs=[smem] + [anywhere]...]
    ppermute x9 -> x12, waiting for transfers between devices: 4.26 us -> 8.81 us  [along_groups(): lax.ppermute(value, 'grp', [(p, (p + shift) % size) for p in range(size)])]
    all_to_all x4, starting transfers between devices: 33.4 us -> 29.8 us  [exchange(): return lax.all_to_all(value, axes, 0, 0)]
  transfers between devices with their start and end apart: 21 -> 25, of which waited for: 5 -> 10; matrix products, arithmetic and copies ran while one was open for 7% -> 5% of each run, Pallas kernels for 35% -> 22%
where the time goes in v3:
time: 157 us
  starting transfers between devices  84.4 us (54%)
  Pallas kernels  36.7 us (23%)
  waiting for transfers between devices  18.9 us (12%)
  matrix products  7.47 us (5%)
  local copies, waits for them, and re-layouts  4.44 us (3%)
  other arithmetic  3.23 us (2%)
  between operations  1.57 us (1%)
    ppermute x9, starting transfers between devices, to_other_core(): return lax.ppermute(value, 'core', [(0, 1), (1, 0)])  36.2 us
    pallas_call x4, Pallas kernels, mode_call(): pl.pallas_call(kernel, out_shape=out_shape, in_specs=[smem] + [anywhere]...  30.4 us
    all_to_all x4, starting transfers between devices, exchange(): return lax.all_to_all(value, axes, 0, 0)  29.8 us
    ppermute x12, starting transfers between devices, along_groups(): lax.ppermute(value, 'grp', [(p, (p + shift) % size) for p in range(size)])  18.4 us
    ppermute x12, waiting for transfers between devices, along_groups(): lax.ppermute(value, 'grp', [(p, (p + shift) % size) for p in range(size)])  8.81 us
    all_to_all x4, waiting for transfers between devices, exchange(): return lax.all_to_all(value, axes, 0, 0)  7.12 us
  transfers between devices with their start and end apart: 25, of which 10 were waited for; matrix products, arithmetic and copies ran while one was open for 5% of the time, Pallas kernels for 22%

profile of v3, /device:TPU:1, one launch (start us, length us, event | category | flops | bytes accessed | tf_op | source)
XLA Modules:
  0.0 156.7 jit_solution(10235280732324885383)
XLA Ops:
  3.3 2.2 %prepare.1 = (bf16[656,256]{1,0:T(8,128)(2,1)S(1)}, f32[64,8,128]{2,1,0:T(8,128)S(1)}, f32[64,8,128]{2,1,0:T(8,128)S(1)}) custom-call(s32[3]{0:T(128)S(1)} %pad_add_fusion.meta, f32[512,256]{1,0:T(8,128)S(1)} %copy-done, f32[128,256]{1,0:T(8,128)S(1)} %copy-done.1), custom_call_target="tpu_custom_call" | custom-call | tf_op jit(solution)/shard_map/prepare/pallas_call | solution.py:218
  5.5 2.2 %collective-permute-start.1 = (bf16[656,256]{1,0:T(8,128)(2,1)S(1)}, bf16[656,256]{1,0:T(8,128)(2,1)S(1)}, u32[]{:S(2)}, u32[]{:S(2)}) collective-permute-start(bf16[656,256]{1,0:T(8,128)(2,1)S(1)} %get-tuple-element.47.refs_2_.own_0), channel_id=1, source_target_pairs={{0,32},{32,64},{64,96},{96,0},{1,33},{33,65},{65,97},{97,1},{2,34}... | collective-permute-start | bytes 1007624 | tf_op jit(solution)/shard_map/ppermute | solution.py:541
  7.7 2.6 %collective-permute-start.2 = (bf16[656,256]{1,0:T(8,128)(2,1)S(1)}, bf16[656,256]{1,0:T(8,128)(2,1)S(1)}, u32[]{:S(2)}, u32[]{:S(2)}) collective-permute-start(bf16[656,256]{1,0:T(8,128)(2,1)S(1)} %get-tuple-element.47.refs_2_.own_0), channel_id=1, source_target_pairs={{0,64},{32,96},{64,0},{96,32},{1,65},{33,97},{65,1},{97,33},{2,66}... | collective-permute-start | bytes 1007624 | tf_op jit(solution)/shard_map/ppermute | solution.py:541
  14.8 8.6 %all-to-all-start = ((f32[64,1,8,128]{3,2,1,0:T(8,128)}), f32[64,1,8,128]{3,2,1,0:T(8,128)S(1)}, u32[]{:S(2)}, u32[]{:S(2)}) async-start(f32[64,1,8,128]{3,2,1,0:T(8,128)} %bitcast.3), calls=%async_computation | async-start | bytes 524288 | tf_op jit(solution)/shard_map/all_to_all | solution.py:545
  23.5 2.3 %order_slots.1 = (s32[256]{0:T(256)}, s32[256]{0:T(256)}) custom-call(s32[3]{0:T(128)} %copy-done.2, s32[192]{0:T(256)} %i_idx.1, s32[192]{0:T(256)} %j_idx.1, s32[192]{0:T(256)} %k_idx.1), custom_call_target="tpu_custom_call" | custom-call | tf_op jit(solution)/shard_map/order_slots/pallas_call | solution.py:267
  26.5 7.8 %mode_one_other_core.1 = (f32[1024,256]{1,0:T(8,128)}, f32[8,128]{1,0:T(8,128)S(1)}) custom-call(s32[256]{0:T(256)S(1)} %copy-done.5, bf16[192,32,1024]{2,1,0:T(8,128)(2,1)} %blocks.3, bf16[656,256]{1,0:T(8,128)(2,1)S(1)} %get-tuple-element.47.refs_2_.own_0, bf16[656,256]{1,0:T(8,128)(2,1)S(1)} %collective-permute-done.1.refs_3_.own_1, ...), custom_call_target="tpu_custom_call" | custom-call | flops 15000000512 | bytes 48000000 | tf_op jit(solution)/shard_map/mode_one_other_core/pallas_call | solution.py:479
  35.1 11.3 %all-to-all-start.1 = ((f32[64,1,8,128]{3,2,1,0:T(8,128)}), f32[64,1,8,128]{3,2,1,0:T(8,128)S(1)}, u32[]{:S(2)}, u32[]{:S(2)}) async-start(f32[64,1,8,128]{3,2,1,0:T(8,128)} %broadcast_in_dim.18), calls=%async_computation.1 | async-start | bytes 524288 | tf_op jit(solution)/shard_map/all_to_all | solution.py:545
  46.5 5.5 %collective-permute-start.4 = (f32[1024,256]{1,0:T(8,128)}, f32[1024,256]{1,0:T(8,128)}, u32[]{:S(2)}, u32[]{:S(2)}) collective-permute-start(f32[1024,256]{1,0:T(8,128)} %get-tuple-element.52), channel_id=1, source_target_pairs={{0,1},{1,0},{2,3},{3,2},{4,5},{5,4},{6,7},{7,6},{8,9},{9,8},{10,11... | collective-permute-start | bytes 3145736 | tf_op jit(solution)/shard_map/ppermute | solution.py:536
  52.0 6.9 %mode_one_own_core.1 = f32[1024,256]{1,0:T(8,128)S(1)} custom-call(s32[256]{0:T(256)S(1)} %copy-done.6, bf16[192,32,1024]{2,1,0:T(8,128)(2,1)} %blocks.3, bf16[656,256]{1,0:T(8,128)(2,1)S(1)} %get-tuple-element.47.refs_2_.own_0, bf16[656,256]{1,0:T(8,128)(2,1)S(1)} %collective-permute-done.1.refs_3_.own_1, ...), custom_call_target="tpu_custom_call" | custom-call | flops 15000000512 | bytes 48000000 | tf_op jit(solution)/shard_map/mode_one_own_core/pallas_call | solution.py:479
  58.9 2.2 %add_convert_fusion = bf16[1024,256]{1,0:T(8,128)(2,1)} fusion(f32[1024,256]{1,0:T(8,128)S(1)} %mode_one_own_core.1, f32[1024,256]{1,0:T(8,128)} %collective-permute-done.4), kind=kLoop, calls=%fused_computation.2 | loop fusion | flops 524288 | bytes 2621440 | tf_op jit(solution)/shard_map/convert_element_type | solution.py:573
  61.1 5.5 %all-to-all-start.2 = ((bf16[16,64,256]{2,1,0:T(8,128)(2,1)}), bf16[16,64,256]{2,1,0:T(8,128)(2,1)S(1)}, u32[]{:S(2)}, u32[]{:S(2)}) async-start(bf16[16,64,256]{2,1,0:T(8,128)(2,1)} %bitcast.6), calls=%async_computation.2 | async-start | bytes 1048576 | tf_op jit(solution)/shard_map/all_to_all | solution.py:545
  66.5 2.0 %collective-permute-start.6 = (f32[64,8,128]{2,1,0:T(8,128)S(1)}, f32[64,8,128]{2,1,0:T(8,128)S(1)}, u32[]{:S(2)}, u32[]{:S(2)}) collective-permute-start(f32[64,8,128]{2,1,0:T(8,128)S(1)} %bitcast.20), channel_id=1, source_target_pairs={{0,1},{1,0},{2,3},{3,2},{4,5},{5,4},{6,7},{7,6},{8,9},{9,8},{10,11... | collective-permute-start | bytes 786440 | tf_op jit(solution)/shard_map/ppermute | solution.py:536
  68.7 7.1 %all-to-all-done.2 = bf16[16,64,256]{2,1,0:T(8,128)(2,1)S(1)} async-done(((bf16[16,64,256]{2,1,0:T(8,128)(2,1)}), bf16[16,64,256]{2,1,0:T(8,128)(2,1)S(1)}, u32[]{:S(2)}, u32[]{:S(2)}) %all-to-all-start.2) | async-done | bytes 524320 | tf_op jit(solution)/shard_map/all_to_all | solution.py:545
  76.9 4.4 %all-to-all-start.3 = ((f32[16,64,256]{2,1,0:T(8,128)}), f32[16,64,256]{2,1,0:T(8,128)}, u32[]{:S(2)}, u32[]{:S(2)}) async-start(f32[16,64,256]{2,1,0:T(8,128)} %broadcast_in_dim.19), calls=%async_computation.3 | async-start | bytes 2097152 | tf_op jit(solution)/shard_map/all_to_all | solution.py:545
  82.2 16.8 %collective-permute-start.7 = (f32[256,256]{1,0:T(8,128)S(1)}, f32[256,256]{1,0:T(8,128)S(1)}, u32[]{:S(2)}, u32[]{:S(2)}) collective-permute-start(f32[256,256]{1,0:T(8,128)S(1)} %first_inverse.1), channel_id=1, source_target_pairs={{0,1},{1,0},{2,3},{3,2},{4,5},{5,4},{6,7},{7,6},{8,9},{9,8},{10,11... | collective-permute-start | bytes 786440 | tf_op jit(solution)/shard_map/ppermute | solution.py:536
  100.2 2.2 %multiply_reduce_fusion = (f32[256]{0:T(256)S(1)}, f32[1024,256]{1,0:T(8,128)S(1)}) fusion(f32[1024,256]{1,0:T(8,128)} %bitcast.8, f32[256,256]{1,0:T(8,128)S(1)} %add.38), kind=kOutput, calls=%fused_computation | convolution fusion | flops 805830400 | bytes 2360320 | tf_op jit(solution)/shard_map/dot_general | solution.py:583
  102.4 1.9 %fusion.8 = f32[256,256]{1,0:T(8,128)S(1)} fusion(f32[1024,256]{1,0:T(8,128)S(1)} %get-tuple-element.75.a_near), kind=kOutput, calls=%fused_computation.13 | convolution fusion | flops 805306368 | bytes 1310720 | tf_op jit(solution)/shard_map/dot_general | solution.py:588
  104.8 3.7 %collective-permute-start.13 = (f32[1,256]{1,0:T(1,128)S(1)}, f32[1,256]{1,0:T(1,128)S(1)}, u32[]{:S(2)}, u32[]{:S(2)}) collective-permute-start(f32[1,256]{1,0:T(1,128)S(1)} %bitcast.23), channel_id=1, source_target_pairs={{0,32},{32,64},{64,96},{96,0},{1,33},{33,65},{65,97},{97,1},{2,34}... | collective-permute-start | bytes 3080 | tf_op jit(solution)/shard_map/ppermute | solution.py:541
  108.5 2.6 %collective-permute-start.14 = (f32[1,256]{1,0:T(1,128)S(1)}, f32[1,256]{1,0:T(1,128)S(1)}, u32[]{:S(2)}, u32[]{:S(2)}) collective-permute-start(f32[1,256]{1,0:T(1,128)S(1)} %bitcast.24), channel_id=1, source_target_pairs={{0,64},{32,96},{64,0},{96,32},{1,65},{33,97},{65,1},{97,33},{2,66}... | collective-permute-start | bytes 3080 | tf_op jit(solution)/shard_map/ppermute | solution.py:541
  120.1 9.8 %mode_two_other_groups.1 = (bf16[512,256]{1,0:T(8,128)(2,1)S(1)}, bf16[512,256]{1,0:T(8,128)(2,1)S(1)}, bf16[512,256]{1,0:T(8,128)(2,1)S(1)}, bf16[2048,256]{1,0:T(8,128)(2,1)S(1)}) custom-call(s32[256]{0:T(256)S(1)} %copy-done.4, bf16[192,32,1024]{2,1,0:T(8,128)(2,1)} %blocks.3, bf16[656,256]{1,0:T(8,128)(2,1)S(1)} %get-tuple-element.47.refs_2_.own_0, ...), custom_call_target="tpu_custom_call" | custom-call | flops 15000000512 | bytes 48000000 | tf_op jit(solution)/shard_map/mode_two_other_groups/pallas_call | solution.py:479
  131.7 2.3 %collective-permute-start.18 = (bf16[512,256]{1,0:T(8,128)(2,1)S(1)}, bf16[512,256]{1,0:T(8,128)(2,1)S(1)}, u32[]{:S(2)}, u32[]{:S(2)}) collective-permute-start(bf16[512,256]{1,0:T(8,128)(2,1)S(1)} %get-tuple-element.60), channel_id=1, source_target_pairs={{0,64},{32,96},{64,0},{96,32},{1,65},{33,97},{65,1},{97,33},{2,66}... | collective-permute-start | bytes 786440 | tf_op jit(solution)/shard_map/ppermute | solution.py:541
  136.0 5.9 %mode_two_own_group.1 = f32[512,256]{1,0:T(8,128)S(1)} custom-call(s32[256]{0:T(256)S(1)} %copy-done.4, bf16[192,32,1024]{2,1,0:T(8,128)(2,1)} %blocks.3, bf16[656,256]{1,0:T(8,128)(2,1)S(1)} %get-tuple-element.47.refs_2_.own_0, bf16[656,256]{1,0:T(8,128)(2,1)S(1)} %collective-permute-done.1.refs_3_.own_1, ...), custom_call_target="tpu_custom_call" | custom-call | flops 2000000000 | bytes 6000000 | tf_op jit(solution)/shard_map/mode_two_own_group/pallas_call | solution.py:479
  141.9 3.8 %collective-permute-done.18 = bf16[512,256]{1,0:T(8,128)(2,1)S(1)} collective-permute-done((bf16[512,256]{1,0:T(8,128)(2,1)S(1)}, bf16[512,256]{1,0:T(8,128)(2,1)S(1)}, u32[]{:S(2)}, u32[]{:S(2)}) %collective-permute-start.18) | collective-permute-done | bytes 262176 | tf_op jit(solution)/shard_map/ppermute | solution.py:541
  146.3 7.8 %collective-permute-start.20 = (f32[256,256]{1,0:T(8,128)S(1)}, f32[256,256]{1,0:T(8,128)S(1)}, u32[]{:S(2)}, u32[]{:S(2)}) collective-permute-start(f32[256,256]{1,0:T(8,128)S(1)} %second_inverse.1), channel_id=1, source_target_pairs={{0,1},{1,0},{2,3},{3,2},{4,5},{5,4},{6,7},{7,6},{8,9},{9,8},{10,11... | collective-permute-start | bytes 786440 | tf_op jit(solution)/shard_map/ppermute | solution.py:536
  (65 shorter events, 27.7 us)
Async XLA Ops:
  5.5 20.3 %collective-permute-start.1 = (bf16[656,256]{1,0:T(8,128)(2,1)S(1)}, bf16[656,256]{1,0:T(8,128)(2,1)S(1)}, u32[]{:S(2)}, u32[]{:S(2)}) collective-permute-start(bf16[656,256]{1,0:T(8,128)(2,1)S(1)} %get-tuple-element.47.refs_2_.own_0), channel_id=1, source_target_pairs={{0,32},{32,64},{64,96},{96,0},{1,33},{33,65},{65,97},{97,1},{2,34}... | collective-permute-start | bytes 1007624 | tf_op jit(solution)/shard_map/ppermute | solution.py:541
  7.7 18.1 %collective-permute-start.2 = (bf16[656,256]{1,0:T(8,128)(2,1)S(1)}, bf16[656,256]{1,0:T(8,128)(2,1)S(1)}, u32[]{:S(2)}, u32[]{:S(2)}) collective-permute-start(bf16[656,256]{1,0:T(8,128)(2,1)S(1)} %get-tuple-element.47.refs_2_.own_0), channel_id=1, source_target_pairs={{0,64},{32,96},{64,0},{96,32},{1,65},{33,97},{65,1},{97,33},{2,66}... | collective-permute-start | bytes 1007624 | tf_op jit(solution)/shard_map/ppermute | solution.py:541
  10.3 15.5 %collective-permute-start.3 = (bf16[656,256]{1,0:T(8,128)(2,1)S(1)}, bf16[656,256]{1,0:T(8,128)(2,1)S(1)}, u32[]{:S(2)}, u32[]{:S(2)}) collective-permute-start(bf16[656,256]{1,0:T(8,128)(2,1)S(1)} %get-tuple-element.47.refs_2_.own_0), channel_id=1, source_target_pairs={{0,96},{32,0},{64,32},{96,64},{1,97},{33,1},{65,33},{97,65},{2,98}... | collective-permute-start | bytes 1007624 | tf_op jit(solution)/shard_map/ppermute | solution.py:541
  11.4 2.7 %collective-permute-start = (f32[64,8,128]{2,1,0:T(8,128)S(1)}, f32[64,8,128]{2,1,0:T(8,128)S(1)}, u32[]{:S(2)}, u32[]{:S(2)}) collective-permute-start(f32[64,8,128]{2,1,0:T(8,128)S(1)} %get-tuple-element.39), channel_id=1, source_target_pairs={{0,1},{1,0},{2,3},{3,2},{4,5},{5,4},{6,7},{7,6},{8,9},{9,8},{10,11... | collective-permute-start | bytes 786440 | tf_op jit(solution)/shard_map/ppermute | solution.py:536
  14.8 19.5 %all-to-all-start = ((f32[64,1,8,128]{3,2,1,0:T(8,128)}), f32[64,1,8,128]{3,2,1,0:T(8,128)S(1)}, u32[]{:S(2)}, u32[]{:S(2)}) async-start(f32[64,1,8,128]{3,2,1,0:T(8,128)} %bitcast.3), calls=%async_computation | async-start | bytes 524288 | tf_op jit(solution)/shard_map/all_to_all | solution.py:545
  35.1 23.8 %all-to-all-start.1 = ((f32[64,1,8,128]{3,2,1,0:T(8,128)}), f32[64,1,8,128]{3,2,1,0:T(8,128)S(1)}, u32[]{:S(2)}, u32[]{:S(2)}) async-start(f32[64,1,8,128]{3,2,1,0:T(8,128)} %broadcast_in_dim.18), calls=%async_computation.1 | async-start | bytes 524288 | tf_op jit(solution)/shard_map/all_to_all | solution.py:545
  46.5 12.4 %collective-permute-start.4 = (f32[1024,256]{1,0:T(8,128)}, f32[1024,256]{1,0:T(8,128)}, u32[]{:S(2)}, u32[]{:S(2)}) collective-permute-start(f32[1024,256]{1,0:T(8,128)} %get-tuple-element.52), channel_id=1, source_target_pairs={{0,1},{1,0},{2,3},{3,2},{4,5},{5,4},{6,7},{7,6},{8,9},{9,8},{10,11... | collective-permute-start | bytes 3145736 | tf_op jit(solution)/shard_map/ppermute | solution.py:536
  61.1 14.7 %all-to-all-start.2 = ((bf16[16,64,256]{2,1,0:T(8,128)(2,1)}), bf16[16,64,256]{2,1,0:T(8,128)(2,1)S(1)}, u32[]{:S(2)}, u32[]{:S(2)}) async-start(bf16[16,64,256]{2,1,0:T(8,128)(2,1)} %bitcast.6), calls=%async_computation.2 | async-start | bytes 1048576 | tf_op jit(solution)/shard_map/all_to_all | solution.py:545
  66.5 14.8 %collective-permute-start.6 = (f32[64,8,128]{2,1,0:T(8,128)S(1)}, f32[64,8,128]{2,1,0:T(8,128)S(1)}, u32[]{:S(2)}, u32[]{:S(2)}) collective-permute-start(f32[64,8,128]{2,1,0:T(8,128)S(1)} %bitcast.20), channel_id=1, source_target_pairs={{0,1},{1,0},{2,3},{3,2},{4,5},{5,4},{6,7},{7,6},{8,9},{9,8},{10,11... | collective-permute-start | bytes 786440 | tf_op jit(solution)/shard_map/ppermute | solution.py:536
  68.6 12.7 %collective-permute-start.5 = (f32[8,128]{1,0:T(8,128)S(1)}, f32[8,128]{1,0:T(8,128)S(1)}, u32[]{:S(2)}, u32[]{:S(2)}) collective-permute-start(f32[8,128]{1,0:T(8,128)S(1)} %get-tuple-element.53.ring), channel_id=1, source_target_pairs={{0,1},{1,0},{2,3},{3,2},{4,5},{5,4},{6,7},{7,6},{8,9},{9,8},{10,11... | collective-permute-start | bytes 12296 | tf_op jit(solution)/shard_map/ppermute | solution.py:536
  76.9 22.1 %all-to-all-start.3 = ((f32[16,64,256]{2,1,0:T(8,128)}), f32[16,64,256]{2,1,0:T(8,128)}, u32[]{:S(2)}, u32[]{:S(2)}) async-start(f32[16,64,256]{2,1,0:T(8,128)} %broadcast_in_dim.19), calls=%async_computation.3 | async-start | bytes 2097152 | tf_op jit(solution)/shard_map/all_to_all | solution.py:545
  82.2 18.0 %collective-permute-start.7 = (f32[256,256]{1,0:T(8,128)S(1)}, f32[256,256]{1,0:T(8,128)S(1)}, u32[]{:S(2)}, u32[]{:S(2)}) collective-permute-start(f32[256,256]{1,0:T(8,128)S(1)} %first_inverse.1), channel_id=1, source_target_pairs={{0,1},{1,0},{2,3},{3,2},{4,5},{5,4},{6,7},{7,6},{8,9},{9,8},{10,11... | collective-permute-start | bytes 786440 | tf_op jit(solution)/shard_map/ppermute | solution.py:536
  99.0 20.1 %collective-permute-start.12 = (f32[1024,256]{1,0:T(8,128)}, f32[1024,256]{1,0:T(8,128)S(1)}, u32[]{:S(2)}, u32[]{:S(2)}) collective-permute-start(f32[1024,256]{1,0:T(8,128)} %bitcast.8), channel_id=1, source_target_pairs={{0,1},{1,0},{2,3},{3,2},{4,5},{5,4},{6,7},{7,6},{8,9},{9,8},{10,11... | collective-permute-start | bytes 3145736 | tf_op jit(solution)/shard_map/ppermute | solution.py:536
  104.4 11.9 %collective-permute-start.8 = (f32[256,256]{1,0:T(8,128)S(1)}, f32[256,256]{1,0:T(8,128)S(1)}, u32[]{:S(2)}, u32[]{:S(2)}) collective-permute-start(f32[256,256]{1,0:T(8,128)S(1)} %fusion.8), channel_id=1, source_target_pairs={{0,1},{1,0},{2,3},{3,2},{4,5},{5,4},{6,7},{7,6},{8,9},{9,8},{10,11... | collective-permute-start | bytes 786440 | tf_op jit(solution)/shard_map/ppermute | solution.py:536
  104.8 6.3 %collective-permute-start.13 = (f32[1,256]{1,0:T(1,128)S(1)}, f32[1,256]{1,0:T(1,128)S(1)}, u32[]{:S(2)}, u32[]{:S(2)}) collective-permute-start(f32[1,256]{1,0:T(1,128)S(1)} %bitcast.23), channel_id=1, source_target_pairs={{0,32},{32,64},{64,96},{96,0},{1,33},{33,65},{65,97},{97,1},{2,34}... | collective-permute-start | bytes 3080 | tf_op jit(solution)/shard_map/ppermute | solution.py:541
  108.5 3.9 %collective-permute-start.14 = (f32[1,256]{1,0:T(1,128)S(1)}, f32[1,256]{1,0:T(1,128)S(1)}, u32[]{:S(2)}, u32[]{:S(2)}) collective-permute-start(f32[1,256]{1,0:T(1,128)S(1)} %bitcast.24), channel_id=1, source_target_pairs={{0,64},{32,96},{64,0},{96,32},{1,65},{33,97},{65,1},{97,33},{2,66}... | collective-permute-start | bytes 3080 | tf_op jit(solution)/shard_map/ppermute | solution.py:541
  111.1 2.7 %collective-permute-start.15 = (f32[1,256]{1,0:T(1,128)S(1)}, f32[1,256]{1,0:T(1,128)S(1)}, u32[]{:S(2)}, u32[]{:S(2)}) collective-permute-start(f32[1,256]{1,0:T(1,128)S(1)} %bitcast.25), channel_id=1, source_target_pairs={{0,96},{32,0},{64,32},{96,64},{1,97},{33,1},{65,33},{97,65},{2,98}... | collective-permute-start | bytes 3080 | tf_op jit(solution)/shard_map/ppermute | solution.py:541
  116.3 13.7 %collective-permute-start.10 = (f32[256,256]{1,0:T(8,128)S(1)}, f32[256,256]{1,0:T(8,128)S(1)}, u32[]{:S(2)}, u32[]{:S(2)}) collective-permute-start(f32[256,256]{1,0:T(8,128)S(1)} %add.39.part_0), channel_id=1, source_target_pairs={{0,64},{32,96},{64,0},{96,32},{1,65},{33,97},{65,1},{97,33},{2,66}... | collective-permute-start | bytes 786440 | tf_op jit(solution)/shard_map/ppermute | solution.py:541
  117.6 12.4 %collective-permute-start.11 = (f32[256,256]{1,0:T(8,128)S(1)}, f32[256,256]{1,0:T(8,128)S(1)}, u32[]{:S(2)}, u32[]{:S(2)}) collective-permute-start(f32[256,256]{1,0:T(8,128)S(1)} %add.39.part_0), channel_id=1, source_target_pairs={{0,96},{32,0},{64,32},{96,64},{1,97},{33,1},{65,33},{97,65},{2,98}... | collective-permute-start | bytes 786440 | tf_op jit(solution)/shard_map/ppermute | solution.py:541
  118.2 13.5 %collective-permute-start.9 = (f32[256,256]{1,0:T(8,128)S(1)}, f32[256,256]{1,0:T(8,128)S(1)}, u32[]{:S(2)}, u32[]{:S(2)}) collective-permute-start(f32[256,256]{1,0:T(8,128)S(1)} %add.39.part_0), channel_id=1, source_target_pairs={{0,32},{32,64},{64,96},{96,0},{1,33},{33,65},{65,97},{97,1},{2,34}... | collective-permute-start | bytes 786440 | tf_op jit(solution)/shard_map/ppermute | solution.py:541
  131.7 10.2 %collective-permute-start.17 = (bf16[512,256]{1,0:T(8,128)(2,1)S(1)}, bf16[512,256]{1,0:T(8,128)(2,1)S(1)}, u32[]{:S(2)}, u32[]{:S(2)}) collective-permute-start(bf16[512,256]{1,0:T(8,128)(2,1)S(1)} %get-tuple-element.59), channel_id=1, source_target_pairs={{0,32},{32,64},{64,96},{96,0},{1,33},{33,65},{65,97},{97,1},{2,34}... | collective-permute-start | bytes 786440 | tf_op jit(solution)/shard_map/ppermute | solution.py:541
  131.7 14.0 %collective-permute-start.18 = (bf16[512,256]{1,0:T(8,128)(2,1)S(1)}, bf16[512,256]{1,0:T(8,128)(2,1)S(1)}, u32[]{:S(2)}, u32[]{:S(2)}) collective-permute-start(bf16[512,256]{1,0:T(8,128)(2,1)S(1)} %get-tuple-element.60), channel_id=1, source_target_pairs={{0,64},{32,96},{64,0},{96,32},{1,65},{33,97},{65,1},{97,33},{2,66}... | collective-permute-start | bytes 786440 | tf_op jit(solution)/shard_map/ppermute | solution.py:541
  134.0 12.3 %collective-permute-start.19 = (bf16[512,256]{1,0:T(8,128)(2,1)S(1)}, bf16[512,256]{1,0:T(8,128)(2,1)S(1)}, u32[]{:S(2)}, u32[]{:S(2)}) collective-permute-start(bf16[512,256]{1,0:T(8,128)(2,1)S(1)} %get-tuple-element.61), channel_id=1, source_target_pairs={{0,96},{32,0},{64,32},{96,64},{1,97},{33,1},{65,33},{97,65},{2,98}... | collective-permute-start | bytes 786440 | tf_op jit(solution)/shard_map/ppermute | solution.py:541
  146.3 9.0 %collective-permute-start.20 = (f32[256,256]{1,0:T(8,128)S(1)}, f32[256,256]{1,0:T(8,128)S(1)}, u32[]{:S(2)}, u32[]{:S(2)}) collective-permute-start(f32[256,256]{1,0:T(8,128)S(1)} %second_inverse.1), channel_id=1, source_target_pairs={{0,1},{1,0},{2,3},{3,2},{4,5},{5,4},{6,7},{7,6},{8,9},{9,8},{10,11... | collective-permute-start | bytes 786440 | tf_op jit(solution)/shard_map/ppermute | solution.py:536
  (8 other events, 124.4 us)

commit v4 on v3

--- a/solution.py
+++ b/solution.py
@@ -90,31 +90,39 @@
     ]
 
 
-def invert(out, work):
-    n = work.shape[0]
-    width = 64
+WIDTH = 64
+
+
+def scales(matrix):
+    n = matrix.shape[0]
     row = lax.broadcasted_iota(jnp.int32, (n, n), 0)
     col = lax.broadcasted_iota(jnp.int32, (n, n), 1)
-    diag = jnp.where(row == col, work[...], 0.0)
-    scale_row = lax.rsqrt(jnp.sum(diag, axis=0, keepdims=True))
-    scale_col = lax.rsqrt(jnp.sum(diag, axis=1, keepdims=True))
-    work[...] = work[...] * scale_row * scale_col
-    for b in range(n // width):
-        span = slice(b * width, (b + 1) * width)
+    diag = jnp.where(row == col, matrix, 0.0)
+    return (
+        lax.rsqrt(jnp.sum(diag, axis=0, keepdims=True)),
+        lax.rsqrt(jnp.sum(diag, axis=1, keepdims=True)),
+    )
+
+
+def eliminate(work, blocks):
+    n = work.shape[0]
+    row = lax.broadcasted_iota(jnp.int32, (n, n), 0)
+    col = lax.broadcasted_iota(jnp.int32, (n, n), 1)
+    for b in blocks:
+        span = slice(b * WIDTH, (b + 1) * WIDTH)
         block = invert_block(work[span, span])
         rows = jnp.dot(block, work[span, :], precision=HIGHEST, preferred_element_type=F32)
-        parts = [jnp.zeros((width, width), F32)] * (n // width)
+        parts = [jnp.zeros((WIDTH, WIDTH), F32)] * (n // WIDTH)
         parts[b] = block
         padded = jnp.concatenate(parts, axis=1)
-        in_block = (col >= b * width) & (col < (b + 1) * width)
-        rows = jnp.where(in_block[0:width], padded, rows)
+        in_block = (col >= b * WIDTH) & (col < (b + 1) * WIDTH)
+        rows = jnp.where(in_block[0:WIDTH], padded, rows)
         left = work[:, span]
-        left_row = row[:, 0:width]
-        left = jnp.where((left_row >= b * width) & (left_row < (b + 1) * width), 0.0, left)
+        left_row = row[:, 0:WIDTH]
+        left = jnp.where((left_row >= b * WIDTH) & (left_row < (b + 1) * WIDTH), 0.0, left)
         base = jnp.where(in_block, 0.0, work[...])
         work[...] = base - jnp.dot(left, rows, precision=HIGHEST, preferred_element_type=F32)
         work[span, :] = rows
-    out[...] = work[...] * scale_row * scale_col
 
 
 def takes_turn(meta, ring, other_ring):
@@ -122,7 +130,17 @@
     return (mine < other) | ((mine == other) & (meta[2] == 0))
 
 
-def first_inverse_kernel(meta, ring, other_ring, near, far, out, work):
+def first_inverse_start_kernel(meta, ring, other_ring, near, far, work):
+    @pl.when(takes_turn(meta, ring, other_ring))
+    def _():
+        for t, rows, cols in tiles_of(work):
+            work[rows, cols] = near[t] * far[t]
+        scale_row, scale_col = scales(work[...])
+        work[...] = work[...] * scale_row * scale_col
+        eliminate(work, [0])
+
+
+def first_inverse_end_kernel(meta, ring, other_ring, near, far, begun, out, work):
     mine = takes_turn(meta, ring, other_ring)
 
     @pl.when(jnp.logical_not(mine))
@@ -131,9 +149,12 @@
 
     @pl.when(mine)
     def _():
-        for t, rows, cols in tiles_of(work):
-            work[rows, cols] = near[t] * far[t]
-        invert(out, work)
+        for t, rows, cols in tiles_of(out):
+            out[rows, cols] = near[t] * far[t]
+        scale_row, scale_col = scales(out[...])
+        work[...] = begun[...]
+        eliminate(work, range(1, work.shape[0] // WIDTH))
+        out[...] = work[...] * scale_row * scale_col
 
 
 def second_inverse_kernel(
@@ -158,10 +179,13 @@
         third_is_near = meta[2] == 1
         for t, rows, cols in tiles_of(work):
             work[rows, cols] = work[rows, cols] * jnp.where(third_is_near, near[t], far[t])
-        invert(out, work)
-
-
-def inverse_of(kernel, name, meta, *arrays):
+        scale_row, scale_col = scales(work[...])
+        work[...] = work[...] * scale_row * scale_col
+        eliminate(work, range(n // WIDTH))
+        out[...] = work[...] * scale_row * scale_col
+
+
+def inverse_of(kernel, name, meta, *arrays, scratch=1):
     n = 256
     return pl.pallas_call(
         kernel,
@@ -169,24 +193,42 @@
         in_specs=[pl.BlockSpec(memory_space=pltpu.SMEM)]
         + [pl.BlockSpec(memory_space=pltpu.VMEM)] * len(arrays),
         out_specs=pl.BlockSpec(memory_space=pltpu.VMEM),
-        scratch_shapes=[pltpu.VMEM((n, n), F32)],
+        scratch_shapes=[pltpu.VMEM((n, n), F32)] * scratch,
         compiler_params=pltpu.CompilerParams(vmem_limit_bytes=VMEM_BYTES),
         cost_estimate=INVERSE_COST,
         name=name,
     )(meta, *arrays)
 
 
-def prepare_kernel(meta, b_hbm, c_hbm, own, gram_keep, gram_send, b_factor, c_factor, sems):
+def solve_kernel(sums, inverse_0, inverse_1, solved, squares, gram, inverse):
+    inverse[...] = inverse_0[...] + inverse_1[...]
+    rows = jnp.dot(sums[...], inverse[...], precision=HIGHEST, preferred_element_type=F32)
+    solved[...] = rows
+    squares[...] = jnp.sum(rows * rows, axis=0, keepdims=True)
+    gram[...] = lax.dot_general(
+        rows, rows, (((0,), (0,)), ((), ())), precision=HIGHEST, preferred_element_type=F32
+    )
+
+
+def solve(sums, inverse_0, inverse_1):
+    rank = sums.shape[1]
+    square = jax.ShapeDtypeStruct((rank, rank), F32)
+    return pl.pallas_call(
+        solve_kernel,
+        out_shape=[
+            jax.ShapeDtypeStruct(sums.shape, F32),
+            jax.ShapeDtypeStruct((1, rank), F32),
+            square,
+            square,
+        ],
+        compiler_params=pltpu.CompilerParams(vmem_limit_bytes=2 * VMEM_BYTES),
+        name="solve",
+    )(sums, inverse_0, inverse_1)
+
+
+def prepare_kernel(meta, b_factor, c_factor, own, gram_keep, gram_send):
     rows = b_factor.shape[0]
     core = meta[2]
-    wait_all(
-        copy_all(
-            [
-                pltpu.make_async_copy(b_hbm, b_factor, sems.at[0]),
-                pltpu.make_async_copy(c_hbm, c_factor, sems.at[1]),
-            ]
-        )
-    )
     own[0:rows, :] = b_factor[...].astype(BF16)
     own[rows : rows + C_ROWS, :] = c_factor[...].astype(BF16)
     count = meta[0].astype(F32)
@@ -218,14 +260,20 @@
     return pl.pallas_call(
         prepare_kernel,
         out_shape=[jax.ShapeDtypeStruct((rows, rank), BF16), tiles, tiles],
-        in_specs=[pl.BlockSpec(memory_space=pltpu.SMEM)]
-        + [pl.BlockSpec(memory_space=pl.ANY)] * 2,
-        scratch_shapes=[
-            pltpu.VMEM(b_factor.shape, F32),
-            pltpu.VMEM(c_factor.shape, F32),
-            pltpu.SemaphoreType.DMA((2,)),
-        ],
-        compiler_params=pltpu.CompilerParams(vmem_limit_bytes=VMEM_BYTES),
+        grid_spec=pltpu.PrefetchScalarGridSpec(
+            num_scalar_prefetch=1,
+            grid=(1,),
+            in_specs=[
+                pl.BlockSpec(b_factor.shape, lambda step, meta: (0, 0)),
+                pl.BlockSpec(c_factor.shape, lambda step, meta: (0, 0)),
+            ],
+            out_specs=[
+                pl.BlockSpec((rows, rank), lambda step, meta: (0, 0)),
+                pl.BlockSpec(tiles.shape, lambda step, meta: (0, 0, 0)),
+                pl.BlockSpec(tiles.shape, lambda step, meta: (0, 0, 0)),
+            ],
+        ),
+        compiler_params=pltpu.CompilerParams(vmem_limit_bytes=2 * VMEM_BYTES),
         name="prepare",
     )(meta, b_factor, c_factor)
 
@@ -572,20 +620,23 @@
 
     pair_sum = (keep + to_other_core(send)).astype(BF16)
     arrived = exchange(pair_sum.reshape(plane, -1, rank), PLANE)
+    begun = inverse_of(
+        first_inverse_start_kernel, "first_inverse_start", meta, *rings, gram_near, gram_far, scratch=0
+    )
+    begun, arrived = lax.optimization_barrier((begun, arrived))
     sum_own = jnp.sum(arrived.astype(F32), axis=0)
     sum_near = exchange(jnp.broadcast_to(sum_own[None], (plane,) + sum_own.shape), PLANE)
     sum_near = sum_near.reshape(-1, rank)
 
-    inverse = inverse_of(first_inverse_kernel, "first_inverse", meta, *rings, gram_near, gram_far)
-    inverse = lax.optimization_barrier(inverse + to_other_core(inverse))
-
+    inverse = inverse_of(
+        first_inverse_end_kernel, "first_inverse_end", meta, *rings, gram_near, gram_far, begun
+    )
+    inverse, sum_near = lax.optimization_barrier((inverse, sum_near))
     sum_far = to_other_core(sum_near)
-    a_near = jnp.dot(sum_near, inverse, precision=HIGHEST)
-    squares = jnp.sum(a_near * a_near, axis=0, keepdims=True)
+    a_near, squares, gram_core, inverse = solve(sum_near, inverse, to_other_core(inverse))
     squares = squares + along_groups(squares, 1) + along_groups(squares, 2) + along_groups(squares, 3)
     squares = squares + to_other_core(squares)
     a_far = jnp.dot(sum_far, inverse, precision=HIGHEST)
-    gram_core = jnp.dot(a_near.T, a_near, precision=HIGHEST)
     gram_plane = gram_core + to_other_core(gram_core)
     gram_parts = [gram_plane] + [along_groups(gram_plane, q) for q in (1, 2, 3)]
 

time: 157 us -> 159 us (1.013); the launches traced: 157 us -> 160 us
  waiting for transfers between devices: 18.9 us -> 43.7 us
  starting transfers between devices: 84.4 us -> 68.5 us
  matrix products: 7.47 us -> 3.33 us
    all_to_all x4, waiting for transfers between devices: 7.12 us -> 28 us  [exchange(): return lax.all_to_all(value, axes, 0, 0)]
    ppermute x9, starting transfers between devices: 36.2 us -> 19.3 us  [to_other_core(): return lax.ppermute(value, 'core', [(0, 1), (1, 0)])]
    pallas_call x4, Pallas kernels: 30.4 us -> 26 us  [mode_call(): pl.pallas_call(kernel, out_shape=out_shape, in_specs=[smem] + [anywhere]...]
    dot_general x2 -> x0, matrix products: 4.15 us -> none  [the longest x1 2.24 us: on_device(): a_near = jnp.dot(sum_near, inverse, precision=HIGHEST)]
    pallas_call x0 -> x1, Pallas kernels: none -> 3.37 us  [solve(): pl.pallas_call(solve_kernel, out_shape=[jax.ShapeDtypeStruct(sums.shape,...]
    ppermute x9, waiting for transfers between devices: 2.96 us -> 4.93 us  [to_other_core(): return lax.ppermute(value, 'core', [(0, 1), (1, 0)])]
    ppermute x12, waiting for transfers between devices: 8.81 us -> 10.7 us  [along_groups(): lax.ppermute(value, 'grp', [(p, (p + shift) % size) for p in range(size)])]
  transfers between devices with their start and end apart: 25 -> 25, of which waited for: 10 -> 13; matrix products, arithmetic and copies ran while one was open for 5% -> 3% of each run, Pallas kernels for 22% -> 21%
where the time goes in v4:
time: 159 us; the launch traced here: 160 us
  starting transfers between devices  68.5 us (43%)
  waiting for transfers between devices  43.7 us (27%)
  Pallas kernels  35.7 us (22%)
  local copies, waits for them, and re-layouts  4.44 us (3%)
  matrix products  3.33 us (2%)
  other arithmetic  3.19 us (2%)
    all_to_all x4, starting transfers between devices, exchange(): return lax.all_to_all(value, axes, 0, 0)  31 us
    all_to_all x4, waiting for transfers between devices, exchange(): return lax.all_to_all(value, axes, 0, 0)  28 us
    pallas_call x4, Pallas kernels, mode_call(): pl.pallas_call(kernel, out_shape=out_shape, in_specs=[smem] + [anywhere]...  26 us
    ppermute x9, starting transfers between devices, to_other_core(): return lax.ppermute(value, 'core', [(0, 1), (1, 0)])  19.3 us
    ppermute x12, starting transfers between devices, along_groups(): lax.ppermute(value, 'grp', [(p, (p + shift) % size) for p in range(size)])  18.2 us
    ppermute x12, waiting for transfers between devices, along_groups(): lax.ppermute(value, 'grp', [(p, (p + shift) % size) for p in range(size)])  10.7 us
    ppermute x9, waiting for transfers between devices, to_other_core(): return lax.ppermute(value, 'core', [(0, 1), (1, 0)])  4.93 us
    pallas_call x1, Pallas kernels, solve(): pl.pallas_call(solve_kernel, out_shape=[jax.ShapeDtypeStruct(sums.shape,...  3.37 us
  transfers between devices with their start and end apart: 25, of which 13 were waited for; matrix products, arithmetic and copies ran while one was open for 3% of the time, Pallas kernels for 21%

profile of v4, /device:TPU:1, one launch (start us, length us, event | category | flops | bytes accessed | tf_op | source)
XLA Modules:
  0.0 160.3 jit_solution(15417548284181550836)
XLA Ops:
  5.3 2.2 %collective-permute-start.1 = (bf16[656,256]{1,0:T(8,128)(2,1)S(1)}, bf16[656,256]{1,0:T(8,128)(2,1)S(1)}, u32[]{:S(2)}, u32[]{:S(2)}) collective-permute-start(bf16[656,256]{1,0:T(8,128)(2,1)S(1)} %get-tuple-element.56.refs_2_.own_0), channel_id=1, source_target_pairs={{0,32},{32,64},{64,96},{96,0},{1,33},{33,65},{65,97},{97,1},{2,34}... | collective-permute-start | bytes 1007624 | tf_op jit(solution)/shard_map/ppermute | solution.py:589
  7.5 2.6 %collective-permute-start.2 = (bf16[656,256]{1,0:T(8,128)(2,1)S(1)}, bf16[656,256]{1,0:T(8,128)(2,1)S(1)}, u32[]{:S(2)}, u32[]{:S(2)}) collective-permute-start(bf16[656,256]{1,0:T(8,128)(2,1)S(1)} %get-tuple-element.56.refs_2_.own_0), channel_id=1, source_target_pairs={{0,64},{32,96},{64,0},{96,32},{1,65},{33,97},{65,1},{97,33},{2,66}... | collective-permute-start | bytes 1007624 | tf_op jit(solution)/shard_map/ppermute | solution.py:589
  14.6 8.6 %all-to-all-start = ((f32[64,1,8,128]{3,2,1,0:T(8,128)}), f32[64,1,8,128]{3,2,1,0:T(8,128)S(1)}, u32[]{:S(2)}, u32[]{:S(2)}) async-start(f32[64,1,8,128]{3,2,1,0:T(8,128)} %bitcast.3), calls=%async_computation | async-start | bytes 524288 | tf_op jit(solution)/shard_map/all_to_all | solution.py:593
  23.2 2.1 %order_slots.1 = (s32[256]{0:T(256)}, s32[256]{0:T(256)}) custom-call(s32[3]{0:T(128)} %copy-done.2, s32[192]{0:T(256)} %i_idx.1, s32[192]{0:T(256)} %j_idx.1, s32[192]{0:T(256)} %k_idx.1), custom_call_target="tpu_custom_call" | custom-call | tf_op jit(solution)/shard_map/order_slots/pallas_call | solution.py:315
  26.1 7.0 %mode_one_other_core.1 = (f32[1024,256]{1,0:T(8,128)}, f32[8,128]{1,0:T(8,128)S(1)}) custom-call(s32[256]{0:T(256)S(1)} %copy-done.5, bf16[192,32,1024]{2,1,0:T(8,128)(2,1)} %blocks.3, bf16[656,256]{1,0:T(8,128)(2,1)S(1)} %get-tuple-element.56.refs_2_.own_0, bf16[656,256]{1,0:T(8,128)(2,1)S(1)} %collective-permute-done.1.refs_3_.own_1, ...), custom_call_target="tpu_custom_call" | custom-call | flops 15000000512 | bytes 48000000 | tf_op jit(solution)/shard_map/mode_one_other_core/pallas_call | solution.py:527
  34.7 15.2 %all-to-all-start.1 = ((f32[64,1,8,128]{3,2,1,0:T(8,128)}), f32[64,1,8,128]{3,2,1,0:T(8,128)S(1)}, u32[]{:S(2)}, u32[]{:S(2)}) async-start(f32[64,1,8,128]{3,2,1,0:T(8,128)} %broadcast_in_dim.7), calls=%async_computation.1 | async-start | bytes 524288 | tf_op jit(solution)/shard_map/all_to_all | solution.py:593
  50.8 5.2 %mode_one_own_core.1 = f32[1024,256]{1,0:T(8,128)S(1)} custom-call(s32[256]{0:T(256)S(1)} %copy-done.6, bf16[192,32,1024]{2,1,0:T(8,128)(2,1)} %blocks.3, bf16[656,256]{1,0:T(8,128)(2,1)S(1)} %get-tuple-element.56.refs_2_.own_0, bf16[656,256]{1,0:T(8,128)(2,1)S(1)} %collective-permute-done.1.refs_3_.own_1, ...), custom_call_target="tpu_custom_call" | custom-call | flops 15000000512 | bytes 48000000 | tf_op jit(solution)/shard_map/mode_one_own_core/pallas_call | solution.py:527
  56.0 3.4 %all-to-all-done.1 = f32[64,1,8,128]{3,2,1,0:T(8,128)S(1)} async-done(((f32[64,1,8,128]{3,2,1,0:T(8,128)}), f32[64,1,8,128]{3,2,1,0:T(8,128)S(1)}, u32[]{:S(2)}, u32[]{:S(2)}) %all-to-all-start.1) | async-done | bytes 262176 | tf_op jit(solution)/shard_map/all_to_all | solution.py:593
  59.4 2.0 %collective-permute-start.5 = (f32[64,8,128]{2,1,0:T(8,128)S(1)}, f32[64,8,128]{2,1,0:T(8,128)S(1)}, u32[]{:S(2)}, u32[]{:S(2)}) collective-permute-start(f32[64,8,128]{2,1,0:T(8,128)S(1)} %bitcast.17), channel_id=1, source_target_pairs={{0,1},{1,0},{2,3},{3,2},{4,5},{5,4},{6,7},{7,6},{8,9},{9,8},{10,11... | collective-permute-start | bytes 786440 | tf_op jit(solution)/shard_map/ppermute | solution.py:584
  61.4 2.2 %add_convert_fusion = bf16[1024,256]{1,0:T(8,128)(2,1)} fusion(f32[1024,256]{1,0:T(8,128)S(1)} %mode_one_own_core.1, f32[1024,256]{1,0:T(8,128)} %collective-permute-done.6), kind=kLoop, calls=%fused_computation.1 | loop fusion | flops 524288 | bytes 2621440 | tf_op jit(solution)/shard_map/convert_element_type | solution.py:621
  63.6 3.6 %all-to-all-start.2 = ((bf16[16,64,256]{2,1,0:T(8,128)(2,1)}), bf16[16,64,256]{2,1,0:T(8,128)(2,1)S(1)}, u32[]{:S(2)}, u32[]{:S(2)}) async-start(bf16[16,64,256]{2,1,0:T(8,128)(2,1)} %bitcast.7), calls=%async_computation.2 | async-start | bytes 1048576 | tf_op jit(solution)/shard_map/all_to_all | solution.py:593
  67.9 10.3 %all-to-all-done.2 = bf16[16,64,256]{2,1,0:T(8,128)(2,1)S(1)} async-done(((bf16[16,64,256]{2,1,0:T(8,128)(2,1)}), bf16[16,64,256]{2,1,0:T(8,128)(2,1)S(1)}, u32[]{:S(2)}, u32[]{:S(2)}) %all-to-all-start.2) | async-done | bytes 524320 | tf_op jit(solution)/shard_map/all_to_all | solution.py:593
  79.3 3.7 %all-to-all-start.3 = ((f32[16,64,256]{2,1,0:T(8,128)}), f32[16,64,256]{2,1,0:T(8,128)S(1)}, u32[]{:S(2)}, u32[]{:S(2)}) async-start(f32[16,64,256]{2,1,0:T(8,128)} %broadcast_in_dim.16), calls=%async_computation.3 | async-start | bytes 2097152 | tf_op jit(solution)/shard_map/all_to_all | solution.py:593
  83.8 14.3 %all-to-all-done.3 = f32[16,64,256]{2,1,0:T(8,128)S(1)} async-done(((f32[16,64,256]{2,1,0:T(8,128)}), f32[16,64,256]{2,1,0:T(8,128)S(1)}, u32[]{:S(2)}, u32[]{:S(2)}) %all-to-all-start.3) | async-done | bytes 1048608 | tf_op jit(solution)/shard_map/all_to_all | solution.py:593
  98.2 3.2 %collective-permute-start.12 = (f32[1024,256]{1,0:T(8,128)S(1)}, f32[1024,256]{1,0:T(8,128)S(1)}, u32[]{:S(2)}, u32[]{:S(2)}) collective-permute-start(f32[1024,256]{1,0:T(8,128)S(1)} %bitcast.15), channel_id=1, source_target_pairs={{0,1},{1,0},{2,3},{3,2},{4,5},{5,4},{6,7},{7,6},{8,9},{9,8},{10,11... | collective-permute-start | bytes 3145736 | tf_op jit(solution)/shard_map/ppermute | solution.py:584
  101.4 2.7 %collective-permute-done.7.inverse_1 = f32[256,256]{1,0:T(8,128)S(1)} collective-permute-done((f32[256,256]{1,0:T(8,128)S(1)}, f32[256,256]{1,0:T(8,128)S(1)}, u32[]{:S(2)}, u32[]{:S(2)}) %collective-permute-start.7) | collective-permute-done | bytes 262176 | tf_op jit(solution)/shard_map/ppermute | solution.py:584
  104.0 3.4 %solve.1 = (f32[1024,256]{1,0:T(8,128)S(1)}, f32[1,256]{1,0:T(1,128)S(1)}, f32[256,256]{1,0:T(8,128)S(1)}, f32[256,256]{1,0:T(8,128)S(1)}) custom-call(f32[1024,256]{1,0:T(8,128)S(1)} %bitcast.16, f32[256,256]{1,0:T(8,128)S(1)} %first_inverse_end.1.inverse_0, f32[256,256]{1,0:T(8,128)S(1)} %collective-permute-done.7.inverse_1), custom_call_target="tpu_custom_call" | custom-call | tf_op jit(solution)/shard_map/solve/pallas_call | solution.py:216
  108.0 6.0 %collective-permute-start.14 = (f32[1,256]{1,0:T(1,128)S(1)}, f32[1,256]{1,0:T(1,128)S(1)}, u32[]{:S(2)}, u32[]{:S(2)}) collective-permute-start(f32[1,256]{1,0:T(1,128)S(1)} %get-tuple-element.71), channel_id=1, source_target_pairs={{0,64},{32,96},{64,0},{96,32},{1,65},{33,97},{65,1},{97,33},{2,66}... | collective-permute-start | bytes 3080 | tf_op jit(solution)/shard_map/ppermute | solution.py:589
  123.0 8.9 %mode_two_other_groups.1 = (bf16[512,256]{1,0:T(8,128)(2,1)S(1)}, bf16[512,256]{1,0:T(8,128)(2,1)S(1)}, bf16[512,256]{1,0:T(8,128)(2,1)S(1)}, bf16[2048,256]{1,0:T(8,128)(2,1)S(1)}) custom-call(s32[256]{0:T(256)S(1)} %copy-done.4, bf16[192,32,1024]{2,1,0:T(8,128)(2,1)} %blocks.3, bf16[656,256]{1,0:T(8,128)(2,1)S(1)} %get-tuple-element.56.refs_2_.own_0, ...), custom_call_target="tpu_custom_call" | custom-call | flops 15000000512 | bytes 48000000 | tf_op jit(solution)/shard_map/mode_two_other_groups/pallas_call | solution.py:527
  132.5 2.1 %collective-permute-done.9.part_1 = f32[256,256]{1,0:T(8,128)S(1)} collective-permute-done((f32[256,256]{1,0:T(8,128)S(1)}, f32[256,256]{1,0:T(8,128)S(1)}, u32[]{:S(2)}, u32[]{:S(2)}) %collective-permute-start.9) | collective-permute-done | bytes 262176 | tf_op jit(solution)/shard_map/ppermute | solution.py:589
  134.6 2.3 %collective-permute-start.18 = (bf16[512,256]{1,0:T(8,128)(2,1)S(1)}, bf16[512,256]{1,0:T(8,128)(2,1)S(1)}, u32[]{:S(2)}, u32[]{:S(2)}) collective-permute-start(bf16[512,256]{1,0:T(8,128)(2,1)S(1)} %get-tuple-element.76), channel_id=1, source_target_pairs={{0,64},{32,96},{64,0},{96,32},{1,65},{33,97},{65,1},{97,33},{2,66}... | collective-permute-start | bytes 786440 | tf_op jit(solution)/shard_map/ppermute | solution.py:589
  138.6 4.9 %mode_two_own_group.1 = f32[512,256]{1,0:T(8,128)S(1)} custom-call(s32[256]{0:T(256)S(1)} %copy-done.4, bf16[192,32,1024]{2,1,0:T(8,128)(2,1)} %blocks.3, bf16[656,256]{1,0:T(8,128)(2,1)S(1)} %get-tuple-element.56.refs_2_.own_0, bf16[656,256]{1,0:T(8,128)(2,1)S(1)} %collective-permute-done.1.refs_3_.own_1, ...), custom_call_target="tpu_custom_call" | custom-call | flops 2000000000 | bytes 6000000 | tf_op jit(solution)/shard_map/mode_two_own_group/pallas_call | solution.py:527
  143.5 5.2 %collective-permute-done.18 = bf16[512,256]{1,0:T(8,128)(2,1)S(1)} collective-permute-done((bf16[512,256]{1,0:T(8,128)(2,1)S(1)}, bf16[512,256]{1,0:T(8,128)(2,1)S(1)}, u32[]{:S(2)}, u32[]{:S(2)}) %collective-permute-start.18) | collective-permute-done | bytes 262176 | tf_op jit(solution)/shard_map/ppermute | solution.py:589
  149.2 8.5 %collective-permute-start.20 = (f32[256,256]{1,0:T(8,128)S(1)}, f32[256,256]{1,0:T(8,128)S(1)}, u32[]{:S(2)}, u32[]{:S(2)}) collective-permute-start(f32[256,256]{1,0:T(8,128)S(1)} %second_inverse.1), channel_id=1, source_target_pairs={{0,1},{1,0},{2,3},{3,2},{4,5},{5,4},{6,7},{7,6},{8,9},{9,8},{10,11... | collective-permute-start | bytes 786440 | tf_op jit(solution)/shard_map/ppermute | solution.py:584
  (64 shorter events, 29.4 us)
Async XLA Ops:
  5.3 20.0 %collective-permute-start.1 = (bf16[656,256]{1,0:T(8,128)(2,1)S(1)}, bf16[656,256]{1,0:T(8,128)(2,1)S(1)}, u32[]{:S(2)}, u32[]{:S(2)}) collective-permute-start(bf16[656,256]{1,0:T(8,128)(2,1)S(1)} %get-tuple-element.56.refs_2_.own_0), channel_id=1, source_target_pairs={{0,32},{32,64},{64,96},{96,0},{1,33},{33,65},{65,97},{97,1},{2,34}... | collective-permute-start | bytes 1007624 | tf_op jit(solution)/shard_map/ppermute | solution.py:589
  7.5 17.9 %collective-permute-start.2 = (bf16[656,256]{1,0:T(8,128)(2,1)S(1)}, bf16[656,256]{1,0:T(8,128)(2,1)S(1)}, u32[]{:S(2)}, u32[]{:S(2)}) collective-permute-start(bf16[656,256]{1,0:T(8,128)(2,1)S(1)} %get-tuple-element.56.refs_2_.own_0), channel_id=1, source_target_pairs={{0,64},{32,96},{64,0},{96,32},{1,65},{33,97},{65,1},{97,33},{2,66}... | collective-permute-start | bytes 1007624 | tf_op jit(solution)/shard_map/ppermute | solution.py:589
  10.1 15.2 %collective-permute-start.3 = (bf16[656,256]{1,0:T(8,128)(2,1)S(1)}, bf16[656,256]{1,0:T(8,128)(2,1)S(1)}, u32[]{:S(2)}, u32[]{:S(2)}) collective-permute-start(bf16[656,256]{1,0:T(8,128)(2,1)S(1)} %get-tuple-element.56.refs_2_.own_0), channel_id=1, source_target_pairs={{0,96},{32,0},{64,32},{96,64},{1,97},{33,1},{65,33},{97,65},{2,98}... | collective-permute-start | bytes 1007624 | tf_op jit(solution)/shard_map/ppermute | solution.py:589
  11.2 2.7 %collective-permute-start = (f32[64,8,128]{2,1,0:T(8,128)S(1)}, f32[64,8,128]{2,1,0:T(8,128)S(1)}, u32[]{:S(2)}, u32[]{:S(2)}) collective-permute-start(f32[64,8,128]{2,1,0:T(8,128)S(1)} %get-tuple-element.47), channel_id=1, source_target_pairs={{0,1},{1,0},{2,3},{3,2},{4,5},{5,4},{6,7},{7,6},{8,9},{9,8},{10,11... | collective-permute-start | bytes 786440 | tf_op jit(solution)/shard_map/ppermute | solution.py:584
  14.6 19.3 %all-to-all-start = ((f32[64,1,8,128]{3,2,1,0:T(8,128)}), f32[64,1,8,128]{3,2,1,0:T(8,128)S(1)}, u32[]{:S(2)}, u32[]{:S(2)}) async-start(f32[64,1,8,128]{3,2,1,0:T(8,128)} %bitcast.3), calls=%async_computation | async-start | bytes 524288 | tf_op jit(solution)/shard_map/all_to_all | solution.py:593
  33.1 34.1 %collective-permute-start.4 = (f32[8,128]{1,0:T(8,128)S(1)}, f32[8,128]{1,0:T(8,128)S(1)}, u32[]{:S(2)}, u32[]{:S(2)}) collective-permute-start(f32[8,128]{1,0:T(8,128)S(1)} %get-tuple-element.51.ring), channel_id=1, source_target_pairs={{0,1},{1,0},{2,3},{3,2},{4,5},{5,4},{6,7},{7,6},{8,9},{9,8},{10,11... | collective-permute-start | bytes 12296 | tf_op jit(solution)/shard_map/ppermute | solution.py:584
  34.7 24.7 %all-to-all-start.1 = ((f32[64,1,8,128]{3,2,1,0:T(8,128)}), f32[64,1,8,128]{3,2,1,0:T(8,128)S(1)}, u32[]{:S(2)}, u32[]{:S(2)}) async-start(f32[64,1,8,128]{3,2,1,0:T(8,128)} %broadcast_in_dim.7), calls=%async_computation.1 | async-start | bytes 524288 | tf_op jit(solution)/shard_map/all_to_all | solution.py:593
  49.9 11.5 %collective-permute-start.6 = (f32[1024,256]{1,0:T(8,128)}, f32[1024,256]{1,0:T(8,128)}, u32[]{:S(2)}, u32[]{:S(2)}) collective-permute-start(f32[1024,256]{1,0:T(8,128)} %get-tuple-element.62), channel_id=1, source_target_pairs={{0,1},{1,0},{2,3},{3,2},{4,5},{5,4},{6,7},{7,6},{8,9},{9,8},{10,11... | collective-permute-start | bytes 3145736 | tf_op jit(solution)/shard_map/ppermute | solution.py:584
  59.4 7.8 %collective-permute-start.5 = (f32[64,8,128]{2,1,0:T(8,128)S(1)}, f32[64,8,128]{2,1,0:T(8,128)S(1)}, u32[]{:S(2)}, u32[]{:S(2)}) collective-permute-start(f32[64,8,128]{2,1,0:T(8,128)S(1)} %bitcast.17), channel_id=1, source_target_pairs={{0,1},{1,0},{2,3},{3,2},{4,5},{5,4},{6,7},{7,6},{8,9},{9,8},{10,11... | collective-permute-start | bytes 786440 | tf_op jit(solution)/shard_map/ppermute | solution.py:584
  63.6 14.6 %all-to-all-start.2 = ((bf16[16,64,256]{2,1,0:T(8,128)(2,1)}), bf16[16,64,256]{2,1,0:T(8,128)(2,1)S(1)}, u32[]{:S(2)}, u32[]{:S(2)}) async-start(bf16[16,64,256]{2,1,0:T(8,128)(2,1)} %bitcast.7), calls=%async_computation.2 | async-start | bytes 1048576 | tf_op jit(solution)/shard_map/all_to_all | solution.py:593
  79.3 18.9 %all-to-all-start.3 = ((f32[16,64,256]{2,1,0:T(8,128)}), f32[16,64,256]{2,1,0:T(8,128)S(1)}, u32[]{:S(2)}, u32[]{:S(2)}) async-start(f32[16,64,256]{2,1,0:T(8,128)} %broadcast_in_dim.16), calls=%async_computation.3 | async-start | bytes 2097152 | tf_op jit(solution)/shard_map/all_to_all | solution.py:593
  98.2 23.8 %collective-permute-start.12 = (f32[1024,256]{1,0:T(8,128)S(1)}, f32[1024,256]{1,0:T(8,128)S(1)}, u32[]{:S(2)}, u32[]{:S(2)}) collective-permute-start(f32[1024,256]{1,0:T(8,128)S(1)} %bitcast.15), channel_id=1, source_target_pairs={{0,1},{1,0},{2,3},{3,2},{4,5},{5,4},{6,7},{7,6},{8,9},{9,8},{10,11... | collective-permute-start | bytes 3145736 | tf_op jit(solution)/shard_map/ppermute | solution.py:584
  101.4 2.7 %collective-permute-start.7 = (f32[256,256]{1,0:T(8,128)S(1)}, f32[256,256]{1,0:T(8,128)S(1)}, u32[]{:S(2)}, u32[]{:S(2)}) collective-permute-start(f32[256,256]{1,0:T(8,128)S(1)} %first_inverse_end.1.inverse_0), channel_id=1, source_target_pairs={{0,1},{1,0},{2,3},{3,2},{4,5},{5,4},{6,7},{7,6},{8,9},{9,8},{10,11... | collective-permute-start | bytes 786440 | tf_op jit(solution)/shard_map/ppermute | solution.py:584
  107.4 11.7 %collective-permute-start.8 = (f32[256,256]{1,0:T(8,128)S(1)}, f32[256,256]{1,0:T(8,128)S(1)}, u32[]{:S(2)}, u32[]{:S(2)}) collective-permute-start(f32[256,256]{1,0:T(8,128)S(1)} %get-tuple-element.68), channel_id=1, source_target_pairs={{0,1},{1,0},{2,3},{3,2},{4,5},{5,4},{6,7},{7,6},{8,9},{9,8},{10,11... | collective-permute-start | bytes 786440 | tf_op jit(solution)/shard_map/ppermute | solution.py:584
  107.9 6.1 %collective-permute-start.13 = (f32[1,256]{1,0:T(1,128)S(1)}, f32[1,256]{1,0:T(1,128)S(1)}, u32[]{:S(2)}, u32[]{:S(2)}) collective-permute-start(f32[1,256]{1,0:T(1,128)S(1)} %get-tuple-element.71), channel_id=1, source_target_pairs={{0,32},{32,64},{64,96},{96,0},{1,33},{33,65},{65,97},{97,1},{2,34}... | collective-permute-start | bytes 3080 | tf_op jit(solution)/shard_map/ppermute | solution.py:589
  108.0 6.9 %collective-permute-start.14 = (f32[1,256]{1,0:T(1,128)S(1)}, f32[1,256]{1,0:T(1,128)S(1)}, u32[]{:S(2)}, u32[]{:S(2)}) collective-permute-start(f32[1,256]{1,0:T(1,128)S(1)} %get-tuple-element.71), channel_id=1, source_target_pairs={{0,64},{32,96},{64,0},{96,32},{1,65},{33,97},{65,1},{97,33},{2,66}... | collective-permute-start | bytes 3080 | tf_op jit(solution)/shard_map/ppermute | solution.py:589
  116.4 2.7 %collective-permute-start.16 = (f32[1,256]{1,0:T(1,128)S(1)}, f32[1,256]{1,0:T(1,128)S(1)}, u32[]{:S(2)}, u32[]{:S(2)}) collective-permute-start(f32[1,256]{1,0:T(1,128)S(1)} %add_add_fusion), channel_id=1, source_target_pairs={{0,1},{1,0},{2,3},{3,2},{4,5},{5,4},{6,7},{7,6},{8,9},{9,8},{10,11... | collective-permute-start | bytes 3080 | tf_op jit(solution)/shard_map/ppermute | solution.py:584
  119.1 12.7 %collective-permute-start.10 = (f32[256,256]{1,0:T(8,128)S(1)}, f32[256,256]{1,0:T(8,128)S(1)}, u32[]{:S(2)}, u32[]{:S(2)}) collective-permute-start(f32[256,256]{1,0:T(8,128)S(1)} %add.35.part_0), channel_id=1, source_target_pairs={{0,64},{32,96},{64,0},{96,32},{1,65},{33,97},{65,1},{97,33},{2,66}... | collective-permute-start | bytes 786440 | tf_op jit(solution)/shard_map/ppermute | solution.py:589
  120.5 12.0 %collective-permute-start.11 = (f32[256,256]{1,0:T(8,128)S(1)}, f32[256,256]{1,0:T(8,128)S(1)}, u32[]{:S(2)}, u32[]{:S(2)}) collective-permute-start(f32[256,256]{1,0:T(8,128)S(1)} %add.35.part_0), channel_id=1, source_target_pairs={{0,96},{32,0},{64,32},{96,64},{1,97},{33,1},{65,33},{97,65},{2,98}... | collective-permute-start | bytes 786440 | tf_op jit(solution)/shard_map/ppermute | solution.py:589
  121.1 13.5 %collective-permute-start.9 = (f32[256,256]{1,0:T(8,128)S(1)}, f32[256,256]{1,0:T(8,128)S(1)}, u32[]{:S(2)}, u32[]{:S(2)}) collective-permute-start(f32[256,256]{1,0:T(8,128)S(1)} %add.35.part_0), channel_id=1, source_target_pairs={{0,32},{32,64},{64,96},{96,0},{1,33},{33,65},{65,97},{97,1},{2,34}... | collective-permute-start | bytes 786440 | tf_op jit(solution)/shard_map/ppermute | solution.py:589
  134.6 9.0 %collective-permute-start.17 = (bf16[512,256]{1,0:T(8,128)(2,1)S(1)}, bf16[512,256]{1,0:T(8,128)(2,1)S(1)}, u32[]{:S(2)}, u32[]{:S(2)}) collective-permute-start(bf16[512,256]{1,0:T(8,128)(2,1)S(1)} %get-tuple-element.75), channel_id=1, source_target_pairs={{0,32},{32,64},{64,96},{96,0},{1,33},{33,65},{65,97},{97,1},{2,34}... | collective-permute-start | bytes 786440 | tf_op jit(solution)/shard_map/ppermute | solution.py:589
  134.6 14.2 %collective-permute-start.18 = (bf16[512,256]{1,0:T(8,128)(2,1)S(1)}, bf16[512,256]{1,0:T(8,128)(2,1)S(1)}, u32[]{:S(2)}, u32[]{:S(2)}) collective-permute-start(bf16[512,256]{1,0:T(8,128)(2,1)S(1)} %get-tuple-element.76), channel_id=1, source_target_pairs={{0,64},{32,96},{64,0},{96,32},{1,65},{33,97},{65,1},{97,33},{2,66}... | collective-permute-start | bytes 786440 | tf_op jit(solution)/shard_map/ppermute | solution.py:589
  136.9 12.3 %collective-permute-start.19 = (bf16[512,256]{1,0:T(8,128)(2,1)S(1)}, bf16[512,256]{1,0:T(8,128)(2,1)S(1)}, u32[]{:S(2)}, u32[]{:S(2)}) collective-permute-start(bf16[512,256]{1,0:T(8,128)(2,1)S(1)} %get-tuple-element.77), channel_id=1, source_target_pairs={{0,96},{32,0},{64,32},{96,64},{1,97},{33,1},{65,33},{97,65},{2,98}... | collective-permute-start | bytes 786440 | tf_op jit(solution)/shard_map/ppermute | solution.py:589
  149.2 9.7 %collective-permute-start.20 = (f32[256,256]{1,0:T(8,128)S(1)}, f32[256,256]{1,0:T(8,128)S(1)}, u32[]{:S(2)}, u32[]{:S(2)}) collective-permute-start(f32[256,256]{1,0:T(8,128)S(1)} %second_inverse.1), channel_id=1, source_target_pairs={{0,1},{1,0},{2,3},{3,2},{4,5},{5,4},{6,7},{7,6},{8,9},{9,8},{10,11... | collective-permute-start | bytes 786440 | tf_op jit(solution)/shard_map/ppermute | solution.py:584
  (8 other events, 107.0 us)

commit v5 on v3

--- a/solution.py
+++ b/solution.py
@@ -176,6 +176,30 @@
     )(meta, *arrays)
 
 
+def solve_kernel(near, far, inverse_0, inverse_1, solved_near, solved_far, squares, gram, inverse):
+    inverse[...] = inverse_0[...] + inverse_1[...]
+    solved_far[...] = jnp.dot(
+        far[...], inverse[...], precision=HIGHEST, preferred_element_type=F32
+    )
+    rows = jnp.dot(near[...], inverse[...], precision=HIGHEST, preferred_element_type=F32)
+    solved_near[...] = rows
+    squares[...] = jnp.sum(rows * rows, axis=0, keepdims=True)
+    gram[...] = lax.dot_general(
+        rows, rows, (((0,), (0,)), ((), ())), precision=HIGHEST, preferred_element_type=F32
+    )
+
+
+def solve(near, far, inverse_0, inverse_1):
+    rank = near.shape[1]
+    rows, square = jax.ShapeDtypeStruct(near.shape, F32), jax.ShapeDtypeStruct((rank, rank), F32)
+    return pl.pallas_call(
+        solve_kernel,
+        out_shape=[rows, rows, jax.ShapeDtypeStruct((1, rank), F32), square, square],
+        compiler_params=pltpu.CompilerParams(vmem_limit_bytes=2 * VMEM_BYTES),
+        name="solve",
+    )(near, far, inverse_0, inverse_1)
+
+
 def prepare_kernel(meta, b_hbm, c_hbm, own, gram_keep, gram_send, b_factor, c_factor, sems):
     rows = b_factor.shape[0]
     core = meta[2]
@@ -553,19 +577,16 @@
     meta = jnp.stack([block_count[0], grp, core])
 
     own, gram_keep, gram_send = prepare(meta, b_factor, c_factor)
+    order_one, order_two = order_slots(meta, i_index, j_index, k_index)
+    pieces = [own] + [along_groups(own, q) for q in (1, 2, 3)]
     gram_pair = gram_keep + to_other_core(gram_send)
-    gram_pair, late_meta = lax.optimization_barrier((gram_pair, meta))
-    order_one, order_two = order_slots(late_meta, i_index, j_index, k_index)
-    pieces = [own] + [along_groups(own, q) for q in (1, 2, 3)]
+    send, ring = mode_one(True, order_one, blocks, pieces)
+    gram_pair, send, pieces = lax.optimization_barrier((gram_pair, send, pieces))
     gram_parts = exchange(gram_pair.reshape(chips, -1, 8, 128), CHIPS)
-    send, ring = mode_one(True, order_one, blocks, pieces)
+    [keep] = mode_one(False, order_one, blocks, pieces)
+    gram_parts, keep = lax.optimization_barrier((gram_parts, keep))
     piece = jnp.sum(gram_parts, axis=0)
-    piece, send = lax.optimization_barrier((piece, send))
-    spread = jnp.broadcast_to(piece[None], (chips,) + piece.shape)
-    spread, pieces = lax.optimization_barrier((spread, pieces))
-    gram_near = exchange(spread, CHIPS)
-    [keep] = mode_one(False, order_one, blocks, pieces)
-    gram_near, keep = lax.optimization_barrier((gram_near, keep))
+    gram_near = exchange(jnp.broadcast_to(piece[None], (chips,) + piece.shape), CHIPS)
     gram_near = gram_near.reshape(-1, 8, 128)
     gram_far = to_other_core(gram_near)
     rings = (ring, to_other_core(ring))
@@ -577,15 +598,13 @@
     sum_near = sum_near.reshape(-1, rank)
 
     inverse = inverse_of(first_inverse_kernel, "first_inverse", meta, *rings, gram_near, gram_far)
-    inverse = lax.optimization_barrier(inverse + to_other_core(inverse))
-
+    inverse, sum_near = lax.optimization_barrier((inverse, sum_near))
     sum_far = to_other_core(sum_near)
-    a_near = jnp.dot(sum_near, inverse, precision=HIGHEST)
-    squares = jnp.sum(a_near * a_near, axis=0, keepdims=True)
+    a_near, a_far, squares, gram_core, inverse = solve(
+        sum_near, sum_far, inverse, to_other_core(inverse)
+    )
     squares = squares + along_groups(squares, 1) + along_groups(squares, 2) + along_groups(squares, 3)
     squares = squares + to_other_core(squares)
-    a_far = jnp.dot(sum_far, inverse, precision=HIGHEST)
-    gram_core = jnp.dot(a_near.T, a_near, precision=HIGHEST)
     gram_plane = gram_core + to_other_core(gram_core)
     gram_parts = [gram_plane] + [along_groups(gram_plane, q) for q in (1, 2, 3)]
 

time: 157 us -> 173 us (1.10)
  starting transfers between devices: 84.4 us -> 48.9 us
  waiting for transfers between devices: 18.9 us -> 51.1 us
  Pallas kernels: 36.7 us -> 60.3 us
  matrix products: 7.47 us -> 2.33 us
    ppermute x9, starting transfers between devices: 36.2 us -> 7.7 us  [to_other_core(): return lax.ppermute(value, 'core', [(0, 1), (1, 0)])]
    pallas_call x2, Pallas kernels: 1.8 us -> 28.7 us  [inverse_of(): pl.pallas_call(kernel, out_shape=jax.ShapeDtypeStruct((n, n), F32), in_sp...]
    all_to_all x4, waiting for transfers between devices: 7.12 us -> 23.2 us  [exchange(): return lax.all_to_all(value, axes, 0, 0)]
    ppermute x12, waiting for transfers between devices: 8.81 us -> 23.7 us  [along_groups(): lax.ppermute(value, 'grp', [(p, (p + shift) % size) for p in range(size)])]
    ppermute x12, starting transfers between devices: 18.4 us -> 10.9 us  [along_groups(): lax.ppermute(value, 'grp', [(p, (p + shift) % size) for p in range(size)])]
    pallas_call x4, Pallas kernels: 30.4 us -> 23.2 us  [mode_call(): pl.pallas_call(kernel, out_shape=out_shape, in_specs=[smem] + [anywhere]...]
    dot_general x3 -> x0, matrix products: 5.15 us -> none  [the longest x1 2.24 us: on_device(): a_near = jnp.dot(sum_near, inverse, precision=HIGHEST)]
    pallas_call x0 -> x1, Pallas kernels: none -> 4.25 us  [solve(): pl.pallas_call(solve_kernel, out_shape=[rows, rows, jax.ShapeDtypeStruct(...]
  transfers between devices with their start and end apart: 25 -> 25, of which waited for: 10 -> 14; matrix products, arithmetic and copies ran while one was open for 5% -> 3% of each run, Pallas kernels for 22% -> 28%
where the time goes in v5:
time: 173 us; the launch traced here: 172 us
  Pallas kernels  60.3 us (35%)
  waiting for transfers between devices  51.1 us (30%)
  starting transfers between devices  48.9 us (28%)
  local copies, waits for them, and re-layouts  4.46 us (3%)
  other arithmetic  3.23 us (2%)
  matrix products  2.33 us (1%)
    all_to_all x4, starting transfers between devices, exchange(): return lax.all_to_all(value, axes, 0, 0)  30.3 us
    pallas_call x2, Pallas kernels, inverse_of(): pl.pallas_call(kernel, out_shape=jax.ShapeDtypeStruct((n, n), F32), in_sp...  28.7 us
    ppermute x12, waiting for transfers between devices, along_groups(): lax.ppermute(value, 'grp', [(p, (p + shift) % size) for p in range(size)])  23.7 us
    all_to_all x4, waiting for transfers between devices, exchange(): return lax.all_to_all(value, axes, 0, 0)  23.2 us
    pallas_call x4, Pallas kernels, mode_call(): pl.pallas_call(kernel, out_shape=out_shape, in_specs=[smem] + [anywhere]...  23.2 us
    ppermute x12, starting transfers between devices, along_groups(): lax.ppermute(value, 'grp', [(p, (p + shift) % size) for p in range(size)])  10.9 us
    ppermute x9, starting transfers between devices, to_other_core(): return lax.ppermute(value, 'core', [(0, 1), (1, 0)])  7.7 us
    pallas_call x1, Pallas kernels, solve(): pl.pallas_call(solve_kernel, out_shape=[rows, rows, jax.ShapeDtypeStruct(...  4.25 us
  transfers between devices with their start and end apart: 25, of which 14 were waited for; matrix products, arithmetic and copies ran while one was open for 3% of the time, Pallas kernels for 28%

profile of v5, /device:TPU:1, one launch (start us, length us, event | category | flops | bytes accessed | tf_op | source)
XLA Modules:
  0.0 171.8 jit_solution(6921623900793149194)
XLA Ops:
  3.3 2.2 %prepare.1 = (bf16[656,256]{1,0:T(8,128)(2,1)S(1)}, f32[64,8,128]{2,1,0:T(8,128)S(1)}, f32[64,8,128]{2,1,0:T(8,128)S(1)}) custom-call(s32[3]{0:T(128)S(1)} %pad_add_fusion.meta, f32[512,256]{1,0:T(8,128)S(1)} %copy-done, f32[128,256]{1,0:T(8,128)S(1)} %copy-done.1), custom_call_target="tpu_custom_call" | custom-call | tf_op jit(solution)/shard_map/prepare/pallas_call | solution.py:242
  5.5 3.6 %collective-permute-start.3 = (bf16[656,256]{1,0:T(8,128)(2,1)S(1)}, bf16[656,256]{1,0:T(8,128)(2,1)S(1)}, u32[]{:S(2)}, u32[]{:S(2)}) collective-permute-start(bf16[656,256]{1,0:T(8,128)(2,1)S(1)} %get-tuple-element.48.refs_2_.own_0), channel_id=1, source_target_pairs={{0,96},{32,0},{64,32},{96,64},{1,97},{33,1},{65,33},{97,65},{2,98}... | collective-permute-start | bytes 1007624 | tf_op jit(solution)/shard_map/ppermute | solution.py:565
  14.4 8.4 %collective-permute-done.3.refs_5_.own_3 = bf16[656,256]{1,0:T(8,128)(2,1)S(1)} collective-permute-done((bf16[656,256]{1,0:T(8,128)(2,1)S(1)}, bf16[656,256]{1,0:T(8,128)(2,1)S(1)}, u32[]{:S(2)}, u32[]{:S(2)}) %collective-permute-start.3) | collective-permute-done | bytes 335904 | tf_op jit(solution)/shard_map/ppermute | solution.py:565
  22.8 4.9 %collective-permute-done.1.refs_3_.own_1 = bf16[656,256]{1,0:T(8,128)(2,1)S(1)} collective-permute-done((bf16[656,256]{1,0:T(8,128)(2,1)S(1)}, bf16[656,256]{1,0:T(8,128)(2,1)S(1)}, u32[]{:S(2)}, u32[]{:S(2)}) %collective-permute-start.1) | collective-permute-done | bytes 335904 | tf_op jit(solution)/shard_map/ppermute | solution.py:565
  28.3 6.2 %mode_one_other_core.1 = (f32[1024,256]{1,0:T(8,128)}, f32[8,128]{1,0:T(8,128)S(1)}) custom-call(s32[256]{0:T(256)S(1)} %copy-done.5, bf16[192,32,1024]{2,1,0:T(8,128)(2,1)} %blocks.3, bf16[656,256]{1,0:T(8,128)(2,1)S(1)} %get-tuple-element.48.refs_2_.own_0, bf16[656,256]{1,0:T(8,128)(2,1)S(1)} %collective-permute-done.1.refs_3_.own_1, ...), custom_call_target="tpu_custom_call" | custom-call | flops 15000000512 | bytes 48000000 | tf_op jit(solution)/shard_map/mode_one_other_core/pallas_call | solution.py:503
  34.5 13.3 %all-to-all-start = ((f32[64,1,8,128]{3,2,1,0:T(8,128)}), f32[64,1,8,128]{3,2,1,0:T(8,128)S(1)}, u32[]{:S(2)}, u32[]{:S(2)}) async-start(f32[64,1,8,128]{3,2,1,0:T(8,128)} %bitcast.3), calls=%async_computation | async-start | bytes 524288 | tf_op jit(solution)/shard_map/all_to_all | solution.py:569
  47.9 5.2 %mode_one_own_core.1 = f32[1024,256]{1,0:T(8,128)S(1)} custom-call(s32[256]{0:T(256)S(1)} %copy-done.5, bf16[192,32,1024]{2,1,0:T(8,128)(2,1)} %blocks.3, bf16[656,256]{1,0:T(8,128)(2,1)S(1)} %get-tuple-element.48.refs_2_.own_0, bf16[656,256]{1,0:T(8,128)(2,1)S(1)} %collective-permute-done.1.refs_3_.own_1, ...), custom_call_target="tpu_custom_call" | custom-call | flops 15000000512 | bytes 48000000 | tf_op jit(solution)/shard_map/mode_one_own_core/pallas_call | solution.py:503
  53.2 4.1 %all-to-all-done = f32[64,1,8,128]{3,2,1,0:T(8,128)S(1)} async-done(((f32[64,1,8,128]{3,2,1,0:T(8,128)}), f32[64,1,8,128]{3,2,1,0:T(8,128)S(1)}, u32[]{:S(2)}, u32[]{:S(2)}) %all-to-all-start) | async-done | bytes 262176 | tf_op jit(solution)/shard_map/all_to_all | solution.py:569
  58.0 9.8 %all-to-all-start.2 = ((f32[64,1,8,128]{3,2,1,0:T(8,128)}), f32[64,1,8,128]{3,2,1,0:T(8,128)S(1)}, u32[]{:S(2)}, u32[]{:S(2)}) async-start(f32[64,1,8,128]{3,2,1,0:T(8,128)} %broadcast_in_dim.4), calls=%async_computation.2 | async-start | bytes 524288 | tf_op jit(solution)/shard_map/all_to_all | solution.py:569
  67.9 2.2 %add_convert_fusion = bf16[1024,256]{1,0:T(8,128)(2,1)} fusion(f32[1024,256]{1,0:T(8,128)S(1)} %mode_one_own_core.1, f32[1024,256]{1,0:T(8,128)} %collective-permute-done.4), kind=kLoop, calls=%fused_computation.1 | loop fusion | flops 524288 | bytes 2621440 | tf_op jit(solution)/shard_map/convert_element_type | solution.py:594
  70.1 7.9 %all-to-all-done.2 = f32[64,1,8,128]{3,2,1,0:T(8,128)S(1)} async-done(((f32[64,1,8,128]{3,2,1,0:T(8,128)}), f32[64,1,8,128]{3,2,1,0:T(8,128)S(1)}, u32[]{:S(2)}, u32[]{:S(2)}) %all-to-all-start.2) | async-done | bytes 262176 | tf_op jit(solution)/shard_map/all_to_all | solution.py:569
  78.0 3.6 %all-to-all-start.1 = ((bf16[16,64,256]{2,1,0:T(8,128)(2,1)}), bf16[16,64,256]{2,1,0:T(8,128)(2,1)S(1)}, u32[]{:S(2)}, u32[]{:S(2)}) async-start(bf16[16,64,256]{2,1,0:T(8,128)(2,1)} %bitcast.4), calls=%async_computation.1 | async-start | bytes 1048576 | tf_op jit(solution)/shard_map/all_to_all | solution.py:569
  82.2 10.4 %all-to-all-done.1 = bf16[16,64,256]{2,1,0:T(8,128)(2,1)S(1)} async-done(((bf16[16,64,256]{2,1,0:T(8,128)(2,1)}), bf16[16,64,256]{2,1,0:T(8,128)(2,1)S(1)}, u32[]{:S(2)}, u32[]{:S(2)}) %all-to-all-start.1) | async-done | bytes 524320 | tf_op jit(solution)/shard_map/all_to_all | solution.py:569
  93.8 3.7 %all-to-all-start.3 = ((f32[16,64,256]{2,1,0:T(8,128)}), f32[16,64,256]{2,1,0:T(8,128)S(1)}, u32[]{:S(2)}, u32[]{:S(2)}) async-start(f32[16,64,256]{2,1,0:T(8,128)} %broadcast_in_dim.5), calls=%async_computation.3 | async-start | bytes 2097152 | tf_op jit(solution)/shard_map/all_to_all | solution.py:569
  97.5 14.4 %first_inverse.1.inverse_0 = f32[256,256]{1,0:T(8,128)S(1)} custom-call(s32[3]{0:T(128)S(1)} %copy-done.3, f32[8,128]{1,0:T(8,128)S(1)} %get-tuple-element.54.ring, f32[8,128]{1,0:T(8,128)S(1)} %collective-permute-done.5.other_ring, f32[64,8,128]{2,1,0:T(8,128)S(1)} %bitcast.14, f32[64,8,128]{2,1,0:T(8,128)S(1)} %collective-permute-done.6.far), custom_call_target="tpu_custom_call" | custom-call | flops 16000000000 | bytes 50000000 | tf_op jit(solution)/shard_map/first_inverse/pallas_call | solution.py:166
  112.6 3.2 %collective-permute-start.7 = (f32[1024,256]{1,0:T(8,128)S(1)}, f32[1024,256]{1,0:T(8,128)S(1)}, u32[]{:S(2)}, u32[]{:S(2)}) collective-permute-start(f32[1024,256]{1,0:T(8,128)S(1)} %bitcast.11), channel_id=1, source_target_pairs={{0,1},{1,0},{2,3},{3,2},{4,5},{5,4},{6,7},{7,6},{8,9},{9,8},{10,11... | collective-permute-start | bytes 3145736 | tf_op jit(solution)/shard_map/ppermute | solution.py:560
  115.8 2.7 %collective-permute-done.8.inverse_1 = f32[256,256]{1,0:T(8,128)S(1)} collective-permute-done((f32[256,256]{1,0:T(8,128)S(1)}, f32[256,256]{1,0:T(8,128)S(1)}, u32[]{:S(2)}, u32[]{:S(2)}) %collective-permute-start.8) | collective-permute-done | bytes 262176 | tf_op jit(solution)/shard_map/ppermute | solution.py:560
  118.5 4.3 %solve.1 = (f32[1024,256]{1,0:T(8,128)S(1)}, f32[1024,256]{1,0:T(8,128)S(1)}, f32[1,256]{1,0:T(1,128)S(1)}, f32[256,256]{1,0:T(8,128)S(1)}, f32[256,256]{1,0:T(8,128)S(1)}) custom-call(f32[1024,256]{1,0:T(8,128)S(1)} %bitcast.12, f32[1024,256]{1,0:T(8,128)S(1)} %collective-permute-done.7.far, f32[256,256]{1,0:T(8,128)S(1)} %first_inverse.1.inverse_0, ...), custom_call_target="tpu_custom_call" | custom-call | tf_op jit(solution)/shard_map/solve/pallas_call | solution.py:195
  125.6 2.0 %collective-permute-done.14 = f32[1,256]{1,0:T(1,128)S(1)} collective-permute-done((f32[1,256]{1,0:T(1,128)S(1)}, f32[1,256]{1,0:T(1,128)S(1)}, u32[]{:S(2)}, u32[]{:S(2)}) %collective-permute-start.14) | collective-permute-done | bytes 1056 | tf_op jit(solution)/shard_map/ppermute | solution.py:565
  133.0 7.9 %mode_two_other_groups.1 = (bf16[512,256]{1,0:T(8,128)(2,1)S(1)}, bf16[512,256]{1,0:T(8,128)(2,1)S(1)}, bf16[512,256]{1,0:T(8,128)(2,1)S(1)}, bf16[2048,256]{1,0:T(8,128)(2,1)S(1)}) custom-call(s32[256]{0:T(256)S(1)} %copy-done.4, bf16[192,32,1024]{2,1,0:T(8,128)(2,1)} %blocks.3, bf16[656,256]{1,0:T(8,128)(2,1)S(1)} %get-tuple-element.48.refs_2_.own_0, ...), custom_call_target="tpu_custom_call" | custom-call | flops 15000000512 | bytes 48000000 | tf_op jit(solution)/shard_map/mode_two_other_groups/pallas_call | solution.py:503
  141.1 6.5 %collective-permute-done.10.part_1 = f32[256,256]{1,0:T(8,128)S(1)} collective-permute-done((f32[256,256]{1,0:T(8,128)S(1)}, f32[256,256]{1,0:T(8,128)S(1)}, u32[]{:S(2)}, u32[]{:S(2)}) %collective-permute-start.10) | collective-permute-done | bytes 262176 | tf_op jit(solution)/shard_map/ppermute | solution.py:565
  148.3 2.1 %collective-permute-start.19 = (bf16[512,256]{1,0:T(8,128)(2,1)S(1)}, bf16[512,256]{1,0:T(8,128)(2,1)S(1)}, u32[]{:S(2)}, u32[]{:S(2)}) collective-permute-start(bf16[512,256]{1,0:T(8,128)(2,1)S(1)} %get-tuple-element.69), channel_id=1, source_target_pairs={{0,96},{32,0},{64,32},{96,64},{1,97},{33,1},{65,33},{97,65},{2,98}... | collective-permute-start | bytes 786440 | tf_op jit(solution)/shard_map/ppermute | solution.py:565
  150.4 14.4 %second_inverse.1 = f32[256,256]{1,0:T(8,128)S(1)} custom-call(s32[3]{0:T(128)S(1)} %copy-done.3, f32[8,128]{1,0:T(8,128)S(1)} %get-tuple-element.54.ring, f32[8,128]{1,0:T(8,128)S(1)} %collective-permute-done.5.other_ring, f32[256,256]{1,0:T(8,128)S(1)} %add.35.part_0, f32[256,256]{1,0:T(8,128)S(1)} %collective-permute-done.10.part_1, ...), custom_call_target="tpu_custom_call" | custom-call | flops 16000000000 | bytes 50000000 | tf_op jit(solution)/shard_map/second_inverse/pallas_call | solution.py:166
  164.8 3.9 %mode_two_own_group.1 = f32[512,256]{1,0:T(8,128)S(1)} custom-call(s32[256]{0:T(256)S(1)} %copy-done.4, bf16[192,32,1024]{2,1,0:T(8,128)(2,1)} %blocks.3, bf16[656,256]{1,0:T(8,128)(2,1)S(1)} %get-tuple-element.48.refs_2_.own_0, bf16[656,256]{1,0:T(8,128)(2,1)S(1)} %collective-permute-done.1.refs_3_.own_1, ...), custom_call_target="tpu_custom_call" | custom-call | flops 2000000000 | bytes 6000000 | tf_op jit(solution)/shard_map/mode_two_own_group/pallas_call | solution.py:503
  (60 shorter events, 23.7 us)
Async XLA Ops:
  5.5 17.2 %collective-permute-start.3 = (bf16[656,256]{1,0:T(8,128)(2,1)S(1)}, bf16[656,256]{1,0:T(8,128)(2,1)S(1)}, u32[]{:S(2)}, u32[]{:S(2)}) collective-permute-start(bf16[656,256]{1,0:T(8,128)(2,1)S(1)} %get-tuple-element.48.refs_2_.own_0), channel_id=1, source_target_pairs={{0,96},{32,0},{64,32},{96,64},{1,97},{33,1},{65,33},{97,65},{2,98}... | collective-permute-start | bytes 1007624 | tf_op jit(solution)/shard_map/ppermute | solution.py:565
  9.1 13.6 %collective-permute-start.2 = (bf16[656,256]{1,0:T(8,128)(2,1)S(1)}, bf16[656,256]{1,0:T(8,128)(2,1)S(1)}, u32[]{:S(2)}, u32[]{:S(2)}) collective-permute-start(bf16[656,256]{1,0:T(8,128)(2,1)S(1)} %get-tuple-element.48.refs_2_.own_0), channel_id=1, source_target_pairs={{0,64},{32,96},{64,0},{96,32},{1,65},{33,97},{65,1},{97,33},{2,66}... | collective-permute-start | bytes 1007624 | tf_op jit(solution)/shard_map/ppermute | solution.py:565
  9.5 18.2 %collective-permute-start.1 = (bf16[656,256]{1,0:T(8,128)(2,1)S(1)}, bf16[656,256]{1,0:T(8,128)(2,1)S(1)}, u32[]{:S(2)}, u32[]{:S(2)}) collective-permute-start(bf16[656,256]{1,0:T(8,128)(2,1)S(1)} %get-tuple-element.48.refs_2_.own_0), channel_id=1, source_target_pairs={{0,32},{32,64},{64,96},{96,0},{1,33},{33,65},{65,97},{97,1},{2,34}... | collective-permute-start | bytes 1007624 | tf_op jit(solution)/shard_map/ppermute | solution.py:565
  10.2 3.5 %collective-permute-start = (f32[64,8,128]{2,1,0:T(8,128)S(1)}, f32[64,8,128]{2,1,0:T(8,128)S(1)}, u32[]{:S(2)}, u32[]{:S(2)}) collective-permute-start(f32[64,8,128]{2,1,0:T(8,128)S(1)} %get-tuple-element.43), channel_id=1, source_target_pairs={{0,1},{1,0},{2,3},{3,2},{4,5},{5,4},{6,7},{7,6},{8,9},{9,8},{10,11... | collective-permute-start | bytes 786440 | tf_op jit(solution)/shard_map/ppermute | solution.py:560
  34.5 22.7 %all-to-all-start = ((f32[64,1,8,128]{3,2,1,0:T(8,128)}), f32[64,1,8,128]{3,2,1,0:T(8,128)S(1)}, u32[]{:S(2)}, u32[]{:S(2)}) async-start(f32[64,1,8,128]{3,2,1,0:T(8,128)} %bitcast.3), calls=%async_computation | async-start | bytes 524288 | tf_op jit(solution)/shard_map/all_to_all | solution.py:569
  47.8 20.0 %collective-permute-start.4 = (f32[1024,256]{1,0:T(8,128)}, f32[1024,256]{1,0:T(8,128)}, u32[]{:S(2)}, u32[]{:S(2)}) collective-permute-start(f32[1024,256]{1,0:T(8,128)} %get-tuple-element.53), channel_id=1, source_target_pairs={{0,1},{1,0},{2,3},{3,2},{4,5},{5,4},{6,7},{7,6},{8,9},{9,8},{10,11... | collective-permute-start | bytes 3145736 | tf_op jit(solution)/shard_map/ppermute | solution.py:560
  58.0 19.9 %all-to-all-start.2 = ((f32[64,1,8,128]{3,2,1,0:T(8,128)}), f32[64,1,8,128]{3,2,1,0:T(8,128)S(1)}, u32[]{:S(2)}, u32[]{:S(2)}) async-start(f32[64,1,8,128]{3,2,1,0:T(8,128)} %broadcast_in_dim.4), calls=%async_computation.2 | async-start | bytes 524288 | tf_op jit(solution)/shard_map/all_to_all | solution.py:569
  78.0 14.6 %all-to-all-start.1 = ((bf16[16,64,256]{2,1,0:T(8,128)(2,1)}), bf16[16,64,256]{2,1,0:T(8,128)(2,1)S(1)}, u32[]{:S(2)}, u32[]{:S(2)}) async-start(bf16[16,64,256]{2,1,0:T(8,128)(2,1)} %bitcast.4), calls=%async_computation.1 | async-start | bytes 1048576 | tf_op jit(solution)/shard_map/all_to_all | solution.py:569
  81.6 15.9 %collective-permute-start.6 = (f32[64,8,128]{2,1,0:T(8,128)S(1)}, f32[64,8,128]{2,1,0:T(8,128)S(1)}, u32[]{:S(2)}, u32[]{:S(2)}) collective-permute-start(f32[64,8,128]{2,1,0:T(8,128)S(1)} %bitcast.13), channel_id=1, source_target_pairs={{0,1},{1,0},{2,3},{3,2},{4,5},{5,4},{6,7},{7,6},{8,9},{9,8},{10,11... | collective-permute-start | bytes 786440 | tf_op jit(solution)/shard_map/ppermute | solution.py:560
  81.7 15.7 %collective-permute-start.5 = (f32[8,128]{1,0:T(8,128)S(1)}, f32[8,128]{1,0:T(8,128)S(1)}, u32[]{:S(2)}, u32[]{:S(2)}) collective-permute-start(f32[8,128]{1,0:T(8,128)S(1)} %get-tuple-element.54.ring), channel_id=1, source_target_pairs={{0,1},{1,0},{2,3},{3,2},{4,5},{5,4},{6,7},{7,6},{8,9},{9,8},{10,11... | collective-permute-start | bytes 12296 | tf_op jit(solution)/shard_map/ppermute | solution.py:560
  93.8 18.9 %all-to-all-start.3 = ((f32[16,64,256]{2,1,0:T(8,128)}), f32[16,64,256]{2,1,0:T(8,128)S(1)}, u32[]{:S(2)}, u32[]{:S(2)}) async-start(f32[16,64,256]{2,1,0:T(8,128)} %broadcast_in_dim.5), calls=%async_computation.3 | async-start | bytes 2097152 | tf_op jit(solution)/shard_map/all_to_all | solution.py:569
  112.6 5.9 %collective-permute-start.7 = (f32[1024,256]{1,0:T(8,128)S(1)}, f32[1024,256]{1,0:T(8,128)S(1)}, u32[]{:S(2)}, u32[]{:S(2)}) collective-permute-start(f32[1024,256]{1,0:T(8,128)S(1)} %bitcast.11), channel_id=1, source_target_pairs={{0,1},{1,0},{2,3},{3,2},{4,5},{5,4},{6,7},{7,6},{8,9},{9,8},{10,11... | collective-permute-start | bytes 3145736 | tf_op jit(solution)/shard_map/ppermute | solution.py:560
  115.8 2.7 %collective-permute-start.8 = (f32[256,256]{1,0:T(8,128)S(1)}, f32[256,256]{1,0:T(8,128)S(1)}, u32[]{:S(2)}, u32[]{:S(2)}) collective-permute-start(f32[256,256]{1,0:T(8,128)S(1)} %first_inverse.1.inverse_0), channel_id=1, source_target_pairs={{0,1},{1,0},{2,3},{3,2},{4,5},{5,4},{6,7},{7,6},{8,9},{9,8},{10,11... | collective-permute-start | bytes 786440 | tf_op jit(solution)/shard_map/ppermute | solution.py:560
  122.7 8.6 %collective-permute-start.9 = (f32[256,256]{1,0:T(8,128)S(1)}, f32[256,256]{1,0:T(8,128)S(1)}, u32[]{:S(2)}, u32[]{:S(2)}) collective-permute-start(f32[256,256]{1,0:T(8,128)S(1)} %get-tuple-element.59), channel_id=1, source_target_pairs={{0,1},{1,0},{2,3},{3,2},{4,5},{5,4},{6,7},{7,6},{8,9},{9,8},{10,11... | collective-permute-start | bytes 786440 | tf_op jit(solution)/shard_map/ppermute | solution.py:560
  123.2 2.4 %collective-permute-start.15 = (f32[1,256]{1,0:T(1,128)S(1)}, f32[1,256]{1,0:T(1,128)S(1)}, u32[]{:S(2)}, u32[]{:S(2)}) collective-permute-start(f32[1,256]{1,0:T(1,128)S(1)} %get-tuple-element.63), channel_id=1, source_target_pairs={{0,96},{32,0},{64,32},{96,64},{1,97},{33,1},{65,33},{97,65},{2,98}... | collective-permute-start | bytes 3080 | tf_op jit(solution)/shard_map/ppermute | solution.py:565
  123.7 3.9 %collective-permute-start.14 = (f32[1,256]{1,0:T(1,128)S(1)}, f32[1,256]{1,0:T(1,128)S(1)}, u32[]{:S(2)}, u32[]{:S(2)}) collective-permute-start(f32[1,256]{1,0:T(1,128)S(1)} %get-tuple-element.63), channel_id=1, source_target_pairs={{0,64},{32,96},{64,0},{96,32},{1,65},{33,97},{65,1},{97,33},{2,66}... | collective-permute-start | bytes 3080 | tf_op jit(solution)/shard_map/ppermute | solution.py:565
  125.0 3.7 %collective-permute-start.13 = (f32[1,256]{1,0:T(1,128)S(1)}, f32[1,256]{1,0:T(1,128)S(1)}, u32[]{:S(2)}, u32[]{:S(2)}) collective-permute-start(f32[1,256]{1,0:T(1,128)S(1)} %get-tuple-element.63), channel_id=1, source_target_pairs={{0,32},{32,64},{64,96},{96,0},{1,33},{33,65},{65,97},{97,1},{2,34}... | collective-permute-start | bytes 3080 | tf_op jit(solution)/shard_map/ppermute | solution.py:565
  128.8 2.6 %collective-permute-start.16 = (f32[1,256]{1,0:T(1,128)S(1)}, f32[1,256]{1,0:T(1,128)S(1)}, u32[]{:S(2)}, u32[]{:S(2)}) collective-permute-start(f32[1,256]{1,0:T(1,128)S(1)} %add_add_fusion), channel_id=1, source_target_pairs={{0,1},{1,0},{2,3},{3,2},{4,5},{5,4},{6,7},{7,6},{8,9},{9,8},{10,11... | collective-permute-start | bytes 3080 | tf_op jit(solution)/shard_map/ppermute | solution.py:560
  131.4 9.5 %collective-permute-start.12 = (f32[256,256]{1,0:T(8,128)S(1)}, f32[256,256]{1,0:T(8,128)S(1)}, u32[]{:S(2)}, u32[]{:S(2)}) collective-permute-start(f32[256,256]{1,0:T(8,128)S(1)} %add.35.part_0), channel_id=1, source_target_pairs={{0,96},{32,0},{64,32},{96,64},{1,97},{33,1},{65,33},{97,65},{2,98}... | collective-permute-start | bytes 786440 | tf_op jit(solution)/shard_map/ppermute | solution.py:565
  132.3 8.8 %collective-permute-start.11 = (f32[256,256]{1,0:T(8,128)S(1)}, f32[256,256]{1,0:T(8,128)S(1)}, u32[]{:S(2)}, u32[]{:S(2)}) collective-permute-start(f32[256,256]{1,0:T(8,128)S(1)} %add.35.part_0), channel_id=1, source_target_pairs={{0,64},{32,96},{64,0},{96,32},{1,65},{33,97},{65,1},{97,33},{2,66}... | collective-permute-start | bytes 786440 | tf_op jit(solution)/shard_map/ppermute | solution.py:565
  133.0 14.6 %collective-permute-start.10 = (f32[256,256]{1,0:T(8,128)S(1)}, f32[256,256]{1,0:T(8,128)S(1)}, u32[]{:S(2)}, u32[]{:S(2)}) collective-permute-start(f32[256,256]{1,0:T(8,128)S(1)} %add.35.part_0), channel_id=1, source_target_pairs={{0,32},{32,64},{64,96},{96,0},{1,33},{33,65},{65,97},{97,1},{2,34}... | collective-permute-start | bytes 786440 | tf_op jit(solution)/shard_map/ppermute | solution.py:565
  147.6 21.1 %collective-permute-start.17 = (bf16[512,256]{1,0:T(8,128)(2,1)S(1)}, bf16[512,256]{1,0:T(8,128)(2,1)S(1)}, u32[]{:S(2)}, u32[]{:S(2)}) collective-permute-start(bf16[512,256]{1,0:T(8,128)(2,1)S(1)} %get-tuple-element.67), channel_id=1, source_target_pairs={{0,32},{32,64},{64,96},{96,0},{1,33},{33,65},{65,97},{97,1},{2,34}... | collective-permute-start | bytes 786440 | tf_op jit(solution)/shard_map/ppermute | solution.py:565
  147.6 21.1 %collective-permute-start.18 = (bf16[512,256]{1,0:T(8,128)(2,1)S(1)}, bf16[512,256]{1,0:T(8,128)(2,1)S(1)}, u32[]{:S(2)}, u32[]{:S(2)}) collective-permute-start(bf16[512,256]{1,0:T(8,128)(2,1)S(1)} %get-tuple-element.68), channel_id=1, source_target_pairs={{0,64},{32,96},{64,0},{96,32},{1,65},{33,97},{65,1},{97,33},{2,66}... | collective-permute-start | bytes 786440 | tf_op jit(solution)/shard_map/ppermute | solution.py:565
  148.3 20.4 %collective-permute-start.19 = (bf16[512,256]{1,0:T(8,128)(2,1)S(1)}, bf16[512,256]{1,0:T(8,128)(2,1)S(1)}, u32[]{:S(2)}, u32[]{:S(2)}) collective-permute-start(bf16[512,256]{1,0:T(8,128)(2,1)S(1)} %get-tuple-element.69), channel_id=1, source_target_pairs={{0,96},{32,0},{64,32},{96,64},{1,97},{33,1},{65,33},{97,65},{2,98}... | collective-permute-start | bytes 786440 | tf_op jit(solution)/shard_map/ppermute | solution.py:565
  (7 other events, 97.8 us)
